TPU v7x, 32 devices: a whole 2x2x4 slice. The times are simulated.
32 devices in a mesh: ops: 16 (over z, x, core), sec: 2 (over y).
Axes of the slice: x: 2, y: 2, z: 4, core: 2. Of those that a mesh axis runs over, the one named last changes fastest.
Arguments:
- wavefunction: bfloat16 [8, 512, 512], P('sec'), may hold values from -6 to 6
- left_ops: bfloat16 [16, 512, 512], P('ops'), may hold values from -0.25 to 0.25
- right_ops: bfloat16 [16, 512, 512], P('ops'), may hold values from -0.25 to 0.25
- shift_map: int32 [16], P('ops'), may hold values from 0 to 7
- sector_sizes: int32 [8], replicated, may hold values from 256 to 512, as said below
- step_sizes: int32 [2], replicated, may hold values from 1 to 5
- integrals: float32 [16, 3], P('ops'), may hold values from 0.25 to 1
Outputs:
- final_wave: float32 [8, 512, 512], P('sec')
- mixed_ops: bfloat16 [16, 512, 512], P('ops', None, 'sec')
Inputs may be any that keep to these rules, and one draw needn't show every extreme that they name: `sector_sizes`: each sector holds between 256 and 512 states; some sector holds exactly 512.
All inputs are finite; a program needn't handle non-finite values.
Results may differ from a plain program's by a relative error of at most 0.015.
Values may be sent and summed in bfloat16 or wider, within the bound.
No kernel may reach another device: no remote copies, remote signals or barrier semaphores. Data moves between devices by JAX's collectives and lax.ppermute only.
A program may use at most 64 MiB of HBM per device.

v0:
```python
import math

import jax
import jax.numpy as jnp
from jax import lax
from jax.sharding import PartitionSpec as P

ITERS = 2


def broadcast(value, axis, source):
    kept = jnp.where(lax.axis_index(axis) == source, value, 0).astype(value.dtype)
    return lax.psum(kept, axis)


def padded_2(cells, sides, width):
    for axis, dim in sides:
        count = lax.axis_size(axis)
        ends = count - 1
        head = lax.slice_in_dim(cells, 0, width, axis=dim)
        tail = lax.slice_in_dim(cells, cells.shape[dim] - width, cells.shape[dim], axis=dim)
        cells = jnp.concatenate(
            [
                lax.ppermute(tail, axis, [(i, (i + 1) % count) for i in range(ends)]),
                cells,
                lax.ppermute(head, axis, [((i + 1) % count, i) for i in range(ends)]),
            ],
            axis=dim,
        )
    return cells


def shards(wavefunction, left_ops, right_ops, shift_map, sector_sizes, step_sizes, integrals):
    highest = lax.Precision.HIGHEST
    local_sec = wavefunction.shape[0]
    width = wavefunction.shape[1]
    sectors = sector_sizes.shape[0]
    count = lax.axis_size("ops") * left_ops.shape[0]
    first = lax.axis_index("sec") * local_sec
    local_sizes = lax.dynamic_slice_in_dim(sector_sizes, first, local_sec, 0)
    column = jnp.arange(width, dtype=jnp.int32)
    row_ok = (column[None, :] < local_sizes[:, None]).astype(jnp.float32)
    mask = row_ok[:, :, None] * row_ok[:, None, :]
    psi = wavefunction.astype(jnp.float32) * mask
    sources = first + jnp.arange(local_sec, dtype=jnp.int32)
    target = (sources[None, :] + shift_map[:, None]) % sectors
    routing = (jnp.arange(sectors, dtype=jnp.int32)[:, None, None] == target[None]).astype(
        jnp.float32
    )
    for step in range(ITERS):
        psi_low = psi.astype(jnp.bfloat16)
        inner = jnp.einsum(
            "kmn,snp->ksmp", left_ops, psi_low, preferred_element_type=jnp.float32
        ).astype(jnp.bfloat16)
        terms = jnp.einsum("ksmp,kqp->ksmq", inner, right_ops, preferred_element_type=jnp.float32)
        contrib = jnp.einsum("tks,ksmq->tmq", routing, terms, precision=highest)
        partial_rows = lax.psum_scatter(contrib, "ops", scatter_dimension=1, tiled=True)
        own_rows = lax.psum_scatter(
            partial_rows.astype(jnp.bfloat16), "sec", scatter_dimension=0, tiled=True
        ).astype(jnp.float32)
        hpsi = lax.all_gather(own_rows.astype(jnp.bfloat16), "ops", axis=1, tiled=True).astype(
            own_rows.dtype
        )
        factor = step_sizes[step].astype(jnp.float32) / (8.0 * math.sqrt(count))
        psi = mask * (psi - factor * hpsi)
        total = lax.psum(jnp.sum(psi * psi), "sec")
        psi = psi / jnp.sqrt(total / (sectors * width * width) + 1e-06)
    basis = broadcast(psi[0].astype(jnp.bfloat16), "sec", 0)
    col_count = width // lax.axis_size("sec")
    basis_cols = lax.dynamic_slice_in_dim(basis, lax.axis_index("sec") * col_count, col_count, 1)
    half = jnp.einsum("mp,kmn->kpn", basis, left_ops, preferred_element_type=jnp.float32).astype(
        jnp.bfloat16
    )
    rotated = (
        jnp.einsum("kpn,nq->kpq", half, basis_cols, preferred_element_type=jnp.float32) / width
    )
    padded = padded_2(rotated.astype(jnp.bfloat16), (("ops", 0),), 1).astype(rotated.dtype)
    mixed = (
        integrals[:, 0, None, None] * padded[:-2]
        + integrals[:, 1, None, None] * padded[1:-1]
        + integrals[:, 2, None, None] * padded[2:]
    )
    return (psi, mixed.astype(jnp.bfloat16))


def solution(mesh):
    placed = (
        P("sec", None, None),
        P("ops", None, None),
        P("ops", None, None),
        P("ops"),
        P(),
        P(),
        P("ops", None),
    )
    return jax.shard_map(
        shards,
        mesh=mesh,
        in_specs=placed,
        out_specs=(P("sec", None, None), P("ops", None, "sec")),
        check_vma=False,
    )
```

profile of v0, /device:TPU:1, one launch (start us, length us, event | category | flops | bytes accessed | tf_op | source)
XLA Modules:
  0.0 447.5 jit_solution(1569361862758402138)
XLA Ops:
  7.2 0.0 reduce-scatter.5.cloned.1.call-start
  7.2 0.8 dynamic_slice.6
  8.0 0.1 fusion.45
  8.8 6.5 %fusion.11 = f32[4,512,512]{2,1,0:T(8,128)} fusion(bf16[4,512,512]{2,1,0:T(8,128)(2,1)} %param.7, f32[4,512]{1,0:T(4,128)S(1)} %fusion.45, bf16[1,512,512]{2,1,0:T(8,128)(2,1)} %param.9, bf16[1,512,512]{2,1,0:T(8,128)(2,1)S(1)} %copy-done), kind=kOutput, calls=%fused_computation.15 | convolution fusion | flops 2152726528 | bytes 7348224 | tf_op jit(solution)/shard_map/ksmp,kqp->ksmq/dot_general | solution.py:55
  15.2 11.7 %fusion.2 = f32[8,512,512]{2,0,1:T(8,128)} fusion(f32[4,512,512]{2,1,0:T(8,128)} %fusion.11, s32[4]{0:T(128)S(1)} %and_select_fusion), kind=kOutput, calls=%fused_computation.5 | convolution fusion | flops 100663328 | bytes 12582928 | tf_op jit(solution)/shard_map/tks,ksmq->tmq/dot_general | solution.py:56
  26.9 0.0 reduce-scatter.5.cloned.1.call-update
  27.0 0.0 reduce-scatter.7.cloned.1.call-start
  27.0 105.3 %reduce-scatter.5.cloned.1.call-done = f32[8,32,512]{2,0,1:T(8,128)} async-done(((f32[8,512,512]{2,0,1:T(8,128)}), f32[8,32,512]{2,0,1:T(8,128)}) %reduce-scatter.5.cloned.1.call-update) | async-done | bytes 524304 | tf_op jit(solution)/shard_map/reduce_scatter | solution.py:57
  132.3 1.1 convert_element_type.92
  133.3 0.8 copy.22
  134.1 0.0 reduce-scatter.7.cloned.1.call-update
  134.2 0.0 all-gather.3.cloned.1.call-start
  134.2 12.5 %reduce-scatter.7.cloned.1.call-done = bf16[4,32,512]{2,1,0:T(8,128)(2,1)} async-done(((bf16[8,32,512]{2,1,0:T(8,128)(2,1)}), bf16[4,32,512]{2,1,0:T(8,128)(2,1)}) %reduce-scatter.7.cloned.1.call-update) | async-done | bytes 131088 | tf_op jit(solution)/shard_map/reduce_scatter | solution.py:58
  146.7 1.7 copy.23
  148.4 0.0 all-gather.3.cloned.1.call-update
  148.4 0.0 reduce-scatter.9.cloned.1.call-start
  148.4 0.6 fusion.56
  149.7 41.8 %all-gather.3.cloned.1.call-done = bf16[4,512,512]{2,0,1:T(4,128)(2,1)} async-done(((bf16[4,32,512]{2,0,1:T(4,128)(2,1)}), bf16[4,512,512]{2,0,1:T(4,128)(2,1)}) %all-gather.3.cloned.1.call-update) | async-done | bytes 2097168 | tf_op jit(solution)/shard_map/all_gather | solution.py:61
  191.5 3.8 multiply_reduce_fusion.1
  195.2 4.6 %psum.21 = f32[]{:T(128)} all-reduce(f32[]{:T(128)} %multiply_reduce_fusion.1), channel_id=1, replica_groups=mesh['ops'=16,'sec'=2] {'sec'}, use_global_device_ids=true, to_apply=%region_3.4 | all-reduce | flops 1 | bytes 8 | tf_op jit(solution)/shard_map/psum | solution.py:66
  200.5 7.0 %fusion.9 = f32[4,512,512]{2,1,0:T(8,128)} fusion(bf16[1,512,512]{2,1,0:T(8,128)(2,1)S(1)} %copy-done.5, bf16[1,512,512]{2,1,0:T(8,128)(2,1)S(1)} %copy-done, bf16[4,512,512]{2,1,0:T(8,128)(2,1)S(1)} %copy-done.1, f32[]{:T(128)S(6)} %sqrt.6, f32[]{:T(128)} %bitcast, f32[4,512]{1,0:T(4,128)S(1)} %fusion.45, bf16[4,512,512]{2,0,1:T(4,128)(2,1)} %all-gather.3.cloned.1.call-done), kind=kOutput, calls=%fused_computation.13 | convolution fusion | flops 2157969408 | bytes 9445384 | tf_op jit(solution)/shard_map/ksmp,kqp->ksmq/dot_general | solution.py:55
  207.5 11.7 %fusion = f32[8,512,512]{2,0,1:T(8,128)} fusion(f32[4,512,512]{2,1,0:T(8,128)} %fusion.9, s32[4]{0:T(128)S(1)} %and_select_fusion), kind=kOutput, calls=%fused_computation.3 | convolution fusion | flops 100663328 | bytes 12582928 | tf_op jit(solution)/shard_map/tks,ksmq->tmq/dot_general | solution.py:56
  219.2 0.0 reduce-scatter.9.cloned.1.call-update
  219.2 0.0 reduce-scatter.11.cloned.1.call-start
  219.2 102.7 %reduce-scatter.9.cloned.1.call-done = f32[8,32,512]{2,0,1:T(8,128)} async-done(((f32[8,512,512]{2,0,1:T(8,128)}), f32[8,32,512]{2,0,1:T(8,128)}) %reduce-scatter.9.cloned.1.call-update) | async-done | bytes 524304 | tf_op jit(solution)/shard_map/reduce_scatter | solution.py:57
  321.9 1.1 convert_element_type.99
  323.0 0.8 copy.28
  323.8 0.0 all-gather.5.cloned.1.call-start
  323.8 12.4 %reduce-scatter.11.cloned.1.call-done = bf16[4,32,512]{2,1,0:T(8,128)(2,1)} async-done(((bf16[8,32,512]{2,1,0:T(8,128)(2,1)}), bf16[4,32,512]{2,1,0:T(8,128)(2,1)}) %reduce-scatter.11.cloned.1.call-update) | async-done | bytes 131088 | tf_op jit(solution)/shard_map/reduce_scatter | solution.py:58
  336.2 1.7 copy.29
  337.9 0.0 all-gather.5.cloned.1.call-update
  337.9 0.0 all-reduce.2.cloned.1.call-start
  338.5 42.3 %all-gather.5.cloned.1.call-done = bf16[4,512,512]{2,0,1:T(4,128)(2,1)} async-done(((bf16[4,32,512]{2,0,1:T(4,128)(2,1)}), bf16[4,512,512]{2,0,1:T(4,128)(2,1)}) %all-gather.5.cloned.1.call-update) | async-done | bytes 2097168 | tf_op jit(solution)/shard_map/all_gather | solution.py:61
  380.8 4.8 %multiply_reduce_fusion = f32[]{:T(128)} fusion(f32[]{:T(128)} %bitcast.10, f32[4,512]{1,0:T(4,128)S(1)} %fusion.45, bf16[4,512,512]{2,0,1:T(4,128)(2,1)} %all-gather.5.cloned.1.call-done, f32[]{:T(128)S(6)} %sqrt.6, bf16[4,512,512]{2,0,1:T(4,128)(2,1)} %all-gather.3.cloned.1.call-done, f32[]{:T(128)} %bitcast, bf16[4,512,512]{2,1,0:T(8,128)(2,1)S(1)} %copy-done.1), kind=kLoop, calls=%fused_computation.7 | loop fusion | flops 14680063 | bytes 6299664 | tf_op jit(solution)/shard_map/reduce_sum | solution.py:66
  385.6 4.4 psum.22
  390.7 3.6 fusion.6
  394.3 2.0 copy-done.2
  396.3 0.8 fusion.32
  397.2 0.0 all-reduce.2.cloned.1.call-update
  397.2 28.1 %all-reduce.2.cloned.1.call-done = bf16[512,512]{1,0:T(8,128)(2,1)} async-done(((bf16[512,512]{1,0:T(8,128)(2,1)}), bf16[512,512]{1,0:T(8,128)(2,1)}) %all-reduce.2.cloned.1.call-update) | async-done | bytes 524304 | tf_op jit(solution)/shard_map/psum | solution.py:13
  425.4 1.8 fusion.30
  427.2 2.7 collective-permute-start.1
  429.9 3.0 collective-permute-start
  432.9 0.7 fusion.55
  433.6 1.4 collective-permute-done.1
  435.0 2.8 collective-permute-done
  437.8 0.1 maximum_convert_fusion
  438.0 2.7 fusion.34
  (13 shorter events, 0.1 us)
Async XLA Ops:
  7.2 1.6 copy-start
  7.2 125.1 %reduce-scatter.5.cloned.1.call-start = ((), (), s32[]{:S(2)}) async-start(), calls=%async_computation.4 | async-start | bytes 8912896 | tf_op jit(solution)/shard_map/reduce_scatter | solution.py:57
  26.9 121.5 %copy-start.4 = (s32[2]{0:T(128)S(1)}, s32[2]{0:T(128)}, u32[]{:S(2)}) copy-start(s32[2]{0:T(128)} %param.12) | copy-start | bytes 28
  26.9 164.5 %copy-start.1 = (bf16[4,512,512]{2,1,0:T(8,128)(2,1)S(1)}, bf16[4,512,512]{2,1,0:T(8,128)(2,1)}, u32[]{:S(2)}) copy-start(bf16[4,512,512]{2,1,0:T(8,128)(2,1)} %param.7) | copy-start | bytes 6291460
  27.0 173.5 %copy-start.5 = (bf16[1,512,512]{2,1,0:T(8,128)(2,1)S(1)}, bf16[1,512,512]{2,1,0:T(8,128)(2,1)}, u32[]{:S(2)}) copy-start(bf16[1,512,512]{2,1,0:T(8,128)(2,1)} %param.9) | copy-start | bytes 1572868
  27.0 119.7 %reduce-scatter.7.cloned.1.call-start = ((), (), s32[]{:S(2)}) async-start(), calls=%async_computation.5 | async-start | bytes 393216 | tf_op jit(solution)/shard_map/reduce_scatter | solution.py:58
  134.2 57.3 %all-gather.3.cloned.1.call-start = ((), (), s32[]{:S(2)}) async-start(), calls=%async_computation.6 | async-start | bytes 2228224 | tf_op jit(solution)/shard_map/all_gather | solution.py:61
  148.4 173.5 %reduce-scatter.9.cloned.1.call-start = ((), (), s32[]{:S(2)}) async-start(), calls=%async_computation.7 | async-start | bytes 8912896 | tf_op jit(solution)/shard_map/reduce_scatter | solution.py:57
  219.2 117.0 %reduce-scatter.11.cloned.1.call-start = ((), (), s32[]{:S(2)}) async-start(), calls=%async_computation.8 | async-start | bytes 393216 | tf_op jit(solution)/shard_map/reduce_scatter | solution.py:58
  323.8 57.0 %all-gather.5.cloned.1.call-start = ((), (), s32[]{:S(2)}) async-start(), calls=%async_computation.9 | async-start | bytes 2228224 | tf_op jit(solution)/shard_map/all_gather | solution.py:61
  337.9 87.5 %all-reduce.2.cloned.1.call-start = ((), (), s32[]{:S(2)}) async-start(), calls=%async_computation.10 | async-start | bytes 1048576 | tf_op jit(solution)/shard_map/psum | solution.py:13
  390.7 42.2 %copy-start.3 = (f32[1,3]{1,0:T(1,128)S(1)}, f32[1,3]{1,0:T(1,128)}, u32[]{:S(2)}) copy-start(f32[1,3]{1,0:T(1,128)} %param.13) | copy-start | bytes 40
  394.3 2.0 copy-start.2
  427.2 7.9 %collective-permute-start.1 = (bf16[1,512,256]{2,1,0:T(8,128)(2,1)S(1)}, bf16[1,512,256]{2,1,0:T(8,128)(2,1)S(1)}, u32[]{:S(2)}, u32[]{:S(2)}) collective-permute-start(bf16[1,512,256]{2,1,0:T(8,128)(2,1)S(1)} %fusion.30), channel_id=1, source_target_pairs={{2,0},{4,2},{6,4},{8,6},{10,8},{12,10},{14,12},{16,14},{18,16},{20... | collective-permute-start | bytes 786440 | tf_op jit(solution)/shard_map/ppermute | solution.py:26
  429.9 7.9 %collective-permute-start = (bf16[1,512,256]{2,1,0:T(8,128)(2,1)S(1)}, bf16[1,512,256]{2,1,0:T(8,128)(2,1)S(1)}, u32[]{:S(2)}, u32[]{:S(2)}) collective-permute-start(bf16[1,512,256]{2,1,0:T(8,128)(2,1)S(1)} %fusion.30), channel_id=1, source_target_pairs={{0,2},{2,4},{4,6},{6,8},{8,10},{10,12},{12,14},{14,16},{16,18},{18... | collective-permute-start | bytes 786440 | tf_op jit(solution)/shard_map/ppermute | solution.py:24
Sparse Core Ops, SparseCore 0:
  27.1 105.1 reduce-scatter.4
  135.1 11.5 reduce-scatter.6
  149.4 41.9 all-gather.2
  219.3 102.5 reduce-scatter.8
  324.5 11.6 reduce-scatter.10
  338.8 41.9 all-gather.4
  397.3 27.9 all-reduce.1
where the time goes:
time: 448 us; the launch traced here: 447 us
  waiting for transfers between devices  349 us (78%)
  matrix products  38.6 us (9%)
  other arithmetic  18 us (4%)
  between operations  17.5 us (4%)
  local copies, waits for them, and re-layouts  8.96 us (2%)
  blocking collectives  8.96 us (2%)
  starting transfers between devices  6.03 us (1%)
    reduce_scatter x2, waiting for transfers between devices, shards(): lax.psum_scatter(contrib, 'ops', scatter_dimension=1, tiled=True)  208 us
    all_gather x2, waiting for transfers between devices, shards(): lax.all_gather(own_rows.astype(jnp.bfloat16), 'ops', axis=1, tiled=True)  84.1 us
    psum x1, waiting for transfers between devices, broadcast(): return lax.psum(kept, axis)  28.1 us
    reduce_scatter x2, waiting for transfers between devices, shards(): lax.psum_scatter(partial_rows.astype(jnp.bfloat16), 'sec', scatter_dimens...  24.9 us
    dot_general x2, matrix products, shards(): contrib = jnp.einsum('tks,ksmq->tmq', routing, terms, precision=highest)  23.4 us
    dot_general x2, matrix products, shards(): jnp.einsum('ksmp,kqp->ksmq', inner, right_ops, preferred_element_type=jnp...  13.4 us
  transfers between devices with their start and end apart: 9, of which 9 were waited for; matrix products, arithmetic and copies ran while one was open for 0% of the time, Pallas kernels for 0%

commit v1 on v0

--- a/solution.py
+++ b/solution.py
@@ -1,11 +1,18 @@
+import functools
 import math
 
 import jax
 import jax.numpy as jnp
+import numpy as np
 from jax import lax
+from jax.experimental import pallas as pl
+from jax.experimental.pallas import tpu as pltpu
 from jax.sharding import PartitionSpec as P
 
 ITERS = 2
+GATHER_BYTES = 8 * 1024 * 1024
+VMEM = pltpu.MemorySpace.VMEM
+SMEM = pltpu.MemorySpace.SMEM
 
 
 def broadcast(value, axis, source):
@@ -30,7 +37,7 @@
     return cells
 
 
-def shards(wavefunction, left_ops, right_ops, shift_map, sector_sizes, step_sizes, integrals):
+def reduce_form(wavefunction, left_ops, right_ops, shift_map, sector_sizes, step_sizes, integrals):
     highest = lax.Precision.HIGHEST
     local_sec = wavefunction.shape[0]
     width = wavefunction.shape[1]
@@ -83,6 +90,366 @@
     return (psi, mixed.astype(jnp.bfloat16))
 
 
+def ring_order(chips):
+    return list(range(0, chips, 2)) + list(range(chips - 1, 0, -2))
+
+
+def swap_core(x, n):
+    return lax.ppermute(x, "ops", [(o, o ^ 1) for o in range(n)])
+
+
+def swap_sec(x):
+    return lax.ppermute(x, "sec", [(0, 1), (1, 0)])
+
+
+def along_ring(x, n, by):
+    order = ring_order(n // 2)
+    place = {chip: i for i, chip in enumerate(order)}
+    perm = []
+    for o in range(n):
+        chip = order[(place[o // 2] + by) % len(order)]
+        perm.append((o, 2 * chip + o % 2))
+    return lax.ppermute(x, "ops", perm)
+
+
+def ring_slots(n):
+    chips = n // 2
+    slots = [(0, 0, None)]
+    for step in range(1, chips // 2):
+        slots += [(-step, 0, None), (step, 0, None)]
+    slots += [(chips // 2, 0, 0), (chips // 2, 0, 1)]
+    return slots + [(d, 1, part) for d, _, part in slots]
+
+
+def ring_table(n):
+    order = ring_order(n // 2)
+    place = {chip: i for i, chip in enumerate(order)}
+    rows = []
+    for o in range(n):
+        at = place[o // 2]
+        rows.append([2 * order[(at + d) % len(order)] + ((o % 2) ^ c) for d, c, _ in ring_slots(n)])
+    return np.array(rows, np.int32)
+
+
+def ring_gather(x, n):
+    chips = n // 2
+    half = x.shape[0] // 2
+    up = down = x
+    own = [x]
+    for step in range(1, chips // 2):
+        up, down = along_ring(up, n, 1), along_ring(down, n, -1)
+        own += [up, down]
+    own += [along_ring(up[:half], n, 1), along_ring(down[half:], n, -1)]
+    return own + [swap_core(piece, n) for piece in own]
+
+
+def copy_in(pairs, sems):
+    copies = []
+    for i, (src, dst) in enumerate(pairs):
+        copy = pltpu.make_async_copy(src, dst, sems.at[i])
+        copy.start()
+        copies.append(copy)
+    return copies
+
+
+def place_inner(inner, left_ref, psi, shift_ref, sector, columns):
+    count, sectors, rows, _ = inner.shape
+    product = jnp.dot(left_ref[...], psi, preferred_element_type=jnp.float32).astype(jnp.bfloat16)
+    for k in range(count):
+        target = lax.rem(sector + shift_ref[k], sectors)
+        inner[k, target, :, columns] = product[k * rows : (k + 1) * rows]
+
+
+def first_kernel(scal_ref, shift_ref, sizes_ref, left_ref, own_ref, near_ref, far_ref, inner_ref):
+    core, sec = scal_ref[1], scal_ref[2]
+    local = own_ref.shape[0]
+    width = own_ref.shape[1]
+    for ref, base in (
+        (own_ref, sec * local),
+        (near_ref, (1 - sec) * local + core * (local // 2)),
+        (far_ref, (1 - sec) * local + (1 - core) * (local // 2)),
+    ):
+
+        @pl.loop(0, ref.shape[0])
+        def _(i):
+            sector = base + i
+            size = sizes_ref[sector]
+            psi = ref[i]
+            row = lax.broadcasted_iota(jnp.int32, psi.shape, 0)
+            col = lax.broadcasted_iota(jnp.int32, psi.shape, 1)
+            psi = jnp.where((row < size) & (col < size), psi, jnp.zeros_like(psi))
+            place_inner(inner_ref, left_ref, psi, shift_ref, sector, slice(0, width))
+
+
+def second_stage(inner, right, acc):
+    count, sectors, rows, width = inner.shape
+    acc[...] = jnp.zeros_like(acc)
+
+    @pl.loop(0, count)
+    def _(k):
+        lhs = inner[k].reshape(sectors * rows, width)
+        acc[...] += lax.dot_general(
+            lhs, right[k], (((1,), (1,)), ((), ())), preferred_element_type=jnp.float32
+        )
+
+
+def step_rows(psi, acc, sizes_ref, scal_ref, factor, sector):
+    rows, cols = psi.shape
+    size = sizes_ref[sector]
+    row = lax.broadcasted_iota(jnp.int32, psi.shape, 0) + scal_ref[0] * rows
+    col = lax.broadcasted_iota(jnp.int32, psi.shape, 1) + scal_ref[2] * cols
+    moved = psi - factor * acc[sector * rows : (sector + 1) * rows]
+    return jnp.where((row < size) & (col < size), moved, 0.0)
+
+
+def right_pairs(table_ref, pieces, right, slots):
+    half = right.shape[1] // 2
+    pairs = []
+    for i, (piece, (_, _, part)) in enumerate(zip(pieces, slots)):
+        k = table_ref[i]
+        if part is None:
+            pairs.append((piece, right.at[k]))
+        else:
+            pairs.append((piece, right.at[k, part * half : (part + 1) * half]))
+    return pairs
+
+
+def iter1_kernel(slots, *refs):
+    n_slots = len(slots)
+    scal_ref, table_ref, sizes_ref, factor_ref, inner, own_ref, near_ref, far_ref = refs[:8]
+    pieces = refs[8 : 8 + n_slots]
+    out_ref, send_ref, right, start, acc, sems = refs[8 + n_slots :]
+    o, core, sec = scal_ref[0], scal_ref[1], scal_ref[2]
+    local = own_ref.shape[0]
+    _, rows, cols = out_ref.shape
+    here = (pl.ds(o * rows, rows), pl.ds(sec * cols, cols))
+    foreign = (1 - sec) * local
+    pairs = right_pairs(table_ref, pieces, right, slots)
+    pairs += [
+        (own_ref.at[(slice(None),) + here], start.at[pl.ds(sec * local, local)]),
+        (near_ref.at[(slice(None),) + here], start.at[pl.ds(foreign + core * (local // 2), local // 2)]),
+        (far_ref.at[(slice(None),) + here], start.at[pl.ds(foreign + (1 - core) * (local // 2), local // 2)]),
+    ]
+    for copy in copy_in(pairs, sems):
+        copy.wait()
+    second_stage(inner, right, acc)
+    for s in range(out_ref.shape[0]):
+        moved = step_rows(start[s].astype(jnp.float32), acc, sizes_ref, scal_ref, factor_ref[0], s)
+        out_ref[s] = moved
+        send_ref[s] = moved.astype(jnp.bfloat16)
+
+
+def split_3(value):
+    parts = []
+    for _ in range(3):
+        low = value.astype(jnp.bfloat16)
+        parts.append(low)
+        value = value - low.astype(jnp.float32)
+    return parts
+
+
+def iter2_kernel(slots, *refs):
+    n_slots = len(slots)
+    scal_ref, table_ref, shift_ref, sizes_ref, factor_ref, left_ref, prev_ref = refs[:7]
+    psi_pieces = refs[7 : 7 + n_slots]
+    right_pieces = refs[7 + n_slots : 7 + 2 * n_slots]
+    keep_ref, send_ref, psi, inner, right, acc, low, psems, rsems = refs[7 + 2 * n_slots :]
+    sec = scal_ref[2]
+    sectors, rows, cols = prev_ref.shape
+    local = sectors // 2
+    pairs = []
+    for i, (piece, (_, _, part)) in enumerate(zip(psi_pieces, slots)):
+        at = pl.ds(table_ref[i] * rows, rows)
+        for h in range(2) if part is None else (part,):
+            side = sec if h == 0 else 1 - sec
+            pairs.append((piece.at[h if part is None else 0], psi.at[side, :, at]))
+    psi_copies = copy_in(pairs, psems)
+    right_copies = copy_in(right_pairs(table_ref, right_pieces, right, slots), rsems)
+    for copy in psi_copies:
+        copy.wait()
+
+    @pl.loop(0, sectors)
+    def _(s):
+        for h in range(2):
+            place_inner(inner, left_ref, psi[h, s], shift_ref, s, slice(h * cols, (h + 1) * cols))
+
+    for copy in right_copies:
+        copy.wait()
+    second_stage(inner, right, acc)
+    before = jnp.zeros((rows, cols), jnp.float32)
+    after = jnp.zeros((rows, cols), jnp.float32)
+    for s in range(sectors):
+        old = prev_ref[s]
+        moved = step_rows(old, acc, sizes_ref, scal_ref, factor_ref[0], s)
+        low[s] = moved.astype(jnp.bfloat16)
+        before += old * old
+        after += moved * moved
+    for i in range(local):
+        keep_ref[i * rows : (i + 1) * rows] = low[sec * local + i]
+        send_ref[i * rows : (i + 1) * rows] = low[(1 - sec) * local + i]
+    keep_ref[local * rows : (local + 1) * rows] = low[0]
+    send_ref[local * rows : (local + 1) * rows] = low[0]
+    tail = keep_ref.shape[0] - (local + 1) * rows
+    line = lax.broadcasted_iota(jnp.int32, (tail, cols), 0)
+    stats = jnp.zeros((tail, cols), jnp.float32)
+    for i, total in enumerate((before, after)):
+        parts = split_3(jnp.full((tail, cols), jnp.sum(total), jnp.float32))
+        for p, low_part in enumerate(parts):
+            stats = jnp.where(line == 3 * i + p, low_part.astype(jnp.float32), stats)
+    keep_ref[(local + 1) * rows :] = stats.astype(jnp.bfloat16)
+    send_ref[(local + 1) * rows :] = stats.astype(jnp.bfloat16)
+
+
+def final_kernel(slots, values, *refs):
+    n_slots = len(slots)
+    scal_ref, table_ref, mixer_ref = refs[:3]
+    pieces = refs[3 : 3 + n_slots]
+    wave_ref, mixed_ref, basis, sems = refs[3 + n_slots :]
+    sec = scal_ref[2]
+    local, width, _ = wave_ref.shape
+    cols = width // 2
+    n = n_slots - 2
+    rows = width // n
+    tail = pieces[0].shape[1] - (local + 1) * rows
+    stats = jnp.zeros((tail, cols), jnp.float32)
+    views = []
+    for i, (piece, (_, _, part)) in enumerate(zip(pieces, slots)):
+        at = pl.ds(pl.multiple_of(table_ref[i] * rows, rows), rows)
+        for h in range(2) if part is None else (part,):
+            side = sec if h == 0 else 1 - sec
+            across = pl.ds(pl.multiple_of(side * cols, cols), cols)
+            view = piece.at[h if part is None else 0]
+            views.append((view, at, across))
+            stats += view[(local + 1) * rows :].astype(jnp.float32)
+            basis[at, across] = view[local * rows : (local + 1) * rows]
+    line = lax.broadcasted_iota(jnp.int32, (tail, cols), 0)
+    first = jnp.sum(jnp.where(line < 3, stats, 0.0), axis=0, keepdims=True)[:, :1]
+    second = jnp.sum(jnp.where((line >= 3) & (line < 6), stats, 0.0), axis=0, keepdims=True)[:, :1]
+    norm_1 = jnp.sqrt(first / values + 1e-06)
+    norm_2 = jnp.sqrt(second / (norm_1 * norm_1) / values + 1e-06)
+    scale = 1.0 / (norm_1 * norm_2)
+    for s in range(local):
+        for view, at, across in views:
+            wave_ref[s, at, across] = view[s * rows : (s + 1) * rows].astype(jnp.float32) * scale
+    across = pl.ds(pl.multiple_of(sec * cols, cols), cols)
+    right = jnp.dot(mixer_ref[...], basis[:, across], preferred_element_type=jnp.float32)
+    rotated = lax.dot_general(
+        basis[...], right.astype(jnp.bfloat16), (((0,), (0,)), ((), ())), preferred_element_type=jnp.float32
+    )
+    mixed_ref[...] = (rotated * (scale * scale / width)).astype(jnp.bfloat16)
+
+
+def gather_form(wavefunction, left_ops, right_ops, shift_map, sector_sizes, step_sizes, integrals):
+    f32, bf16 = jnp.float32, jnp.bfloat16
+    n = lax.axis_size("ops")
+    local, width, _ = wavefunction.shape
+    sectors = sector_sizes.shape[0]
+    rows, cols = width // n, width // 2
+    o, sec = lax.axis_index("ops"), lax.axis_index("sec")
+    core = lax.rem(o, 2)
+    slots = ring_slots(n)
+    n_slots = len(slots)
+    scal = jnp.stack([o, core, sec]).astype(jnp.int32)
+    table = lax.dynamic_slice_in_dim(jnp.asarray(ring_table(n)), o, 1, 0)[0]
+    factors = step_sizes.astype(f32) / (8.0 * math.sqrt(n))
+    any_spec = pl.BlockSpec(memory_space=pl.ANY)
+    vmem_spec = pl.BlockSpec(memory_space=VMEM)
+    smem_spec = pl.BlockSpec(memory_space=SMEM)
+    params = pltpu.CompilerParams(vmem_limit_bytes=56 * 1024 * 1024)
+
+    right_cols = lax.dynamic_slice_in_dim(right_ops[0], sec * cols, cols, 0)
+    part = lax.dynamic_slice_in_dim(wavefunction, core * (local // 2), local // 2, 0)
+    near = swap_sec(part)
+    far = swap_core(near, n)
+    right_pieces = ring_gather(right_cols, n)
+    shifts = lax.all_gather(shift_map, "ops", tiled=True)
+    left_rows = lax.all_to_all(left_ops[0], "ops", 0, 0, tiled=True)
+
+    inner = pl.pallas_call(
+        first_kernel,
+        out_shape=jax.ShapeDtypeStruct((n, sectors, rows, width), bf16),
+        in_specs=[smem_spec] * 3 + [vmem_spec] * 4,
+        out_specs=vmem_spec,
+        compiler_params=params,
+        cost_estimate=pl.CostEstimate(flops=2 * sectors * width**3, bytes_accessed=2 * 2 * sectors * width**2, transcendentals=0),
+    )(scal, shifts, sector_sizes, left_rows, wavefunction, near, far)
+
+    psi_1, low_1 = pl.pallas_call(
+        functools.partial(iter1_kernel, slots),
+        out_shape=(
+            jax.ShapeDtypeStruct((sectors, rows, cols), f32),
+            jax.ShapeDtypeStruct((sectors, rows, cols), bf16),
+        ),
+        in_specs=[smem_spec] * 4 + [vmem_spec] + [any_spec] * (3 + n_slots),
+        out_specs=(vmem_spec, vmem_spec),
+        scratch_shapes=[
+            pltpu.VMEM((n, cols, width), bf16),
+            pltpu.VMEM((sectors, rows, cols), bf16),
+            pltpu.VMEM((sectors * rows, cols), f32),
+            pltpu.SemaphoreType.DMA((n_slots + 3,)),
+        ],
+        compiler_params=params,
+        cost_estimate=pl.CostEstimate(flops=2 * sectors * width**2 * cols, bytes_accessed=2 * 2 * sectors * width**2, transcendentals=0),
+    )(scal, table, sector_sizes, factors[:1], inner, wavefunction, near, far, *right_pieces)
+
+    chunk = jnp.stack([low_1, swap_sec(low_1)])
+    psi_pieces = ring_gather(chunk, n)
+
+    below = lax.ppermute(left_ops[0], "ops", [(i, i + 1) for i in range(n - 1)])
+    above = lax.ppermute(left_ops[0], "ops", [(i + 1, i) for i in range(n - 1)])
+    mixer = (
+        integrals[0, 0] * below.astype(f32)
+        + integrals[0, 1] * left_ops[0].astype(f32)
+        + integrals[0, 2] * above.astype(f32)
+    ).astype(bf16)
+
+    message = (local + 1) * rows + 16
+    keep, send = pl.pallas_call(
+        functools.partial(iter2_kernel, slots),
+        out_shape=(jax.ShapeDtypeStruct((message, cols), bf16),) * 2,
+        in_specs=[smem_spec] * 5 + [vmem_spec] * 2 + [any_spec] * (2 * n_slots),
+        out_specs=(vmem_spec, vmem_spec),
+        scratch_shapes=[
+            pltpu.VMEM((2, sectors, width, cols), bf16),
+            pltpu.VMEM((n, sectors, rows, width), bf16),
+            pltpu.VMEM((n, cols, width), bf16),
+            pltpu.VMEM((sectors * rows, cols), f32),
+            pltpu.VMEM((sectors, rows, cols), bf16),
+            pltpu.SemaphoreType.DMA((2 * n,)),
+            pltpu.SemaphoreType.DMA((n_slots,)),
+        ],
+        compiler_params=params,
+        cost_estimate=pl.CostEstimate(flops=3 * sectors * width**3, bytes_accessed=2 * 2 * sectors * width**2, transcendentals=0),
+    )(scal, table, shifts, sector_sizes, factors[1:2], left_rows, psi_1, *psi_pieces, *right_pieces)
+
+    last = jnp.stack([keep, swap_sec(send)])
+    last_pieces = ring_gather(last, n)
+
+    wave, mixed = pl.pallas_call(
+        functools.partial(final_kernel, slots, float(sectors * width * width)),
+        out_shape=(
+            jax.ShapeDtypeStruct((local, width, width), f32),
+            jax.ShapeDtypeStruct((width, cols), bf16),
+        ),
+        in_specs=[smem_spec] * 2 + [vmem_spec] * (1 + n_slots),
+        out_specs=(vmem_spec, vmem_spec),
+        scratch_shapes=[pltpu.VMEM((width, width), bf16), pltpu.SemaphoreType.DMA((1,))],
+        compiler_params=params,
+        cost_estimate=pl.CostEstimate(flops=2 * width**3, bytes_accessed=6 * local * width**2, transcendentals=0),
+    )(scal, table, mixer, *last_pieces)
+    return (wave, mixed[None])
+
+
+def shards(wavefunction, left_ops, right_ops, *rest):
+    n, halves = lax.axis_size("ops"), lax.axis_size("sec")
+    width = right_ops.shape[1]
+    gathered = 2 * n * right_ops.size // halves
+    fits = gathered <= GATHER_BYTES and halves == 2 and right_ops.shape[0] == 1
+    aligned = n % 4 == 0 and width % (16 * n) == 0 and width % 256 == 0 and wavefunction.shape[0] % 2 == 0
+    form = gather_form if fits and aligned else reduce_form
+    return form(wavefunction, left_ops, right_ops, *rest)
+
+
 def solution(mesh):
     placed = (
         P("sec", None, None),

time: 448 us -> 206 us (0.46)
  waiting for transfers between devices: 349 us -> 75.9 us
  starting transfers between devices: 6.03 us -> 61.9 us
  matrix products: 38.6 us -> 0 us
  Pallas kernels: 0 us -> 38.5 us
  between operations: 17.5 us -> 1.86 us
  other arithmetic: 18 us -> 6.07 us
    reduce_scatter x4 -> x0, waiting for transfers between devices: 233 us -> none  [the longest x2 208 us: shards(): lax.psum_scatter(contrib, 'ops', scatter_dimension=1, tiled=True)]
    all_gather x2 -> x0, waiting for transfers between devices: 84.1 us -> none  [shards(): lax.all_gather(own_rows.astype(jnp.bfloat16), 'ops', axis=1, tiled=True)]
    ppermute x2 -> x57, waiting for transfers between devices: 4.25 us -> 75.9 us  [the longest x24 53.9 us: along_ring(): return lax.ppermute(x, 'ops', perm)]
    ppermute x2 -> x57, starting transfers between devices: 5.74 us -> 55.8 us  [the longest x28 26 us: swap_core(): return lax.ppermute(x, 'ops', [(o, o ^ 1) for o in range(n)])]
    dot_general x5 -> x0, matrix products: 38.6 us -> none  [the longest x2 23.4 us: shards(): contrib = jnp.einsum('tks,ksmq->tmq', routing, terms, precision=highest)]
    pallas_call x0 -> x4, Pallas kernels: none -> 38.5 us  [the longest x1 14.6 us: gather_form(): pl.pallas_call(functools.partial(iter2_kernel, slots), out_shape=(jax.Sha...]
    psum x1 -> x0, waiting for transfers between devices: 28.1 us -> none  [broadcast(): return lax.psum(kept, axis)]
    unnamed x0 -> x1, blocking collectives: none -> 9.69 us
  transfers between devices with their start and end apart: 9 -> 58, of which waited for: 9 -> 15; matrix products, arithmetic and copies ran while one was open for 0% -> 5% of each run, Pallas kernels for 0% -> 4%
where the time goes in v1:
time: 206 us
  waiting for transfers between devices  75.9 us (37%)
  starting transfers between devices  61.9 us (30%)
  Pallas kernels  38.5 us (19%)
  local copies, waits for them, and re-layouts  11.6 us (6%)
  blocking collectives  9.69 us (5%)
  other arithmetic  6.07 us (3%)
    ppermute x24, waiting for transfers between devices, along_ring(): return lax.ppermute(x, 'ops', perm)  53.9 us
    ppermute x28, starting transfers between devices, swap_core(): return lax.ppermute(x, 'ops', [(o, o ^ 1) for o in range(n)])  26 us
    ppermute x3, waiting for transfers between devices, swap_sec(): return lax.ppermute(x, 'sec', [(0, 1), (1, 0)])  21 us
    ppermute x24, starting transfers between devices, along_ring(): return lax.ppermute(x, 'ops', perm)  18.6 us
    pallas_call x1, Pallas kernels, gather_form(): pl.pallas_call(functools.partial(iter2_kernel, slots), out_shape=(jax.Sha...  14.6 us
    pallas_call x1, Pallas kernels, gather_form(): pl.pallas_call(functools.partial(iter1_kernel, slots), out_shape=(jax.Sha...  10.3 us
    unnamed x1, blocking collectives  9.69 us
    pallas_call x1, Pallas kernels, gather_form(): pl.pallas_call(first_kernel, out_shape=jax.ShapeDtypeStruct((n, sectors,...  8.53 us
  transfers between devices with their start and end apart: 58, of which 15 were waited for; matrix products, arithmetic and copies ran while one was open for 5% of the time, Pallas kernels for 4%

profile of v1, /device:TPU:1, one launch (start us, length us, event | category | flops | bytes accessed | tf_op | source)
XLA Modules:
  0.0 205.6 jit_solution(11340790654688138660)
XLA Ops:
  0.7 1.4 constant_dynamic-slice_fusion
  2.0 2.1 %collective-permute-start.2 = (bf16[2,512,512]{2,1,0:T(8,128)(2,1)S(1)}, bf16[2,512,512]{2,1,0:T(8,128)(2,1)S(1)}, u32[]{:S(2)}, u32[]{:S(2)}) collective-permute-start(bf16[2,512,512]{2,1,0:T(8,128)(2,1)S(1)} %constant_dynamic-slice_fusion), channel_id=1, source_target_pairs={{0,1},{1,0},{2,3},{3,2},{4,5},{5,4},{6,7},{7,6},{8,9},{9,8},{10,11... | collective-permute-start | bytes 3145736 | tf_op jit(solution)/shard_map/ppermute | solution.py:102
  4.2 1.3 collective-permute-start.4
  5.7 5.5 %collective-permute-done.4.refs_9_.refs_26_ = bf16[256,512]{1,0:T(8,128)(2,1)} collective-permute-done((bf16[256,512]{1,0:T(8,128)(2,1)S(1)}, bf16[256,512]{1,0:T(8,128)(2,1)}, u32[]{:S(2)}, u32[]{:S(2)}) %collective-permute-start.4) | collective-permute-done | bytes 262176 | tf_op jit(solution)/shard_map/ppermute | solution.py:112
  11.2 1.3 collective-permute-start.6
  12.5 14.5 %collective-permute-done.2.near_ref.refs_6_ = bf16[2,512,512]{2,1,0:T(8,128)(2,1)S(1)} collective-permute-done((bf16[2,512,512]{2,1,0:T(8,128)(2,1)S(1)}, bf16[2,512,512]{2,1,0:T(8,128)(2,1)S(1)}, u32[]{:S(2)}, u32[]{:S(2)}) %collective-permute-start.2) | collective-permute-done | bytes 1048608 | tf_op jit(solution)/shard_map/ppermute | solution.py:102
  27.0 1.3 collective-permute-start.3
  28.3 6.2 %all-to-all-start = ((bf16[16,32,512]{2,1,0:T(8,128)(2,1)}), bf16[16,32,512]{2,1,0:T(8,128)(2,1)S(1)}, u32[]{:S(2)}, u32[]{:S(2)}) async-start(bf16[16,32,512]{2,1,0:T(8,128)(2,1)} %bitcast.22), calls=%async_computation | async-start | bytes 1048576 | tf_op jit(solution)/shard_map/all_to_all | solution.py:366
  34.4 1.4 collective-permute-start.7
  36.5 14.2 %collective-permute-done.7.refs_12_.refs_29_ = bf16[256,512]{1,0:T(8,128)(2,1)S(1)} collective-permute-done((bf16[256,512]{1,0:T(8,128)(2,1)}, bf16[256,512]{1,0:T(8,128)(2,1)S(1)}, u32[]{:S(2)}, u32[]{:S(2)}) %collective-permute-start.7) | collective-permute-done | bytes 262176 | tf_op jit(solution)/shard_map/ppermute | solution.py:112
  50.7 1.0 collective-permute-start.13
  53.2 7.3 %collective-permute-done.9.refs_14_.refs_31_ = bf16[256,512]{1,0:T(8,128)(2,1)} collective-permute-done((bf16[256,512]{1,0:T(8,128)(2,1)S(1)}, bf16[256,512]{1,0:T(8,128)(2,1)}, u32[]{:S(2)}, u32[]{:S(2)}) %collective-permute-start.9) | collective-permute-done | bytes 262176 | tf_op jit(solution)/shard_map/ppermute | solution.py:112
  60.5 1.2 collective-permute-start.10
  62.9 1.2 dynamic-slice.1
  64.9 1.6 slice.45
  66.8 1.2 fusion.refs_1_
  68.0 9.7 %all-reduce.shift_ref.refs_2_ = s32[16]{0:T(128)} all-reduce(s32[16]{0:T(128)S(1)} %dynamic-update-slice), channel_id=1, replica_groups=mesh['ops'=16,'sec'=2] {'ops'}, use_global_device_ids=true, to_apply=%add | all-reduce | flops 16 | bytes 128
  77.7 3.1 %collective-permute-start.16 = (bf16[256,512]{1,0:T(8,128)(2,1)}, bf16[256,512]{1,0:T(8,128)(2,1)}, u32[]{:S(2)}, u32[]{:S(2)}) collective-permute-start(bf16[256,512]{1,0:T(8,128)(2,1)} %copy-done.11), channel_id=1, source_target_pairs={{0,2},{2,0},{4,6},{6,4},{8,10},{10,8},{12,14},{14,12},{16,18},{18,... | collective-permute-start | bytes 786440 | tf_op jit(solution)/shard_map/ppermute | solution.py:98
  83.2 8.5 %shard_map.95.refs_4_ = bf16[16,8,32,512]{3,2,1,0:T(8,128)(2,1)} custom-call(s32[3]{0:T(128)} %pad_add_fusion.scal_ref.refs_0_, s32[16]{0:T(128)} %all-reduce.shift_ref.refs_2_, s32[8]{0:T(128)} %refs_3_.1, bf16[512,512]{1,0:T(8,128)(2,1)} %bitcast.20, bf16[4,512,512]{2,1,0:T(8,128)(2,1)} %refs_5_.1, bf16[2,512,512]{2,1,0:T(8,128)(2,1)} %copy-done.1, ...), custom_call_target="tpu_custom_call" | custom-call | flops 2147483648 | bytes 8388608 | tf_op jit(solution)/shard_map/pallas_call | solution.py:368
  92.4 10.3 %shard_map.96 = (f32[8,32,256]{2,1,0:T(8,128)}, bf16[8,32,256]{2,1,0:T(8,128)(2,1)}) custom-call(s32[3]{0:T(128)} %pad_add_fusion.scal_ref.refs_0_, s32[18]{0:T(128)} %fusion.refs_1_, s32[8]{0:T(128)} %refs_3_.1, f32[1]{0:T(128)} %get-tuple-element.14.refs_3_, bf16[16,8,32,512]{3,2,1,0:T(8,128)(2,1)} %shard_map.95.refs_4_, bf16[4,512,512]{2,1,0:T(8,128)(2,1)} %refs_5_.1, ...), custom_call_target="tpu_custom_call" | custom-call | flops 1073741824 | bytes 8388608 | tf_op jit(solution)/shard_map/pallas_call | solution.py:377
  102.7 1.3 collective-permute-start.21
  104.0 3.7 %collective-permute-done.21 = bf16[8,32,256]{2,1,0:T(8,128)(2,1)S(1)} collective-permute-done((bf16[8,32,256]{2,1,0:T(8,128)(2,1)}, bf16[8,32,256]{2,1,0:T(8,128)(2,1)S(1)}, u32[]{:S(2)}, u32[]{:S(2)}) %collective-permute-start.21) | collective-permute-done | bytes 131104 | tf_op jit(solution)/shard_map/ppermute | solution.py:102
  107.7 0.9 pad_maximum_fusion.refs_7_
  108.6 1.5 collective-permute-start.22
  110.1 5.2 %collective-permute-done.22.refs_8_ = bf16[2,8,32,256]{3,2,1,0:T(8,128)(2,1)S(1)} collective-permute-done((bf16[2,8,32,256]{3,2,1,0:T(8,128)(2,1)S(1)}, bf16[2,8,32,256]{3,2,1,0:T(8,128)(2,1)S(1)}, u32[]{:S(2)}, u32[]{:S(2)}) %collective-permute-start.22) | collective-permute-done | bytes 262176 | tf_op jit(solution)/shard_map/ppermute | solution.py:112
  115.3 1.4 collective-permute-start.24
  116.8 4.3 %collective-permute-done.24.refs_10_ = bf16[2,8,32,256]{3,2,1,0:T(8,128)(2,1)S(1)} collective-permute-done((bf16[2,8,32,256]{3,2,1,0:T(8,128)(2,1)S(1)}, bf16[2,8,32,256]{3,2,1,0:T(8,128)(2,1)S(1)}, u32[]{:S(2)}, u32[]{:S(2)}) %collective-permute-start.24) | collective-permute-done | bytes 262176 | tf_op jit(solution)/shard_map/ppermute | solution.py:112
  121.1 1.4 collective-permute-start.26
  122.6 3.5 %collective-permute-start.30 = (bf16[2,8,32,256]{3,2,1,0:T(8,128)(2,1)S(1)}, bf16[2,8,32,256]{3,2,1,0:T(8,128)(2,1)S(1)}, u32[]{:S(2)}, u32[]{:S(2)}) collective-permute-start(bf16[2,8,32,256]{3,2,1,0:T(8,128)(2,1)S(1)} %pad_maximum_fusion.refs_7_), channel_id=1, source_target_pairs={{0,2},{2,0},{4,6},{6,4},{8,10},{10,8},{12,14},{14,12},{16,18},{18,... | collective-permute-start | bytes 786440 | tf_op jit(solution)/shard_map/ppermute | solution.py:98
  126.6 3.8 %collective-permute-start.33 = (bf16[2,8,32,256]{3,2,1,0:T(8,128)(2,1)S(1)}, bf16[2,8,32,256]{3,2,1,0:T(8,128)(2,1)S(1)}, u32[]{:S(2)}, u32[]{:S(2)}) collective-permute-start(bf16[2,8,32,256]{3,2,1,0:T(8,128)(2,1)S(1)} %collective-permute-done.24.refs_10_), channel_id=1, source_target_pairs={{0,2},{2,0},{4,6},{6,4},{8,10},{10,8},{12,14},{14,12},{16,18},{18,... | collective-permute-start | bytes 786440 | tf_op jit(solution)/shard_map/ppermute | solution.py:98
  130.4 1.7 collective-permute-start.34
  132.7 1.0 collective-permute-start.29
  134.4 2.9 %collective-permute-done.28.refs_14_ = bf16[1,8,32,256]{3,2,1,0:T(8,128)(2,1)S(1)} collective-permute-done((bf16[1,8,32,256]{3,2,1,0:T(8,128)(2,1)S(1)}, bf16[1,8,32,256]{3,2,1,0:T(8,128)(2,1)S(1)}, u32[]{:S(2)}, u32[]{:S(2)}) %collective-permute-start.28) | collective-permute-done | bytes 131104 | tf_op jit(solution)/shard_map/ppermute | solution.py:112
  140.5 14.6 %shard_map.97 = (bf16[176,256]{1,0:T(8,128)(2,1)}, bf16[176,256]{1,0:T(8,128)(2,1)}) custom-call(s32[3]{0:T(128)} %pad_add_fusion.scal_ref.refs_0_, s32[18]{0:T(128)} %fusion.refs_1_, s32[16]{0:T(128)} %all-reduce.shift_ref.refs_2_, s32[8]{0:T(128)} %refs_3_.1, f32[1]{0:T(128)} %get-tuple-element.15.refs_4_, bf16[512,512]{1,0:T(8,128)(2,1)} %bitcast.21, ...), custom_call_target="tpu_custom_call" | custom-call | flops 3221225472 | bytes 8388608 | tf_op jit(solution)/shard_map/pallas_call | solution.py:407
  155.1 1.3 collective-permute-start.39
  156.4 2.8 %collective-permute-done.39 = bf16[176,256]{1,0:T(8,128)(2,1)S(1)} collective-permute-done((bf16[176,256]{1,0:T(8,128)(2,1)}, bf16[176,256]{1,0:T(8,128)(2,1)S(1)}, u32[]{:S(2)}, u32[]{:S(2)}) %collective-permute-start.39) | collective-permute-done | bytes 90144 | tf_op jit(solution)/shard_map/ppermute | solution.py:102
  161.6 4.6 %collective-permute-start = (bf16[512,512]{1,0:T(8,128)(2,1)S(1)}, bf16[512,512]{1,0:T(8,128)(2,1)S(1)}, u32[]{:S(2)}, u32[]{:S(2)}) collective-permute-start(bf16[512,512]{1,0:T(8,128)(2,1)S(1)} %bitcast.23), channel_id=1, source_target_pairs={{0,2},{2,4},{4,6},{6,8},{8,10},{10,12},{12,14},{14,16},{16,18},{18... | collective-permute-start | bytes 1572872 | tf_op jit(solution)/shard_map/ppermute | solution.py:398
  166.2 1.9 collective-permute-start.1
  168.2 1.4 collective-permute-start.43
  169.7 4.3 %collective-permute-done.42.refs_6_ = bf16[2,176,256]{2,1,0:T(8,128)(2,1)S(1)} collective-permute-done((bf16[2,176,256]{2,1,0:T(8,128)(2,1)S(1)}, bf16[2,176,256]{2,1,0:T(8,128)(2,1)S(1)}, u32[]{:S(2)}, u32[]{:S(2)}) %collective-permute-start.42) | collective-permute-done | bytes 180256 | tf_op jit(solution)/shard_map/ppermute | solution.py:112
  174.0 7.8 %collective-permute-done.43.refs_7_ = bf16[2,176,256]{2,1,0:T(8,128)(2,1)S(1)} collective-permute-done((bf16[2,176,256]{2,1,0:T(8,128)(2,1)S(1)}, bf16[2,176,256]{2,1,0:T(8,128)(2,1)S(1)}, u32[]{:S(2)}, u32[]{:S(2)}) %collective-permute-start.43) | collective-permute-done | bytes 180256 | tf_op jit(solution)/shard_map/ppermute | solution.py:112
  181.8 1.9 collective-permute-start.45
  183.7 1.1 collective-permute-start.48
  184.8 3.4 %collective-permute-start.50 = (bf16[2,176,256]{2,1,0:T(8,128)(2,1)S(1)}, bf16[2,176,256]{2,1,0:T(8,128)(2,1)S(1)}, u32[]{:S(2)}, u32[]{:S(2)}) collective-permute-start(bf16[2,176,256]{2,1,0:T(8,128)(2,1)S(1)} %collective-permute-done.41.refs_5_), channel_id=1, source_target_pairs={{0,2},{2,0},{4,6},{6,4},{8,10},{10,8},{12,14},{14,12},{16,18},{18,... | collective-permute-start | bytes 540680 | tf_op jit(solution)/shard_map/ppermute | solution.py:98
  189.1 1.7 collective-permute-start.47
  192.3 1.5 collective-permute-done.46.refs_10_
  196.0 3.0 %add_convert_fusion.refs_2_ = bf16[512,512]{1,0:T(8,128)(2,1)} fusion(bf16[512,512]{1,0:T(8,128)(2,1)S(1)} %collective-permute-done.1, bf16[512,512]{1,0:T(8,128)(2,1)S(1)} %collective-permute-done, f32[]{:T(128)} %bitcast.7, f32[]{:T(128)} %bitcast.6, f32[]{:T(128)} %bitcast.4, bf16[1,512,512]{2,1,0:T(8,128)(2,1)S(1)} %copy-done.4), kind=kLoop, calls=%fused_computation | loop fusion | flops 2359296 | bytes 2097164 | tf_op jit(solution)/shard_map/convert_element_type | solution.py:404
  200.5 5.1 %shard_map.98 = (f32[4,512,512]{2,1,0:T(8,128)}, bf16[512,256]{1,0:T(8,128)(2,1)}) custom-call(s32[3]{0:T(128)} %pad_add_fusion.scal_ref.refs_0_, s32[18]{0:T(128)} %fusion.refs_1_, bf16[512,512]{1,0:T(8,128)(2,1)} %add_convert_fusion.refs_2_, bf16[2,176,256]{2,1,0:T(8,128)(2,1)} %copy-done.6, bf16[2,176,256]{2,1,0:T(8,128)(2,1)} %copy-done.13, ...), custom_call_target="tpu_custom_call" | custom-call | flops 268435456 | bytes 6291456 | tf_op jit(solution)/shard_map/pallas_call | solution.py:428
  (186 shorter events, 20.4 us)
Async XLA Ops:
  2.0 25.0 %collective-permute-start.2 = (bf16[2,512,512]{2,1,0:T(8,128)(2,1)S(1)}, bf16[2,512,512]{2,1,0:T(8,128)(2,1)S(1)}, u32[]{:S(2)}, u32[]{:S(2)}) collective-permute-start(bf16[2,512,512]{2,1,0:T(8,128)(2,1)S(1)} %constant_dynamic-slice_fusion), channel_id=1, source_target_pairs={{0,1},{1,0},{2,3},{3,2},{4,5},{5,4},{6,7},{7,6},{8,9},{9,8},{10,11... | collective-permute-start | bytes 3145736 | tf_op jit(solution)/shard_map/ppermute | solution.py:102
  4.2 7.1 %collective-permute-start.4 = (bf16[256,512]{1,0:T(8,128)(2,1)S(1)}, bf16[256,512]{1,0:T(8,128)(2,1)}, u32[]{:S(2)}, u32[]{:S(2)}) collective-permute-start(bf16[256,512]{1,0:T(8,128)(2,1)S(1)} %dynamic-slice_bitcast_fusion.refs_8_.refs_25_), channel_id=1, source_target_pairs={{0,8},{2,10},{4,0},{6,2},{8,16},{10,18},{12,4},{14,6},{16,24},{18,... | collective-permute-start | bytes 786440 | tf_op jit(solution)/shard_map/ppermute | solution.py:112
  5.5 28.9 %collective-permute-start.5 = (bf16[256,512]{1,0:T(8,128)(2,1)S(1)}, bf16[256,512]{1,0:T(8,128)(2,1)}, u32[]{:S(2)}, u32[]{:S(2)}) collective-permute-start(bf16[256,512]{1,0:T(8,128)(2,1)S(1)} %dynamic-slice_bitcast_fusion.refs_8_.refs_25_), channel_id=1, source_target_pairs={{0,4},{2,6},{4,12},{6,14},{8,0},{10,2},{12,20},{14,22},{16,8},{18,... | collective-permute-start | bytes 786440 | tf_op jit(solution)/shard_map/ppermute | solution.py:112
  11.2 25.3 %collective-permute-start.6 = (bf16[256,512]{1,0:T(8,128)(2,1)}, bf16[256,512]{1,0:T(8,128)(2,1)}, u32[]{:S(2)}, u32[]{:S(2)}) collective-permute-start(bf16[256,512]{1,0:T(8,128)(2,1)} %collective-permute-done.4.refs_9_.refs_26_), channel_id=1, source_target_pairs={{0,8},{2,10},{4,0},{6,2},{8,16},{10,18},{12,4},{14,6},{16,24},{18,... | collective-permute-start | bytes 786440 | tf_op jit(solution)/shard_map/ppermute | solution.py:112
  27.0 54.9 %collective-permute-start.3 = (bf16[2,512,512]{2,1,0:T(8,128)(2,1)S(1)}, bf16[2,512,512]{2,1,0:T(8,128)(2,1)S(1)}, u32[]{:S(2)}, u32[]{:S(2)}) collective-permute-start(bf16[2,512,512]{2,1,0:T(8,128)(2,1)S(1)} %collective-permute-done.2.near_ref.refs_6_), channel_id=1, source_target_pairs={{0,2},{2,0},{4,6},{6,4},{8,10},{10,8},{12,14},{14,12},{16,18},{18,... | collective-permute-start | bytes 3145736 | tf_op jit(solution)/shard_map/ppermute | solution.py:98
  28.3 54.1 %all-to-all-start = ((bf16[16,32,512]{2,1,0:T(8,128)(2,1)}), bf16[16,32,512]{2,1,0:T(8,128)(2,1)S(1)}, u32[]{:S(2)}, u32[]{:S(2)}) async-start(bf16[16,32,512]{2,1,0:T(8,128)(2,1)} %bitcast.22), calls=%async_computation | async-start | bytes 1048576 | tf_op jit(solution)/shard_map/all_to_all | solution.py:366
  34.4 16.3 %collective-permute-start.7 = (bf16[256,512]{1,0:T(8,128)(2,1)}, bf16[256,512]{1,0:T(8,128)(2,1)S(1)}, u32[]{:S(2)}, u32[]{:S(2)}) collective-permute-start(bf16[256,512]{1,0:T(8,128)(2,1)} %collective-permute-done.5.refs_10_.refs_27_), channel_id=1, source_target_pairs={{0,4},{2,6},{4,12},{6,14},{8,0},{10,2},{12,20},{14,22},{16,8},{18,... | collective-permute-start | bytes 786440 | tf_op jit(solution)/shard_map/ppermute | solution.py:112
  35.8 15.8 %collective-permute-start.12 = (bf16[256,512]{1,0:T(8,128)(2,1)S(1)}, bf16[256,512]{1,0:T(8,128)(2,1)S(1)}, u32[]{:S(2)}, u32[]{:S(2)}) collective-permute-start(bf16[256,512]{1,0:T(8,128)(2,1)S(1)} %dynamic-slice_bitcast_fusion.refs_8_.refs_25_), channel_id=1, source_target_pairs={{0,2},{2,0},{4,6},{6,4},{8,10},{10,8},{12,14},{14,12},{16,18},{18,... | collective-permute-start | bytes 786440 | tf_op jit(solution)/shard_map/ppermute | solution.py:98
  36.5 15.3 %collective-permute-start.8 = (bf16[256,512]{1,0:T(8,128)(2,1)}, bf16[256,512]{1,0:T(8,128)(2,1)S(1)}, u32[]{:S(2)}, u32[]{:S(2)}) collective-permute-start(bf16[256,512]{1,0:T(8,128)(2,1)} %collective-permute-done.6.refs_11_.refs_28_), channel_id=1, source_target_pairs={{0,8},{2,10},{4,0},{6,2},{8,16},{10,18},{12,4},{14,6},{16,24},{18,... | collective-permute-start | bytes 786440 | tf_op jit(solution)/shard_map/ppermute | solution.py:112
  50.7 9.8 %collective-permute-start.9 = (bf16[256,512]{1,0:T(8,128)(2,1)S(1)}, bf16[256,512]{1,0:T(8,128)(2,1)}, u32[]{:S(2)}, u32[]{:S(2)}) collective-permute-start(bf16[256,512]{1,0:T(8,128)(2,1)S(1)} %collective-permute-done.7.refs_12_.refs_29_), channel_id=1, source_target_pairs={{0,4},{2,6},{4,12},{6,14},{8,0},{10,2},{12,20},{14,22},{16,8},{18,... | collective-permute-start | bytes 786440 | tf_op jit(solution)/shard_map/ppermute | solution.py:112
  50.7 15.8 %collective-permute-start.13 = (bf16[256,512]{1,0:T(8,128)(2,1)}, bf16[256,512]{1,0:T(8,128)(2,1)}, u32[]{:S(2)}, u32[]{:S(2)}) collective-permute-start(bf16[256,512]{1,0:T(8,128)(2,1)} %collective-permute-done.4.refs_9_.refs_26_), channel_id=1, source_target_pairs={{0,2},{2,0},{4,6},{6,4},{8,10},{10,8},{12,14},{14,12},{16,18},{18,... | collective-permute-start | bytes 786440 | tf_op jit(solution)/shard_map/ppermute | solution.py:98
  51.7 26.0 %collective-permute-start.14 = (bf16[256,512]{1,0:T(8,128)(2,1)}, bf16[256,512]{1,0:T(8,128)(2,1)}, u32[]{:S(2)}, u32[]{:S(2)}) collective-permute-start(bf16[256,512]{1,0:T(8,128)(2,1)} %collective-permute-done.5.refs_10_.refs_27_), channel_id=1, source_target_pairs={{0,2},{2,0},{4,6},{6,4},{8,10},{10,8},{12,14},{14,12},{16,18},{18,... | collective-permute-start | bytes 786440 | tf_op jit(solution)/shard_map/ppermute | solution.py:98
  52.4 28.4 %collective-permute-start.15 = (bf16[256,512]{1,0:T(8,128)(2,1)}, bf16[256,512]{1,0:T(8,128)(2,1)}, u32[]{:S(2)}, u32[]{:S(2)}) collective-permute-start(bf16[256,512]{1,0:T(8,128)(2,1)} %collective-permute-done.6.refs_11_.refs_28_), channel_id=1, source_target_pairs={{0,2},{2,0},{4,6},{6,4},{8,10},{10,8},{12,14},{14,12},{16,18},{18,... | collective-permute-start | bytes 786440 | tf_op jit(solution)/shard_map/ppermute | solution.py:98
  60.5 20.4 %collective-permute-start.10 = (bf16[128,512]{1,0:T(8,128)(2,1)S(1)}, bf16[128,512]{1,0:T(8,128)(2,1)}, u32[]{:S(2)}, u32[]{:S(2)}) collective-permute-start(bf16[128,512]{1,0:T(8,128)(2,1)S(1)} %slice.44), channel_id=1, source_target_pairs={{0,8},{2,10},{4,0},{6,2},{8,16},{10,18},{12,4},{14,6},{16,24},{18,... | collective-permute-start | bytes 393224 | tf_op jit(solution)/shard_map/ppermute | solution.py:112
  66.5 15.4 %collective-permute-start.11 = (bf16[128,512]{1,0:T(8,128)(2,1)}, bf16[128,512]{1,0:T(8,128)(2,1)}, u32[]{:S(2)}, u32[]{:S(2)}) collective-permute-start(bf16[128,512]{1,0:T(8,128)(2,1)} %slice.45), channel_id=1, source_target_pairs={{0,4},{2,6},{4,12},{6,14},{8,0},{10,2},{12,20},{14,22},{16,8},{18,... | collective-permute-start | bytes 393224 | tf_op jit(solution)/shard_map/ppermute | solution.py:112
  77.7 14.0 %collective-permute-start.16 = (bf16[256,512]{1,0:T(8,128)(2,1)}, bf16[256,512]{1,0:T(8,128)(2,1)}, u32[]{:S(2)}, u32[]{:S(2)}) collective-permute-start(bf16[256,512]{1,0:T(8,128)(2,1)} %copy-done.11), channel_id=1, source_target_pairs={{0,2},{2,0},{4,6},{6,4},{8,10},{10,8},{12,14},{14,12},{16,18},{18,... | collective-permute-start | bytes 786440 | tf_op jit(solution)/shard_map/ppermute | solution.py:98
  80.8 11.0 %collective-permute-start.17 = (bf16[256,512]{1,0:T(8,128)(2,1)}, bf16[256,512]{1,0:T(8,128)(2,1)}, u32[]{:S(2)}, u32[]{:S(2)}) collective-permute-start(bf16[256,512]{1,0:T(8,128)(2,1)} %copy-done.7), channel_id=1, source_target_pairs={{0,2},{2,0},{4,6},{6,4},{8,10},{10,8},{12,14},{14,12},{16,18},{18,... | collective-permute-start | bytes 786440 | tf_op jit(solution)/shard_map/ppermute | solution.py:98
  80.8 10.9 %collective-permute-start.18 = (bf16[256,512]{1,0:T(8,128)(2,1)}, bf16[256,512]{1,0:T(8,128)(2,1)}, u32[]{:S(2)}, u32[]{:S(2)}) collective-permute-start(bf16[256,512]{1,0:T(8,128)(2,1)} %collective-permute-done.9.refs_14_.refs_31_), channel_id=1, source_target_pairs={{0,2},{2,0},{4,6},{6,4},{8,10},{10,8},{12,14},{14,12},{16,18},{18,... | collective-permute-start | bytes 786440 | tf_op jit(solution)/shard_map/ppermute | solution.py:98
  81.8 9.9 %collective-permute-start.19 = (bf16[128,512]{1,0:T(8,128)(2,1)}, bf16[128,512]{1,0:T(8,128)(2,1)S(1)}, u32[]{:S(2)}, u32[]{:S(2)}) collective-permute-start(bf16[128,512]{1,0:T(8,128)(2,1)} %collective-permute-done.10.refs_15_.refs_32_), channel_id=1, source_target_pairs={{0,2},{2,0},{4,6},{6,4},{8,10},{10,8},{12,14},{14,12},{16,18},{18,... | collective-permute-start | bytes 393224 | tf_op jit(solution)/shard_map/ppermute | solution.py:98
  81.9 9.8 %collective-permute-start.20 = (bf16[128,512]{1,0:T(8,128)(2,1)}, bf16[128,512]{1,0:T(8,128)(2,1)}, u32[]{:S(2)}, u32[]{:S(2)}) collective-permute-start(bf16[128,512]{1,0:T(8,128)(2,1)} %collective-permute-done.11.refs_16_.refs_33_), channel_id=1, source_target_pairs={{0,2},{2,0},{4,6},{6,4},{8,10},{10,8},{12,14},{14,12},{16,18},{18,... | collective-permute-start | bytes 393224 | tf_op jit(solution)/shard_map/ppermute | solution.py:98
  108.6 6.7 %collective-permute-start.22 = (bf16[2,8,32,256]{3,2,1,0:T(8,128)(2,1)S(1)}, bf16[2,8,32,256]{3,2,1,0:T(8,128)(2,1)S(1)}, u32[]{:S(2)}, u32[]{:S(2)}) collective-permute-start(bf16[2,8,32,256]{3,2,1,0:T(8,128)(2,1)S(1)} %pad_maximum_fusion.refs_7_), channel_id=1, source_target_pairs={{0,8},{2,10},{4,0},{6,2},{8,16},{10,18},{12,4},{14,6},{16,24},{18,... | collective-permute-start | bytes 786440 | tf_op jit(solution)/shard_map/ppermute | solution.py:112
  110.1 6.7 %collective-permute-start.23 = (bf16[2,8,32,256]{3,2,1,0:T(8,128)(2,1)S(1)}, bf16[2,8,32,256]{3,2,1,0:T(8,128)(2,1)S(1)}, u32[]{:S(2)}, u32[]{:S(2)}) collective-permute-start(bf16[2,8,32,256]{3,2,1,0:T(8,128)(2,1)S(1)} %pad_maximum_fusion.refs_7_), channel_id=1, source_target_pairs={{0,4},{2,6},{4,12},{6,14},{8,0},{10,2},{12,20},{14,22},{16,8},{18,... | collective-permute-start | bytes 786440 | tf_op jit(solution)/shard_map/ppermute | solution.py:112
  115.3 5.8 %collective-permute-start.24 = (bf16[2,8,32,256]{3,2,1,0:T(8,128)(2,1)S(1)}, bf16[2,8,32,256]{3,2,1,0:T(8,128)(2,1)S(1)}, u32[]{:S(2)}, u32[]{:S(2)}) collective-permute-start(bf16[2,8,32,256]{3,2,1,0:T(8,128)(2,1)S(1)} %collective-permute-done.22.refs_8_), channel_id=1, source_target_pairs={{0,8},{2,10},{4,0},{6,2},{8,16},{10,18},{12,4},{14,6},{16,24},{18,... | collective-permute-start | bytes 786440 | tf_op jit(solution)/shard_map/ppermute | solution.py:112
  116.8 5.8 %collective-permute-start.25 = (bf16[2,8,32,256]{3,2,1,0:T(8,128)(2,1)S(1)}, bf16[2,8,32,256]{3,2,1,0:T(8,128)(2,1)S(1)}, u32[]{:S(2)}, u32[]{:S(2)}) collective-permute-start(bf16[2,8,32,256]{3,2,1,0:T(8,128)(2,1)S(1)} %collective-permute-done.23.refs_9_), channel_id=1, source_target_pairs={{0,4},{2,6},{4,12},{6,14},{8,0},{10,2},{12,20},{14,22},{16,8},{18,... | collective-permute-start | bytes 786440 | tf_op jit(solution)/shard_map/ppermute | solution.py:112
  121.1 5.5 %collective-permute-start.26 = (bf16[2,8,32,256]{3,2,1,0:T(8,128)(2,1)S(1)}, bf16[2,8,32,256]{3,2,1,0:T(8,128)(2,1)S(1)}, u32[]{:S(2)}, u32[]{:S(2)}) collective-permute-start(bf16[2,8,32,256]{3,2,1,0:T(8,128)(2,1)S(1)} %collective-permute-done.24.refs_10_), channel_id=1, source_target_pairs={{0,8},{2,10},{4,0},{6,2},{8,16},{10,18},{12,4},{14,6},{16,24},{18,... | collective-permute-start | bytes 786440 | tf_op jit(solution)/shard_map/ppermute | solution.py:112
  122.6 7.9 %collective-permute-start.27 = (bf16[2,8,32,256]{3,2,1,0:T(8,128)(2,1)S(1)}, bf16[2,8,32,256]{3,2,1,0:T(8,128)(2,1)S(1)}, u32[]{:S(2)}, u32[]{:S(2)}) collective-permute-start(bf16[2,8,32,256]{3,2,1,0:T(8,128)(2,1)S(1)} %collective-permute-done.25.refs_11_), channel_id=1, source_target_pairs={{0,4},{2,6},{4,12},{6,14},{8,0},{10,2},{12,20},{14,22},{16,8},{18,... | collective-permute-start | bytes 786440 | tf_op jit(solution)/shard_map/ppermute | solution.py:112
  122.6 9.6 %collective-permute-start.30 = (bf16[2,8,32,256]{3,2,1,0:T(8,128)(2,1)S(1)}, bf16[2,8,32,256]{3,2,1,0:T(8,128)(2,1)S(1)}, u32[]{:S(2)}, u32[]{:S(2)}) collective-permute-start(bf16[2,8,32,256]{3,2,1,0:T(8,128)(2,1)S(1)} %pad_maximum_fusion.refs_7_), channel_id=1, source_target_pairs={{0,2},{2,0},{4,6},{6,4},{8,10},{10,8},{12,14},{14,12},{16,18},{18,... | collective-permute-start | bytes 786440 | tf_op jit(solution)/shard_map/ppermute | solution.py:98
  126.1 6.6 %collective-permute-start.31 = (bf16[2,8,32,256]{3,2,1,0:T(8,128)(2,1)S(1)}, bf16[2,8,32,256]{3,2,1,0:T(8,128)(2,1)S(1)}, u32[]{:S(2)}, u32[]{:S(2)}) collective-permute-start(bf16[2,8,32,256]{3,2,1,0:T(8,128)(2,1)S(1)} %collective-permute-done.22.refs_8_), channel_id=1, source_target_pairs={{0,2},{2,0},{4,6},{6,4},{8,10},{10,8},{12,14},{14,12},{16,18},{18,... | collective-permute-start | bytes 786440 | tf_op jit(solution)/shard_map/ppermute | solution.py:98
  126.1 7.6 %collective-permute-start.32 = (bf16[2,8,32,256]{3,2,1,0:T(8,128)(2,1)S(1)}, bf16[2,8,32,256]{3,2,1,0:T(8,128)(2,1)S(1)}, u32[]{:S(2)}, u32[]{:S(2)}) collective-permute-start(bf16[2,8,32,256]{3,2,1,0:T(8,128)(2,1)S(1)} %collective-permute-done.23.refs_9_), channel_id=1, source_target_pairs={{0,2},{2,0},{4,6},{6,4},{8,10},{10,8},{12,14},{14,12},{16,18},{18,... | collective-permute-start | bytes 786440 | tf_op jit(solution)/shard_map/ppermute | solution.py:98
  126.6 7.7 %collective-permute-start.33 = (bf16[2,8,32,256]{3,2,1,0:T(8,128)(2,1)S(1)}, bf16[2,8,32,256]{3,2,1,0:T(8,128)(2,1)S(1)}, u32[]{:S(2)}, u32[]{:S(2)}) collective-permute-start(bf16[2,8,32,256]{3,2,1,0:T(8,128)(2,1)S(1)} %collective-permute-done.24.refs_10_), channel_id=1, source_target_pairs={{0,2},{2,0},{4,6},{6,4},{8,10},{10,8},{12,14},{14,12},{16,18},{18,... | collective-permute-start | bytes 786440 | tf_op jit(solution)/shard_map/ppermute | solution.py:98
  130.4 8.2 %collective-permute-start.34 = (bf16[2,8,32,256]{3,2,1,0:T(8,128)(2,1)S(1)}, bf16[2,8,32,256]{3,2,1,0:T(8,128)(2,1)S(1)}, u32[]{:S(2)}, u32[]{:S(2)}) collective-permute-start(bf16[2,8,32,256]{3,2,1,0:T(8,128)(2,1)S(1)} %collective-permute-done.25.refs_11_), channel_id=1, source_target_pairs={{0,2},{2,0},{4,6},{6,4},{8,10},{10,8},{12,14},{14,12},{16,18},{18,... | collective-permute-start | bytes 786440 | tf_op jit(solution)/shard_map/ppermute | solution.py:98
  132.7 5.4 %collective-permute-start.29 = (bf16[1,8,32,256]{3,2,1,0:T(8,128)(2,1)S(1)}, bf16[1,8,32,256]{3,2,1,0:T(8,128)(2,1)S(1)}, u32[]{:S(2)}, u32[]{:S(2)}) collective-permute-start(bf16[1,8,32,256]{3,2,1,0:T(8,128)(2,1)S(1)} %slice.47), channel_id=1, source_target_pairs={{0,4},{2,6},{4,12},{6,14},{8,0},{10,2},{12,20},{14,22},{16,8},{18,... | collective-permute-start | bytes 393224 | tf_op jit(solution)/shard_map/ppermute | solution.py:112
  133.7 5.9 %collective-permute-start.35 = (bf16[2,8,32,256]{3,2,1,0:T(8,128)(2,1)S(1)}, bf16[2,8,32,256]{3,2,1,0:T(8,128)(2,1)S(1)}, u32[]{:S(2)}, u32[]{:S(2)}) collective-permute-start(bf16[2,8,32,256]{3,2,1,0:T(8,128)(2,1)S(1)} %collective-permute-done.26.refs_12_), channel_id=1, source_target_pairs={{0,2},{2,0},{4,6},{6,4},{8,10},{10,8},{12,14},{14,12},{16,18},{18,... | collective-permute-start | bytes 786440 | tf_op jit(solution)/shard_map/ppermute | solution.py:98
  160.1 8.0 %collective-permute-start.40 = (bf16[2,176,256]{2,1,0:T(8,128)(2,1)S(1)}, bf16[2,176,256]{2,1,0:T(8,128)(2,1)S(1)}, u32[]{:S(2)}, u32[]{:S(2)}) collective-permute-start(bf16[2,176,256]{2,1,0:T(8,128)(2,1)S(1)} %pad_maximum_fusion.1.refs_3_), channel_id=1, source_target_pairs={{0,8},{2,10},{4,0},{6,2},{8,16},{10,18},{12,4},{14,6},{16,24},{18,... | collective-permute-start | bytes 540680 | tf_op jit(solution)/shard_map/ppermute | solution.py:112
  160.7 7.5 %collective-permute-start.41 = (bf16[2,176,256]{2,1,0:T(8,128)(2,1)S(1)}, bf16[2,176,256]{2,1,0:T(8,128)(2,1)S(1)}, u32[]{:S(2)}, u32[]{:S(2)}) collective-permute-start(bf16[2,176,256]{2,1,0:T(8,128)(2,1)S(1)} %pad_maximum_fusion.1.refs_3_), channel_id=1, source_target_pairs={{0,4},{2,6},{4,12},{6,14},{8,0},{10,2},{12,20},{14,22},{16,8},{18,... | collective-permute-start | bytes 540680 | tf_op jit(solution)/shard_map/ppermute | solution.py:112
  161.6 23.1 %collective-permute-start = (bf16[512,512]{1,0:T(8,128)(2,1)S(1)}, bf16[512,512]{1,0:T(8,128)(2,1)S(1)}, u32[]{:S(2)}, u32[]{:S(2)}) collective-permute-start(bf16[512,512]{1,0:T(8,128)(2,1)S(1)} %bitcast.23), channel_id=1, source_target_pairs={{0,2},{2,4},{4,6},{6,8},{8,10},{10,12},{12,14},{14,16},{16,18},{18... | collective-permute-start | bytes 1572872 | tf_op jit(solution)/shard_map/ppermute | solution.py:398
  166.2 22.6 %collective-permute-start.1 = (bf16[512,512]{1,0:T(8,128)(2,1)S(1)}, bf16[512,512]{1,0:T(8,128)(2,1)S(1)}, u32[]{:S(2)}, u32[]{:S(2)}) collective-permute-start(bf16[512,512]{1,0:T(8,128)(2,1)S(1)} %bitcast.24), channel_id=1, source_target_pairs={{2,0},{4,2},{6,4},{8,6},{10,8},{12,10},{14,12},{16,14},{18,16},{20... | collective-permute-start | bytes 1572872 | tf_op jit(solution)/shard_map/ppermute | solution.py:399
  168.2 5.9 %collective-permute-start.42 = (bf16[2,176,256]{2,1,0:T(8,128)(2,1)S(1)}, bf16[2,176,256]{2,1,0:T(8,128)(2,1)S(1)}, u32[]{:S(2)}, u32[]{:S(2)}) collective-permute-start(bf16[2,176,256]{2,1,0:T(8,128)(2,1)S(1)} %collective-permute-done.40.refs_4_), channel_id=1, source_target_pairs={{0,8},{2,10},{4,0},{6,2},{8,16},{10,18},{12,4},{14,6},{16,24},{18,... | collective-permute-start | bytes 540680 | tf_op jit(solution)/shard_map/ppermute | solution.py:112
  168.2 13.5 %collective-permute-start.43 = (bf16[2,176,256]{2,1,0:T(8,128)(2,1)S(1)}, bf16[2,176,256]{2,1,0:T(8,128)(2,1)S(1)}, u32[]{:S(2)}, u32[]{:S(2)}) collective-permute-start(bf16[2,176,256]{2,1,0:T(8,128)(2,1)S(1)} %collective-permute-done.41.refs_5_), channel_id=1, source_target_pairs={{0,4},{2,6},{4,12},{6,14},{8,0},{10,2},{12,20},{14,22},{16,8},{18,... | collective-permute-start | bytes 540680 | tf_op jit(solution)/shard_map/ppermute | solution.py:112
  174.0 10.8 %collective-permute-start.44 = (bf16[2,176,256]{2,1,0:T(8,128)(2,1)S(1)}, bf16[2,176,256]{2,1,0:T(8,128)(2,1)S(1)}, u32[]{:S(2)}, u32[]{:S(2)}) collective-permute-start(bf16[2,176,256]{2,1,0:T(8,128)(2,1)S(1)} %collective-permute-done.42.refs_6_), channel_id=1, source_target_pairs={{0,8},{2,10},{4,0},{6,2},{8,16},{10,18},{12,4},{14,6},{16,24},{18,... | collective-permute-start | bytes 540680 | tf_op jit(solution)/shard_map/ppermute | solution.py:112
  181.8 6.4 %collective-permute-start.45 = (bf16[2,176,256]{2,1,0:T(8,128)(2,1)S(1)}, bf16[2,176,256]{2,1,0:T(8,128)(2,1)S(1)}, u32[]{:S(2)}, u32[]{:S(2)}) collective-permute-start(bf16[2,176,256]{2,1,0:T(8,128)(2,1)S(1)} %collective-permute-done.43.refs_7_), channel_id=1, source_target_pairs={{0,4},{2,6},{4,12},{6,14},{8,0},{10,2},{12,20},{14,22},{16,8},{18,... | collective-permute-start | bytes 540680 | tf_op jit(solution)/shard_map/ppermute | solution.py:112
  183.7 5.4 %collective-permute-start.48 = (bf16[2,176,256]{2,1,0:T(8,128)(2,1)S(1)}, bf16[2,176,256]{2,1,0:T(8,128)(2,1)S(1)}, u32[]{:S(2)}, u32[]{:S(2)}) collective-permute-start(bf16[2,176,256]{2,1,0:T(8,128)(2,1)S(1)} %pad_maximum_fusion.1.refs_3_), channel_id=1, source_target_pairs={{0,2},{2,0},{4,6},{6,4},{8,10},{10,8},{12,14},{14,12},{16,18},{18,... | collective-permute-start | bytes 540680 | tf_op jit(solution)/shard_map/ppermute | solution.py:98
  184.8 6.7 %collective-permute-start.49 = (bf16[2,176,256]{2,1,0:T(8,128)(2,1)S(1)}, bf16[2,176,256]{2,1,0:T(8,128)(2,1)S(1)}, u32[]{:S(2)}, u32[]{:S(2)}) collective-permute-start(bf16[2,176,256]{2,1,0:T(8,128)(2,1)S(1)} %collective-permute-done.40.refs_4_), channel_id=1, source_target_pairs={{0,2},{2,0},{4,6},{6,4},{8,10},{10,8},{12,14},{14,12},{16,18},{18,... | collective-permute-start | bytes 540680 | tf_op jit(solution)/shard_map/ppermute | solution.py:98
  184.8 7.0 %collective-permute-start.50 = (bf16[2,176,256]{2,1,0:T(8,128)(2,1)S(1)}, bf16[2,176,256]{2,1,0:T(8,128)(2,1)S(1)}, u32[]{:S(2)}, u32[]{:S(2)}) collective-permute-start(bf16[2,176,256]{2,1,0:T(8,128)(2,1)S(1)} %collective-permute-done.41.refs_5_), channel_id=1, source_target_pairs={{0,2},{2,0},{4,6},{6,4},{8,10},{10,8},{12,14},{14,12},{16,18},{18,... | collective-permute-start | bytes 540680 | tf_op jit(solution)/shard_map/ppermute | solution.py:98
  189.1 6.0 %collective-permute-start.47 = (bf16[1,176,256]{2,1,0:T(8,128)(2,1)S(1)}, bf16[1,176,256]{2,1,0:T(8,128)(2,1)S(1)}, u32[]{:S(2)}, u32[]{:S(2)}) collective-permute-start(bf16[1,176,256]{2,1,0:T(8,128)(2,1)S(1)} %slice.49), channel_id=1, source_target_pairs={{0,4},{2,6},{4,12},{6,14},{8,0},{10,2},{12,20},{14,22},{16,8},{18,... | collective-permute-start | bytes 270344 | tf_op jit(solution)/shard_map/ppermute | solution.py:112
  191.5 7.5 %collective-permute-start.52 = (bf16[2,176,256]{2,1,0:T(8,128)(2,1)S(1)}, bf16[2,176,256]{2,1,0:T(8,128)(2,1)S(1)}, u32[]{:S(2)}, u32[]{:S(2)}) collective-permute-start(bf16[2,176,256]{2,1,0:T(8,128)(2,1)S(1)} %collective-permute-done.43.refs_7_), channel_id=1, source_target_pairs={{0,2},{2,0},{4,6},{6,4},{8,10},{10,8},{12,14},{14,12},{16,18},{18,... | collective-permute-start | bytes 540680 | tf_op jit(solution)/shard_map/ppermute | solution.py:98
  191.8 7.2 %collective-permute-start.53 = (bf16[2,176,256]{2,1,0:T(8,128)(2,1)S(1)}, bf16[2,176,256]{2,1,0:T(8,128)(2,1)S(1)}, u32[]{:S(2)}, u32[]{:S(2)}) collective-permute-start(bf16[2,176,256]{2,1,0:T(8,128)(2,1)S(1)} %collective-permute-done.44.refs_8_), channel_id=1, source_target_pairs={{0,2},{2,0},{4,6},{6,4},{8,10},{10,8},{12,14},{14,12},{16,18},{18,... | collective-permute-start | bytes 540680 | tf_op jit(solution)/shard_map/ppermute | solution.py:98
  192.0 7.0 %collective-permute-start.54 = (bf16[2,176,256]{2,1,0:T(8,128)(2,1)S(1)}, bf16[2,176,256]{2,1,0:T(8,128)(2,1)S(1)}, u32[]{:S(2)}, u32[]{:S(2)}) collective-permute-start(bf16[2,176,256]{2,1,0:T(8,128)(2,1)S(1)} %collective-permute-done.45.refs_9_), channel_id=1, source_target_pairs={{0,2},{2,0},{4,6},{6,4},{8,10},{10,8},{12,14},{14,12},{16,18},{18,... | collective-permute-start | bytes 540680 | tf_op jit(solution)/shard_map/ppermute | solution.py:98
  (57 other events, 649.0 us)

commit v2 on v1

v2 whole, which is shorter than its diff:
```python
import functools
import math

import jax
import jax.numpy as jnp
import numpy as np
from jax import lax
from jax.experimental import pallas as pl
from jax.experimental.pallas import tpu as pltpu
from jax.sharding import PartitionSpec as P


ITERS = 2
GATHER_BYTES = 8 * 1024 * 1024
VMEM = pltpu.MemorySpace.VMEM
SMEM = pltpu.MemorySpace.SMEM


def broadcast(value, axis, source):
    kept = jnp.where(lax.axis_index(axis) == source, value, 0).astype(value.dtype)
    return lax.psum(kept, axis)


def padded_2(cells, sides, width):
    for axis, dim in sides:
        count = lax.axis_size(axis)
        ends = count - 1
        head = lax.slice_in_dim(cells, 0, width, axis=dim)
        tail = lax.slice_in_dim(cells, cells.shape[dim] - width, cells.shape[dim], axis=dim)
        cells = jnp.concatenate(
            [
                lax.ppermute(tail, axis, [(i, (i + 1) % count) for i in range(ends)]),
                cells,
                lax.ppermute(head, axis, [((i + 1) % count, i) for i in range(ends)]),
            ],
            axis=dim,
        )
    return cells


def reduce_form(wavefunction, left_ops, right_ops, shift_map, sector_sizes, step_sizes, integrals):
    highest = lax.Precision.HIGHEST
    local_sec = wavefunction.shape[0]
    width = wavefunction.shape[1]
    sectors = sector_sizes.shape[0]
    count = lax.axis_size("ops") * left_ops.shape[0]
    first = lax.axis_index("sec") * local_sec
    local_sizes = lax.dynamic_slice_in_dim(sector_sizes, first, local_sec, 0)
    column = jnp.arange(width, dtype=jnp.int32)
    row_ok = (column[None, :] < local_sizes[:, None]).astype(jnp.float32)
    mask = row_ok[:, :, None] * row_ok[:, None, :]
    psi = wavefunction.astype(jnp.float32) * mask
    sources = first + jnp.arange(local_sec, dtype=jnp.int32)
    target = (sources[None, :] + shift_map[:, None]) % sectors
    routing = (jnp.arange(sectors, dtype=jnp.int32)[:, None, None] == target[None]).astype(
        jnp.float32
    )
    for step in range(ITERS):
        psi_low = psi.astype(jnp.bfloat16)
        inner = jnp.einsum(
            "kmn,snp->ksmp", left_ops, psi_low, preferred_element_type=jnp.float32
        ).astype(jnp.bfloat16)
        terms = jnp.einsum("ksmp,kqp->ksmq", inner, right_ops, preferred_element_type=jnp.float32)
        contrib = jnp.einsum("tks,ksmq->tmq", routing, terms, precision=highest)
        partial_rows = lax.psum_scatter(contrib, "ops", scatter_dimension=1, tiled=True)
        own_rows = lax.psum_scatter(
            partial_rows.astype(jnp.bfloat16), "sec", scatter_dimension=0, tiled=True
        ).astype(jnp.float32)
        hpsi = lax.all_gather(own_rows.astype(jnp.bfloat16), "ops", axis=1, tiled=True).astype(
            own_rows.dtype
        )
        factor = step_sizes[step].astype(jnp.float32) / (8.0 * math.sqrt(count))
        psi = mask * (psi - factor * hpsi)
        total = lax.psum(jnp.sum(psi * psi), "sec")
        psi = psi / jnp.sqrt(total / (sectors * width * width) + 1e-06)
    basis = broadcast(psi[0].astype(jnp.bfloat16), "sec", 0)
    col_count = width // lax.axis_size("sec")
    basis_cols = lax.dynamic_slice_in_dim(basis, lax.axis_index("sec") * col_count, col_count, 1)
    half = jnp.einsum("mp,kmn->kpn", basis, left_ops, preferred_element_type=jnp.float32).astype(
        jnp.bfloat16
    )
    rotated = (
        jnp.einsum("kpn,nq->kpq", half, basis_cols, preferred_element_type=jnp.float32) / width
    )
    padded = padded_2(rotated.astype(jnp.bfloat16), (("ops", 0),), 1).astype(rotated.dtype)
    mixed = (
        integrals[:, 0, None, None] * padded[:-2]
        + integrals[:, 1, None, None] * padded[1:-1]
        + integrals[:, 2, None, None] * padded[2:]
    )
    return (psi, mixed.astype(jnp.bfloat16))


def ring_order(chips):
    return list(range(0, chips, 2)) + list(range(chips - 1, 0, -2))


def swap_core(x, n):
    return lax.ppermute(x, "ops", [(o, o ^ 1) for o in range(n)])


def swap_sec(x):
    return lax.ppermute(x, "sec", [(0, 1), (1, 0)])


def along_ring(x, n, by):
    order = ring_order(n // 2)
    place = {chip: i for i, chip in enumerate(order)}
    perm = []
    for o in range(n):
        chip = order[(place[o // 2] + by) % len(order)]
        perm.append((o, 2 * chip + o % 2))
    return lax.ppermute(x, "ops", perm)


def ring_slots(n):
    slots = [(0, 0)]
    for step in range(1, n // 4):
        slots += [(-step, 0), (step, 0)]
    slots.append((-(n // 4), 0))
    return slots + [(d, 1) for d, _ in slots]


def ring_table(n):
    order = ring_order(n // 2)
    place = {chip: i for i, chip in enumerate(order)}
    rows = []
    for o in range(n):
        at = place[o // 2]
        rows.append([2 * order[(at + d) % len(order)] + ((o % 2) ^ c) for d, c in ring_slots(n)])
    return np.array(rows, np.int32)


def ring_gather(x, n):
    last = n // 4
    up = down = x
    own = [x]
    for step in range(1, last + 1):
        up = along_ring(up, n, 1)
        own.append(up)
        if step < last:
            down = along_ring(down, n, -1)
            own.append(down)
    other = []
    for piece in own:
        other.append(swap_core(piece, n))
    return own + other


def copy_in(pairs, sems):
    copies = []
    for i, (src, dst) in enumerate(pairs):
        copy = pltpu.make_async_copy(src, dst, sems.at[i])
        copy.start()
        copies.append(copy)
    return copies


def wait_all(copies):
    for copy in copies:
        copy.wait()


def cut_psi(psi, size):
    row = lax.broadcasted_iota(jnp.int32, (psi.shape[0], 1), 0)
    col = lax.broadcasted_iota(jnp.int32, (1, psi.shape[1]), 1)
    rows = jnp.where(row < size, 1.0, 0.0).astype(psi.dtype)
    cols = jnp.where(col < size, 1.0, 0.0).astype(psi.dtype)
    return psi * rows * cols


def first_stage(left_ref, psi, inner_shape):
    product = jnp.dot(left_ref[...], psi, preferred_element_type=jnp.float32).astype(jnp.bfloat16)
    return product.reshape(inner_shape[0], inner_shape[2], psi.shape[1])


def own_kernel(scal_ref, sizes_ref, left_ref, wave_ref, out_ref, waves, sems):
    local = wave_ref.shape[0]
    copies = copy_in([(wave_ref.at[i], waves.at[i]) for i in range(local)], sems)
    for i in range(local):
        copies[i].wait()
        psi = cut_psi(waves[i], sizes_ref[scal_ref[2] * local + i])
        out_ref[:, i] = first_stage(left_ref, psi, out_ref.shape)


def second_stage(terms, right, cols):
    total = None
    for i, inner in enumerate(terms):
        sectors, _, _ = inner.shape
        shift = jnp.max(right[i, cols:, :128].astype(jnp.float32)).astype(jnp.int32)
        rhs = right[i, :cols]
        lhs = jnp.concatenate([inner[lax.rem(t - shift + sectors, sectors)] for t in range(sectors)], axis=0)
        product = lax.dot_general(
            lhs, rhs, (((1,), (1,)), ((), ())), preferred_element_type=jnp.float32
        )
        total = product if total is None else total + product
    return total


def step_rows(psi, acc, sizes_ref, scal_ref, factor, sector):
    rows, cols = psi.shape
    size = sizes_ref[sector]
    row = lax.broadcasted_iota(jnp.int32, psi.shape, 0) + scal_ref[0] * rows
    col = lax.broadcasted_iota(jnp.int32, psi.shape, 1) + scal_ref[2] * cols
    moved = psi - factor * acc[sector * rows : (sector + 1) * rows]
    return jnp.where((row < size) & (col < size), moved, 0.0)


def early_kernel(early, late, *refs):
    scal_ref, table_ref, sizes_ref, left_ref, own_ref, near_ref, far_ref = refs[:7]
    pieces = refs[7 : 7 + len(early)]
    acc_ref, rest_ref, right, inner, waves, wsems, rsems, isem = refs[7 + len(early) :]
    core, sec = scal_ref[1], scal_ref[2]
    cols = acc_ref.shape[1]
    local = own_ref.shape[1]
    half = local // 2
    sources = [(near_ref.at[i], waves.at[i]) for i in range(half)]
    sources += [(far_ref.at[i], waves.at[half + i]) for i in range(half)]
    wave_copies = copy_in(sources, wsems)
    copies = copy_in([(own_ref, inner.at[:, pl.ds(sec * local, local)])], isem)
    copies += copy_in([(piece, right.at[i]) for i, piece in enumerate(pieces)], rsems)
    foreign = (1 - sec) * local
    swapped = core * half

    for slot in range(local):
        wave_copies[slot].wait()
        sector = foreign + lax.rem(swapped + slot, local)
        psi = cut_psi(waves[slot], sizes_ref[sector])
        inner[:, sector] = first_stage(left_ref, psi, inner.shape)

    wait_all(copies)
    acc_ref[...] = second_stage([inner.at[table_ref[i]] for i in early], right, cols)
    for at, i in enumerate(late):
        rest_ref[at] = inner[table_ref[i]]


def late_kernel(*refs):
    scal_ref, sizes_ref, factor_ref, acc_ref, rest_ref, own_ref, near_ref, far_ref = refs[:8]
    pieces = refs[8:10]
    out_ref, send_ref, right, start, rsems, ssems = refs[10:]
    o, core, sec = scal_ref[0], scal_ref[1], scal_ref[2]
    local = own_ref.shape[0]
    _, rows, cols = out_ref.shape
    here = (slice(None), pl.ds(o * rows, rows), pl.ds(sec * cols, cols))
    foreign, half = (1 - sec) * local, local // 2
    copies = copy_in([(piece, right.at[c]) for c, piece in enumerate(pieces)], rsems)
    copies += copy_in(
        [
            (own_ref.at[here], start.at[pl.ds(sec * local, local)]),
            (near_ref.at[here], start.at[pl.ds(foreign + core * half, half)]),
            (far_ref.at[here], start.at[pl.ds(foreign + (1 - core) * half, half)]),
        ],
        ssems,
    )
    wait_all(copies)
    acc = acc_ref[...] + second_stage([rest_ref.at[c] for c in range(2)], right, cols)
    for s in range(out_ref.shape[0]):
        moved = step_rows(start[s].astype(jnp.float32), acc, sizes_ref, scal_ref, factor_ref[0], s)
        out_ref[s] = moved
        send_ref[s] = moved.astype(jnp.bfloat16)


def split_3(value):
    parts = []
    for _ in range(3):
        low = value.astype(jnp.bfloat16)
        parts.append(low)
        value = value - low.astype(jnp.float32)
    return parts


def iter2_kernel(slots, *refs):
    n_slots = len(slots)
    scal_ref, table_ref, sizes_ref, factor_ref, left_ref, prev_ref = refs[:6]
    psi_pieces = refs[6 : 6 + n_slots]
    right_pieces = refs[6 + n_slots : 6 + 2 * n_slots]
    keep_ref, send_ref, psi, inner, right, low, psems, rsems = refs[6 + 2 * n_slots :]
    sec = scal_ref[2]
    sectors, rows, cols = prev_ref.shape
    local = sectors // 2
    pairs = []
    for i, piece in enumerate(psi_pieces):
        at = pl.ds(table_ref[i] * rows, rows)
        pairs += [(piece.at[h], psi.at[sec if h == 0 else 1 - sec, :, at]) for h in range(2)]
    psi_copies = copy_in(pairs, psems)
    right_copies = copy_in([(piece, right.at[i]) for i, piece in enumerate(right_pieces)], rsems)
    wait_all(psi_copies)

    @pl.loop(0, sectors, unroll=2)
    def _(s):
        for h in range(2):
            inner[:, s, :, h * cols : (h + 1) * cols] = first_stage(left_ref, psi[h, s], inner.shape)

    wait_all(right_copies)
    acc = second_stage([inner.at[table_ref[i]] for i in range(n_slots)], right, cols)
    before = jnp.zeros((rows, cols), jnp.float32)
    after = jnp.zeros((rows, cols), jnp.float32)
    for s in range(sectors):
        old = prev_ref[s]
        moved = step_rows(old, acc, sizes_ref, scal_ref, factor_ref[0], s)
        low[s] = moved.astype(jnp.bfloat16)
        before += old * old
        after += moved * moved
    for i in range(local):
        keep_ref[i * rows : (i + 1) * rows] = low[sec * local + i]
        send_ref[i * rows : (i + 1) * rows] = low[(1 - sec) * local + i]
    keep_ref[local * rows : (local + 1) * rows] = low[0]
    send_ref[local * rows : (local + 1) * rows] = low[0]
    tail = keep_ref.shape[0] - (local + 1) * rows
    line = lax.broadcasted_iota(jnp.int32, (tail, cols), 0)
    stats = jnp.zeros((tail, cols), jnp.float32)
    for i, total in enumerate((before, after)):
        parts = split_3(jnp.full((tail, cols), jnp.sum(total), jnp.float32))
        for p, low_part in enumerate(parts):
            stats = jnp.where(line == 3 * i + p, low_part.astype(jnp.float32), stats)
    keep_ref[(local + 1) * rows :] = stats.astype(jnp.bfloat16)
    send_ref[(local + 1) * rows :] = stats.astype(jnp.bfloat16)


def final_kernel(slots, values, *refs):
    n_slots = len(slots)
    scal_ref, table_ref, mixer_ref = refs[:3]
    pieces = refs[3 : 3 + n_slots]
    wave_ref, mixed_ref, basis = refs[3 + n_slots :]
    sec = scal_ref[2]
    local, width, _ = wave_ref.shape
    cols = width // 2
    rows = width // n_slots
    tail = pieces[0].shape[1] - (local + 1) * rows
    stats = jnp.zeros((tail, cols), jnp.float32)
    views = []
    for i, piece in enumerate(pieces):
        at = pl.ds(pl.multiple_of(table_ref[i] * rows, rows), rows)
        for h in range(2):
            side = sec if h == 0 else 1 - sec
            across = pl.ds(pl.multiple_of(side * cols, cols), cols)
            view = piece.at[h]
            views.append((view, at, across))
            stats += view[(local + 1) * rows :].astype(jnp.float32)
            basis[at, across] = view[local * rows : (local + 1) * rows]
    line = lax.broadcasted_iota(jnp.int32, (tail, cols), 0)
    first = jnp.sum(jnp.where(line < 3, stats, 0.0), axis=0, keepdims=True)[:, :1]
    second = jnp.sum(jnp.where((line >= 3) & (line < 6), stats, 0.0), axis=0, keepdims=True)[:, :1]
    norm_1 = jnp.sqrt(first / values + 1e-06)
    norm_2 = jnp.sqrt(second / (norm_1 * norm_1) / values + 1e-06)
    scale = 1.0 / (norm_1 * norm_2)
    for s in range(local):
        for view, at, across in views:
            wave_ref[s, at, across] = view[s * rows : (s + 1) * rows].astype(jnp.float32) * scale
    across = pl.ds(pl.multiple_of(sec * cols, cols), cols)
    right = jnp.dot(mixer_ref[...], basis[:, across], preferred_element_type=jnp.float32)
    rotated = lax.dot_general(
        basis[...], right.astype(jnp.bfloat16), (((0,), (0,)), ((), ())), preferred_element_type=jnp.float32
    )
    mixed_ref[...] = (rotated * (scale * scale / width)).astype(jnp.bfloat16)


def kernel_call(body, out, ins, scratch, mib, flops, moved):
    spaces = {"s": SMEM, "v": VMEM, "a": pl.ANY, "h": pltpu.MemorySpace.HBM}
    multiple = isinstance(out, (tuple, list))
    out_spec = pl.BlockSpec(memory_space=VMEM)
    return pl.pallas_call(
        body,
        out_shape=out,
        in_specs=[pl.BlockSpec(memory_space=spaces[c]) for c in ins],
        out_specs=(out_spec,) * len(out) if multiple else out_spec,
        scratch_shapes=scratch,
        compiler_params=pltpu.CompilerParams(vmem_limit_bytes=mib * 1024 * 1024),
        cost_estimate=pl.CostEstimate(flops=flops, bytes_accessed=moved, transcendentals=0),
    )


def gather_form(wavefunction, left_ops, right_ops, shift_map, sector_sizes, step_sizes, integrals):
    f32, bf16 = jnp.float32, jnp.bfloat16
    n = lax.axis_size("ops")
    local, width, _ = wavefunction.shape
    sectors = sector_sizes.shape[0]
    rows, cols = width // n, width // 2
    o, sec = lax.axis_index("ops"), lax.axis_index("sec")
    core = lax.rem(o, 2)
    slots = ring_slots(n)
    n_slots = len(slots)
    late = [n_slots // 2 - 1, n_slots - 1]
    early = [i for i in range(n_slots) if i not in late]
    scal = jnp.stack([o, core, sec]).astype(jnp.int32)
    table = lax.dynamic_slice_in_dim(jnp.asarray(ring_table(n)), o, 1, 0)[0]
    factors = step_sizes.astype(f32) / (8.0 * math.sqrt(n))
    shape = jax.ShapeDtypeStruct
    dma = pltpu.SemaphoreType.DMA
    psi_bytes = 2 * sectors * width**2
    tall = cols + 16

    right_cols = jnp.concatenate(
        [
            lax.dynamic_slice_in_dim(right_ops[0], sec * cols, cols, 0),
            jnp.broadcast_to(shift_map.astype(bf16)[:, None], (16, width)),
        ]
    )
    right_pieces = ring_gather(right_cols, n)
    left_rows = lax.all_to_all(left_ops[0], "ops", 0, 0, tiled=True)
    part = lax.dynamic_slice_in_dim(wavefunction, core * (local // 2), local // 2, 0)
    near = swap_sec(part)
    far = swap_core(near, n)

    inner = kernel_call(
        own_kernel, shape((n, local, rows, width), bf16), "ssva",
        [pltpu.VMEM((local, width, width), bf16), dma((local,))],
        10, sectors * width**3, psi_bytes,
    )(scal, sector_sizes, left_rows, wavefunction)
    acc, rest = kernel_call(
        functools.partial(early_kernel, early, late),
        (shape((sectors * rows, cols), f32), shape((2, sectors, rows, width), bf16)),
        "sssvaaa" + "a" * len(early),
        [
            pltpu.VMEM((len(early), tall, width), bf16),
            pltpu.VMEM((n, sectors, rows, width), bf16),
            pltpu.VMEM((local, width, width), bf16),
            dma((local,)),
            dma((len(early),)),
            dma((1,)),
        ],
        16, 2 * sectors * width**2 * cols, 2 * psi_bytes,
    )(scal, table, sector_sizes, left_rows, inner, near, far, *[right_pieces[i] for i in early])
    psi_1, low_1 = kernel_call(
        late_kernel,
        (shape((sectors, rows, cols), f32), shape((sectors, rows, cols), bf16)),
        "sssvvaaaaa",
        [pltpu.VMEM((2, tall, width), bf16), pltpu.VMEM((sectors, rows, cols), bf16), dma((2,)), dma((3,))],
        8, sectors * width * cols * cols, psi_bytes // 4,
    )(scal, sector_sizes, factors[:1], acc, rest, wavefunction, near, far, *[right_pieces[i] for i in late])

    low_2 = swap_sec(low_1)
    below = lax.ppermute(left_ops[0], "ops", [(i, i + 1) for i in range(n - 1)])
    above = lax.ppermute(left_ops[0], "ops", [(i + 1, i) for i in range(n - 1)])
    psi_pieces = ring_gather(jnp.stack([low_1, low_2]), n)
    mixer = (
        integrals[0, 0] * below.astype(f32)
        + integrals[0, 1] * left_ops[0].astype(f32)
        + integrals[0, 2] * above.astype(f32)
    ).astype(bf16)

    message = (local + 1) * rows + 16
    keep, send = kernel_call(
        functools.partial(iter2_kernel, slots), (shape((message, cols), bf16),) * 2,
        "ssssvv" + "a" * (2 * n_slots),
        [
            pltpu.VMEM((2, sectors, width, cols), bf16),
            pltpu.VMEM((n, sectors, rows, width), bf16),
            pltpu.VMEM((n, tall, width), bf16),
            pltpu.VMEM((sectors, rows, cols), bf16),
            dma((2 * n_slots,)),
            dma((n_slots,)),
        ],
        18, 3 * sectors * width**3, 2 * psi_bytes,
    )(scal, table, sector_sizes, factors[1:2], left_rows, psi_1, *psi_pieces, *right_pieces)

    recv = swap_sec(send)
    last_pieces = ring_gather(jnp.stack([keep, recv]), n)
    wave, mixed = kernel_call(
        functools.partial(final_kernel, slots, float(sectors * width * width)),
        (shape((local, width, width), f32), shape((width, cols), bf16)),
        "ssv" + "v" * n_slots, [pltpu.VMEM((width, width), bf16)],
        16, 2 * width**3, 6 * local * width**2,
    )(scal, table, mixer, *last_pieces)
    return (wave, mixed[None])


def shards(wavefunction, left_ops, right_ops, *rest):
    n, halves = lax.axis_size("ops"), lax.axis_size("sec")
    width = right_ops.shape[1]
    gathered = 2 * n * right_ops.size // halves
    fits = gathered <= GATHER_BYTES and halves == 2 and right_ops.shape[0] == 1
    aligned = n % 4 == 0 and width % (16 * n) == 0 and width % 256 == 0 and wavefunction.shape[0] % 2 == 0
    form = gather_form if fits and aligned else reduce_form
    return form(wavefunction, left_ops, right_ops, *rest)


def solution(mesh):
    placed = (
        P("sec", None, None),
        P("ops", None, None),
        P("ops", None, None),
        P("ops"),
        P(),
        P(),
        P("ops", None),
    )
    return jax.shard_map(
        shards,
        mesh=mesh,
        in_specs=placed,
        out_specs=(P("sec", None, None), P("ops", None, "sec")),
        check_vma=False,
    )
```

time: 206 us -> 154 us (0.75)
  Pallas kernels: 38.5 us -> 22.9 us
  waiting for transfers between devices: 75.9 us -> 65.4 us
  blocking collectives: 9.69 us -> 0 us
  starting transfers between devices: 61.9 us -> 55.4 us
  local copies, waits for them, and re-layouts: 11.6 us -> 5.94 us
  other arithmetic: 6.07 us -> 2.39 us
    pallas_call x4 -> x5, Pallas kernels: 38.5 us -> 22.9 us  [the longest x1 7.26 us: gather_form(): kernel_call(functools.partial(iter2_kernel, slots), (shape((message, cols...]
    unnamed x1 -> x0, blocking collectives: 9.69 us -> none
    ppermute x3, waiting for transfers between devices: 21 us -> 15.2 us  [swap_sec(): return lax.ppermute(x, 'sec', [(0, 1), (1, 0)])]
    ppermute x24 -> x21, waiting for transfers between devices: 53.9 us -> 48.3 us  [along_ring(): return lax.ppermute(x, 'ops', perm)]
    ppermute x28 -> x25, starting transfers between devices: 26 us -> 21 us  [swap_core(): return lax.ppermute(x, 'ops', [(o, o ^ 1) for o in range(n)])]
    unnamed x97 -> x20, local copies, waits for them, and re-layouts: 6.2 us -> 1.47 us
    ppermute x24 -> x21, starting transfers between devices: 18.6 us -> 19.6 us  [along_ring(): return lax.ppermute(x, 'ops', perm)]
  transfers between devices with their start and end apart: 58 -> 52, of which waited for: 15 -> 17; matrix products, arithmetic and copies ran while one was open for 5% -> 3% of each run, Pallas kernels for 4% -> 6%
where the time goes in v2:
time: 154 us
  waiting for transfers between devices  65.4 us (42%)
  starting transfers between devices  55.4 us (36%)
  Pallas kernels  22.9 us (15%)
  local copies, waits for them, and re-layouts  5.94 us (4%)
  other arithmetic  2.39 us (2%)
  between operations  1.61 us (1%)
    ppermute x21, waiting for transfers between devices, along_ring(): return lax.ppermute(x, 'ops', perm)  48.3 us
    ppermute x25, starting transfers between devices, swap_core(): return lax.ppermute(x, 'ops', [(o, o ^ 1) for o in range(n)])  21 us
    ppermute x21, starting transfers between devices, along_ring(): return lax.ppermute(x, 'ops', perm)  19.6 us
    ppermute x3, waiting for transfers between devices, swap_sec(): return lax.ppermute(x, 'sec', [(0, 1), (1, 0)])  15.2 us
    pallas_call x1, Pallas kernels, gather_form(): kernel_call(functools.partial(iter2_kernel, slots), (shape((message, cols...  7.26 us
    all_to_all x1, starting transfers between devices, gather_form(): left_rows = lax.all_to_all(left_ops[0], 'ops', 0, 0, tiled=True)  6.89 us
    pallas_call x1, Pallas kernels, gather_form(): kernel_call(functools.partial(early_kernel, early, late), (shape((sectors...  6.74 us
    pallas_call x1, Pallas kernels, gather_form(): kernel_call(functools.partial(final_kernel, slots, float(sectors * width...  3.65 us
  transfers between devices with their start and end apart: 52, of which 17 were waited for; matrix products, arithmetic and copies ran while one was open for 3% of the time, Pallas kernels for 6%

profile of v2, /device:TPU:1, one launch (start us, length us, event | category | flops | bytes accessed | tf_op | source)
XLA Modules:
  0.0 153.5 jit_solution(4154683037804697159)
XLA Ops:
  0.7 2.4 %constant_dynamic-slice_fusion = bf16[2,512,512]{2,1,0:T(8,128)(2,1)} fusion(bf16[4,512,512]{2,1,0:T(8,128)(2,1)} %refs_5_.1, s32[]{:T(128)S(6)} %select_n.10), kind=kLoop, calls=%fused_computation.4 | loop fusion | bytes 2097156 | tf_op jit(solution)/shard_map/dynamic_slice | solution.py:401
  3.1 2.1 %collective-permute-start.2 = (bf16[2,512,512]{2,1,0:T(8,128)(2,1)}, bf16[2,512,512]{2,1,0:T(8,128)(2,1)}, u32[]{:S(2)}, u32[]{:S(2)}) collective-permute-start(bf16[2,512,512]{2,1,0:T(8,128)(2,1)} %constant_dynamic-slice_fusion), channel_id=1, source_target_pairs={{0,1},{1,0},{2,3},{3,2},{4,5},{5,4},{6,7},{7,6},{8,9},{9,8},{10,11... | collective-permute-start | bytes 3145736 | tf_op jit(solution)/shard_map/ppermute | solution.py:103
  5.9 1.3 collective-permute-start.4
  7.4 5.9 %collective-permute-done.4.refs_8_.refs_23_ = bf16[272,512]{1,0:T(8,128)(2,1)} collective-permute-done((bf16[272,512]{1,0:T(8,128)(2,1)S(1)}, bf16[272,512]{1,0:T(8,128)(2,1)}, u32[]{:S(2)}, u32[]{:S(2)}) %collective-permute-start.4) | collective-permute-done | bytes 278560 | tf_op jit(solution)/shard_map/ppermute | solution.py:113
  13.3 1.3 collective-permute-start.6
  14.6 6.9 %all-to-all-start = ((bf16[16,32,512]{2,1,0:T(8,128)(2,1)}), bf16[16,32,512]{2,1,0:T(8,128)(2,1)S(1)}, u32[]{:S(2)}, u32[]{:S(2)}) async-start(bf16[16,32,512]{2,1,0:T(8,128)(2,1)} %bitcast.25), calls=%async_computation | async-start | bytes 1048576 | tf_op jit(solution)/shard_map/all_to_all | solution.py:400
  21.5 6.8 %collective-permute-done.2.refs_5_.refs_6_ = bf16[2,512,512]{2,1,0:T(8,128)(2,1)} collective-permute-done((bf16[2,512,512]{2,1,0:T(8,128)(2,1)}, bf16[2,512,512]{2,1,0:T(8,128)(2,1)}, u32[]{:S(2)}, u32[]{:S(2)}) %collective-permute-start.2) | collective-permute-done | bytes 1048608 | tf_op jit(solution)/shard_map/ppermute | solution.py:103
  28.3 1.3 collective-permute-start.3
  29.6 1.4 collective-permute-start.7
  31.0 0.8 collective-permute-start.11
  32.5 0.7 copy-done.2
  33.6 5.7 %collective-permute-done.7.refs_11_.refs_26_ = bf16[272,512]{1,0:T(8,128)(2,1)} collective-permute-done((bf16[272,512]{1,0:T(8,128)(2,1)}, bf16[272,512]{1,0:T(8,128)(2,1)}, u32[]{:S(2)}, u32[]{:S(2)}) %collective-permute-start.7) | collective-permute-done | bytes 278560 | tf_op jit(solution)/shard_map/ppermute | solution.py:113
  39.3 1.1 collective-permute-start.13
  40.4 0.7 copy-done.4
  41.1 0.7 collective-permute-start.9
  41.9 2.1 %collective-permute-start.17 = (bf16[272,512]{1,0:T(8,128)(2,1)}, bf16[272,512]{1,0:T(8,128)(2,1)}, u32[]{:S(2)}, u32[]{:S(2)}) collective-permute-start(bf16[272,512]{1,0:T(8,128)(2,1)} %collective-permute-done.8.refs_12_.refs_27_), channel_id=1, source_target_pairs={{0,8},{2,10},{4,0},{6,2},{8,16},{10,18},{12,4},{14,6},{16,24},{18,... | collective-permute-start | bytes 835592 | tf_op jit(solution)/shard_map/ppermute | solution.py:113
  44.9 6.4 %collective-permute-done.9.refs_13_.refs_28_ = bf16[272,512]{1,0:T(8,128)(2,1)} collective-permute-done((bf16[272,512]{1,0:T(8,128)(2,1)}, bf16[272,512]{1,0:T(8,128)(2,1)}, u32[]{:S(2)}, u32[]{:S(2)}) %collective-permute-start.9) | collective-permute-done | bytes 278560 | tf_op jit(solution)/shard_map/ppermute | solution.py:113
  53.2 2.6 %shard_map.95.refs_4_ = bf16[16,4,32,512]{3,2,1,0:T(8,128)(2,1)S(1)} custom-call(s32[3]{0:T(128)S(1)} %pad_add_fusion.scal_ref.refs_0_, s32[8]{0:T(128)S(1)} %copy-done.6, bf16[512,512]{1,0:T(8,128)(2,1)S(1)} %bitcast.20, bf16[4,512,512]{2,1,0:T(8,128)(2,1)S(1)} %copy-done.1), custom_call_target="tpu_custom_call" | custom-call | flops 1073741824 | bytes 4194304 | tf_op jit(solution)/shard_map/pallas_call | solution.py:405
  55.8 6.7 %shard_map.96 = (f32[256,256]{1,0:T(8,128)S(1)}, bf16[2,8,32,512]{3,2,1,0:T(8,128)(2,1)S(1)}) custom-call(s32[3]{0:T(128)S(1)} %pad_add_fusion.scal_ref.refs_0_, s32[16]{0:T(128)S(1)} %fusion.refs_1_, s32[8]{0:T(128)S(1)} %copy-done.6, bf16[512,512]{1,0:T(8,128)(2,1)S(1)} %bitcast.21, bf16[16,4,32,512]{3,2,1,0:T(8,128)(2,1)S(1)} %shard_map.95.refs_4_, ...), custom_call_target="tpu_custom_call" | custom-call | flops 1073741824 | bytes 8388608 | tf_op jit(solution)/shard_map/pallas_call | solution.py:410
  62.6 2.6 %shard_map.97 = (f32[8,32,256]{2,1,0:T(8,128)S(1)}, bf16[8,32,256]{2,1,0:T(8,128)(2,1)S(1)}) custom-call(s32[3]{0:T(128)S(1)} %pad_add_fusion.scal_ref.refs_0_, s32[8]{0:T(128)S(1)} %copy-done.6, f32[1]{0:T(128)} %get-tuple-element.18.refs_2_, f32[256,256]{1,0:T(8,128)S(1)} %get-tuple-element.10.refs_3_, ...), custom_call_target="tpu_custom_call" | custom-call | flops 268435456 | bytes 1048576 | tf_op jit(solution)/shard_map/pallas_call | solution.py:424
  65.5 4.8 %collective-permute-done.19 = bf16[8,32,256]{2,1,0:T(8,128)(2,1)S(1)} collective-permute-done((bf16[8,32,256]{2,1,0:T(8,128)(2,1)S(1)}, bf16[8,32,256]{2,1,0:T(8,128)(2,1)S(1)}, u32[]{:S(2)}, u32[]{:S(2)}) %collective-permute-start.19) | collective-permute-done | bytes 131104 | tf_op jit(solution)/shard_map/ppermute | solution.py:103
  70.4 1.5 collective-permute-start.20
  71.9 5.5 %collective-permute-done.20.refs_7_ = bf16[2,8,32,256]{3,2,1,0:T(8,128)(2,1)S(1)} collective-permute-done((bf16[2,8,32,256]{3,2,1,0:T(8,128)(2,1)S(1)}, bf16[2,8,32,256]{3,2,1,0:T(8,128)(2,1)S(1)}, u32[]{:S(2)}, u32[]{:S(2)}) %collective-permute-start.20) | collective-permute-done | bytes 262176 | tf_op jit(solution)/shard_map/ppermute | solution.py:113
  77.4 1.5 collective-permute-start.22
  78.9 4.7 %collective-permute-done.22.refs_9_ = bf16[2,8,32,256]{3,2,1,0:T(8,128)(2,1)S(1)} collective-permute-done((bf16[2,8,32,256]{3,2,1,0:T(8,128)(2,1)S(1)}, bf16[2,8,32,256]{3,2,1,0:T(8,128)(2,1)S(1)}, u32[]{:S(2)}, u32[]{:S(2)}) %collective-permute-start.22) | collective-permute-done | bytes 262176 | tf_op jit(solution)/shard_map/ppermute | solution.py:113
  83.6 1.5 collective-permute-start.24
  85.0 2.9 %collective-permute-start.27 = (bf16[2,8,32,256]{3,2,1,0:T(8,128)(2,1)S(1)}, bf16[2,8,32,256]{3,2,1,0:T(8,128)(2,1)S(1)}, u32[]{:S(2)}, u32[]{:S(2)}) collective-permute-start(bf16[2,8,32,256]{3,2,1,0:T(8,128)(2,1)S(1)} %pad_maximum_fusion.refs_6_), channel_id=1, source_target_pairs={{0,2},{2,0},{4,6},{6,4},{8,10},{10,8},{12,14},{14,12},{16,18},{18,... | collective-permute-start | bytes 786440 | tf_op jit(solution)/shard_map/ppermute | solution.py:99
  88.8 1.5 collective-permute-start.26
  90.3 4.6 %collective-permute-start.30 = (bf16[2,8,32,256]{3,2,1,0:T(8,128)(2,1)S(1)}, bf16[2,8,32,256]{3,2,1,0:T(8,128)(2,1)S(1)}, u32[]{:S(2)}, u32[]{:S(2)}) collective-permute-start(bf16[2,8,32,256]{3,2,1,0:T(8,128)(2,1)S(1)} %collective-permute-done.22.refs_9_), channel_id=1, source_target_pairs={{0,2},{2,0},{4,6},{6,4},{8,10},{10,8},{12,14},{14,12},{16,18},{18,... | collective-permute-start | bytes 786440 | tf_op jit(solution)/shard_map/ppermute | solution.py:99
  95.4 0.9 collective-permute-done.25.refs_12_
  96.3 0.9 collective-permute-start.33
  97.1 2.4 %collective-permute-start.34 = (bf16[2,8,32,256]{3,2,1,0:T(8,128)(2,1)S(1)}, bf16[2,8,32,256]{3,2,1,0:T(8,128)(2,1)S(1)}, u32[]{:S(2)}, u32[]{:S(2)}) collective-permute-start(bf16[2,8,32,256]{3,2,1,0:T(8,128)(2,1)S(1)} %collective-permute-done.26.refs_13_), channel_id=1, source_target_pairs={{0,2},{2,0},{4,6},{6,4},{8,10},{10,8},{12,14},{14,12},{16,18},{18,... | collective-permute-start | bytes 786440 | tf_op jit(solution)/shard_map/ppermute | solution.py:99
  99.5 1.1 collective-permute-done.34.refs_21_
  100.7 7.3 %shard_map.98 = (bf16[176,256]{1,0:T(8,128)(2,1)S(1)}, bf16[176,256]{1,0:T(8,128)(2,1)S(1)}) custom-call(s32[3]{0:T(128)S(1)} %pad_add_fusion.scal_ref.refs_0_, s32[16]{0:T(128)S(1)} %fusion.refs_1_, s32[8]{0:T(128)S(1)} %copy-done.6, f32[1]{0:T(128)} %get-tuple-element.19.refs_3_, bf16[512,512]{1,0:T(8,128)(2,1)S(1)} %bitcast.22, ...), custom_call_target="tpu_custom_call" | custom-call | flops 3221225472 | bytes 8388608 | tf_op jit(solution)/shard_map/pallas_call | solution.py:443
  108.2 3.6 %collective-permute-done.35 = bf16[176,256]{1,0:T(8,128)(2,1)S(1)} collective-permute-done((bf16[176,256]{1,0:T(8,128)(2,1)S(1)}, bf16[176,256]{1,0:T(8,128)(2,1)S(1)}, u32[]{:S(2)}, u32[]{:S(2)}) %collective-permute-start.35) | collective-permute-done | bytes 90144 | tf_op jit(solution)/shard_map/ppermute | solution.py:103
  111.8 1.5 collective-permute-start.36
  113.3 3.3 %collective-permute-start = (bf16[512,512]{1,0:T(8,128)(2,1)S(1)}, bf16[512,512]{1,0:T(8,128)(2,1)S(1)}, u32[]{:S(2)}, u32[]{:S(2)}) collective-permute-start(bf16[512,512]{1,0:T(8,128)(2,1)S(1)} %bitcast.26), channel_id=1, source_target_pairs={{0,2},{2,4},{4,6},{6,8},{8,10},{10,12},{12,14},{14,16},{16,18},{18... | collective-permute-start | bytes 1572872 | tf_op jit(solution)/shard_map/ppermute | solution.py:433
  116.7 1.9 %collective-permute-start.1 = (bf16[512,512]{1,0:T(8,128)(2,1)S(1)}, bf16[512,512]{1,0:T(8,128)(2,1)S(1)}, u32[]{:S(2)}, u32[]{:S(2)}) collective-permute-start(bf16[512,512]{1,0:T(8,128)(2,1)S(1)} %bitcast.27), channel_id=1, source_target_pairs={{2,0},{4,2},{6,4},{8,6},{10,8},{12,10},{14,12},{16,14},{18,16},{20... | collective-permute-start | bytes 1572872 | tf_op jit(solution)/shard_map/ppermute | solution.py:434
  118.6 1.5 collective-permute-start.37
  120.1 12.1 %collective-permute-done.37.refs_5_ = bf16[2,176,256]{2,1,0:T(8,128)(2,1)S(1)} collective-permute-done((bf16[2,176,256]{2,1,0:T(8,128)(2,1)S(1)}, bf16[2,176,256]{2,1,0:T(8,128)(2,1)S(1)}, u32[]{:S(2)}, u32[]{:S(2)}) %collective-permute-start.37) | collective-permute-done | bytes 180256 | tf_op jit(solution)/shard_map/ppermute | solution.py:113
  132.2 1.9 %collective-permute-start.39 = (bf16[2,176,256]{2,1,0:T(8,128)(2,1)S(1)}, bf16[2,176,256]{2,1,0:T(8,128)(2,1)S(1)}, u32[]{:S(2)}, u32[]{:S(2)}) collective-permute-start(bf16[2,176,256]{2,1,0:T(8,128)(2,1)S(1)} %collective-permute-done.37.refs_5_), channel_id=1, source_target_pairs={{0,4},{2,6},{4,12},{6,14},{8,0},{10,2},{12,20},{14,22},{16,8},{18,... | collective-permute-start | bytes 540680 | tf_op jit(solution)/shard_map/ppermute | solution.py:113
  134.7 4.0 %collective-permute-done.39.refs_7_ = bf16[2,176,256]{2,1,0:T(8,128)(2,1)S(1)} collective-permute-done((bf16[2,176,256]{2,1,0:T(8,128)(2,1)S(1)}, bf16[2,176,256]{2,1,0:T(8,128)(2,1)S(1)}, u32[]{:S(2)}, u32[]{:S(2)}) %collective-permute-start.39) | collective-permute-done | bytes 180256 | tf_op jit(solution)/shard_map/ppermute | solution.py:113
  138.8 1.6 %collective-permute-start.41 = (bf16[2,176,256]{2,1,0:T(8,128)(2,1)S(1)}, bf16[2,176,256]{2,1,0:T(8,128)(2,1)S(1)}, u32[]{:S(2)}, u32[]{:S(2)}) collective-permute-start(bf16[2,176,256]{2,1,0:T(8,128)(2,1)S(1)} %collective-permute-done.39.refs_7_), channel_id=1, source_target_pairs={{0,4},{2,6},{4,12},{6,14},{8,0},{10,2},{12,20},{14,22},{16,8},{18,... | collective-permute-start | bytes 540680 | tf_op jit(solution)/shard_map/ppermute | solution.py:113
  142.4 2.0 %collective-permute-done.41.refs_9_ = bf16[2,176,256]{2,1,0:T(8,128)(2,1)S(1)} collective-permute-done((bf16[2,176,256]{2,1,0:T(8,128)(2,1)S(1)}, bf16[2,176,256]{2,1,0:T(8,128)(2,1)S(1)}, u32[]{:S(2)}, u32[]{:S(2)}) %collective-permute-start.41) | collective-permute-done | bytes 180256 | tf_op jit(solution)/shard_map/ppermute | solution.py:113
  144.4 1.3 collective-permute-start.49
  146.2 1.4 collective-permute-start.50
  147.6 2.3 %add_convert_fusion.refs_2_ = bf16[512,512]{1,0:T(8,128)(2,1)S(1)} fusion(bf16[512,512]{1,0:T(8,128)(2,1)S(1)} %collective-permute-done.1, bf16[512,512]{1,0:T(8,128)(2,1)S(1)} %collective-permute-done, f32[]{:T(128)} %bitcast.7, f32[]{:T(128)} %bitcast.6, f32[]{:T(128)} %bitcast.4, bf16[1,512,512]{2,1,0:T(8,128)(2,1)S(1)} %copy-done.7), kind=kLoop, calls=%fused_computation | loop fusion | flops 2359296 | bytes 2097164 | tf_op jit(solution)/shard_map/convert_element_type | solution.py:440
  149.9 3.7 %shard_map.99 = (f32[4,512,512]{2,1,0:T(8,128)}, bf16[512,256]{1,0:T(8,128)(2,1)}) custom-call(s32[3]{0:T(128)S(1)} %pad_add_fusion.scal_ref.refs_0_, s32[16]{0:T(128)S(1)} %fusion.refs_1_, bf16[512,512]{1,0:T(8,128)(2,1)S(1)} %add_convert_fusion.refs_2_, bf16[2,176,256]{2,1,0:T(8,128)(2,1)S(1)} %pad_maximum_fusion.1.refs_3_, ...), custom_call_target="tpu_custom_call" | custom-call | flops 268435456 | bytes 6291456 | tf_op jit(solution)/shard_map/pallas_call | solution.py:459
  (92 shorter events, 9.3 us)
Async XLA Ops:
  3.1 25.2 %collective-permute-start.2 = (bf16[2,512,512]{2,1,0:T(8,128)(2,1)}, bf16[2,512,512]{2,1,0:T(8,128)(2,1)}, u32[]{:S(2)}, u32[]{:S(2)}) collective-permute-start(bf16[2,512,512]{2,1,0:T(8,128)(2,1)} %constant_dynamic-slice_fusion), channel_id=1, source_target_pairs={{0,1},{1,0},{2,3},{3,2},{4,5},{5,4},{6,7},{7,6},{8,9},{9,8},{10,11... | collective-permute-start | bytes 3145736 | tf_op jit(solution)/shard_map/ppermute | solution.py:103
  5.9 7.4 %collective-permute-start.4 = (bf16[272,512]{1,0:T(8,128)(2,1)S(1)}, bf16[272,512]{1,0:T(8,128)(2,1)}, u32[]{:S(2)}, u32[]{:S(2)}) collective-permute-start(bf16[272,512]{1,0:T(8,128)(2,1)S(1)} %concatenate.3.refs_7_.refs_22_), channel_id=1, source_target_pairs={{0,8},{2,10},{4,0},{6,2},{8,16},{10,18},{12,4},{14,6},{16,24},{18,... | collective-permute-start | bytes 835592 | tf_op jit(solution)/shard_map/ppermute | solution.py:113
  7.2 22.4 %collective-permute-start.5 = (bf16[272,512]{1,0:T(8,128)(2,1)S(1)}, bf16[272,512]{1,0:T(8,128)(2,1)}, u32[]{:S(2)}, u32[]{:S(2)}) collective-permute-start(bf16[272,512]{1,0:T(8,128)(2,1)S(1)} %concatenate.3.refs_7_.refs_22_), channel_id=1, source_target_pairs={{0,4},{2,6},{4,12},{6,14},{8,0},{10,2},{12,20},{14,22},{16,8},{18,... | collective-permute-start | bytes 835592 | tf_op jit(solution)/shard_map/ppermute | solution.py:113
  13.3 18.5 %collective-permute-start.6 = (bf16[272,512]{1,0:T(8,128)(2,1)}, bf16[272,512]{1,0:T(8,128)(2,1)}, u32[]{:S(2)}, u32[]{:S(2)}) collective-permute-start(bf16[272,512]{1,0:T(8,128)(2,1)} %collective-permute-done.4.refs_8_.refs_23_), channel_id=1, source_target_pairs={{0,8},{2,10},{4,0},{6,2},{8,16},{10,18},{12,4},{14,6},{16,24},{18,... | collective-permute-start | bytes 835592 | tf_op jit(solution)/shard_map/ppermute | solution.py:113
  14.6 38.5 %all-to-all-start = ((bf16[16,32,512]{2,1,0:T(8,128)(2,1)}), bf16[16,32,512]{2,1,0:T(8,128)(2,1)S(1)}, u32[]{:S(2)}, u32[]{:S(2)}) async-start(bf16[16,32,512]{2,1,0:T(8,128)(2,1)} %bitcast.25), calls=%async_computation | async-start | bytes 1048576 | tf_op jit(solution)/shard_map/all_to_all | solution.py:400
  28.3 27.4 %collective-permute-start.3 = (bf16[2,512,512]{2,1,0:T(8,128)(2,1)}, bf16[2,512,512]{2,1,0:T(8,128)(2,1)}, u32[]{:S(2)}, u32[]{:S(2)}) collective-permute-start(bf16[2,512,512]{2,1,0:T(8,128)(2,1)} %collective-permute-done.2.refs_5_.refs_6_), channel_id=1, source_target_pairs={{0,2},{2,0},{4,6},{6,4},{8,10},{10,8},{12,14},{14,12},{16,18},{18,... | collective-permute-start | bytes 3145736 | tf_op jit(solution)/shard_map/ppermute | solution.py:99
  29.6 9.7 %collective-permute-start.7 = (bf16[272,512]{1,0:T(8,128)(2,1)}, bf16[272,512]{1,0:T(8,128)(2,1)}, u32[]{:S(2)}, u32[]{:S(2)}) collective-permute-start(bf16[272,512]{1,0:T(8,128)(2,1)} %collective-permute-done.5.refs_9_.refs_24_), channel_id=1, source_target_pairs={{0,4},{2,6},{4,12},{6,14},{8,0},{10,2},{12,20},{14,22},{16,8},{18,... | collective-permute-start | bytes 835592 | tf_op jit(solution)/shard_map/ppermute | solution.py:113
  31.0 9.4 %collective-permute-start.11 = (bf16[272,512]{1,0:T(8,128)(2,1)}, bf16[272,512]{1,0:T(8,128)(2,1)S(1)}, u32[]{:S(2)}, u32[]{:S(2)}) collective-permute-start(bf16[272,512]{1,0:T(8,128)(2,1)} %collective-permute-done.4.refs_8_.refs_23_), channel_id=1, source_target_pairs={{0,2},{2,0},{4,6},{6,4},{8,10},{10,8},{12,14},{14,12},{16,18},{18,... | collective-permute-start | bytes 835592 | tf_op jit(solution)/shard_map/ppermute | solution.py:99
  31.8 10.0 %collective-permute-start.8 = (bf16[272,512]{1,0:T(8,128)(2,1)}, bf16[272,512]{1,0:T(8,128)(2,1)}, u32[]{:S(2)}, u32[]{:S(2)}) collective-permute-start(bf16[272,512]{1,0:T(8,128)(2,1)} %collective-permute-done.6.refs_10_.refs_25_), channel_id=1, source_target_pairs={{0,8},{2,10},{4,0},{6,2},{8,16},{10,18},{12,4},{14,6},{16,24},{18,... | collective-permute-start | bytes 835592 | tf_op jit(solution)/shard_map/ppermute | solution.py:113
  33.2 11.4 %collective-permute-start.12 = (bf16[272,512]{1,0:T(8,128)(2,1)}, bf16[272,512]{1,0:T(8,128)(2,1)}, u32[]{:S(2)}, u32[]{:S(2)}) collective-permute-start(bf16[272,512]{1,0:T(8,128)(2,1)} %collective-permute-done.5.refs_9_.refs_24_), channel_id=1, source_target_pairs={{0,2},{2,0},{4,6},{6,4},{8,10},{10,8},{12,14},{14,12},{16,18},{18,... | collective-permute-start | bytes 835592 | tf_op jit(solution)/shard_map/ppermute | solution.py:99
  39.3 12.5 %collective-permute-start.13 = (bf16[272,512]{1,0:T(8,128)(2,1)}, bf16[272,512]{1,0:T(8,128)(2,1)}, u32[]{:S(2)}, u32[]{:S(2)}) collective-permute-start(bf16[272,512]{1,0:T(8,128)(2,1)} %collective-permute-done.6.refs_10_.refs_25_), channel_id=1, source_target_pairs={{0,2},{2,0},{4,6},{6,4},{8,10},{10,8},{12,14},{14,12},{16,18},{18,... | collective-permute-start | bytes 835592 | tf_op jit(solution)/shard_map/ppermute | solution.py:99
  41.1 10.1 %collective-permute-start.9 = (bf16[272,512]{1,0:T(8,128)(2,1)}, bf16[272,512]{1,0:T(8,128)(2,1)}, u32[]{:S(2)}, u32[]{:S(2)}) collective-permute-start(bf16[272,512]{1,0:T(8,128)(2,1)} %collective-permute-done.7.refs_11_.refs_26_), channel_id=1, source_target_pairs={{0,4},{2,6},{4,12},{6,14},{8,0},{10,2},{12,20},{14,22},{16,8},{18,... | collective-permute-start | bytes 835592 | tf_op jit(solution)/shard_map/ppermute | solution.py:113
  41.9 10.7 %collective-permute-start.17 = (bf16[272,512]{1,0:T(8,128)(2,1)}, bf16[272,512]{1,0:T(8,128)(2,1)}, u32[]{:S(2)}, u32[]{:S(2)}) collective-permute-start(bf16[272,512]{1,0:T(8,128)(2,1)} %collective-permute-done.8.refs_12_.refs_27_), channel_id=1, source_target_pairs={{0,8},{2,10},{4,0},{6,2},{8,16},{10,18},{12,4},{14,6},{16,24},{18,... | collective-permute-start | bytes 835592 | tf_op jit(solution)/shard_map/ppermute | solution.py:113
  44.6 11.1 %collective-permute-start.14 = (bf16[272,512]{1,0:T(8,128)(2,1)}, bf16[272,512]{1,0:T(8,128)(2,1)}, u32[]{:S(2)}, u32[]{:S(2)}) collective-permute-start(bf16[272,512]{1,0:T(8,128)(2,1)} %collective-permute-done.7.refs_11_.refs_26_), channel_id=1, source_target_pairs={{0,2},{2,0},{4,6},{6,4},{8,10},{10,8},{12,14},{14,12},{16,18},{18,... | collective-permute-start | bytes 835592 | tf_op jit(solution)/shard_map/ppermute | solution.py:99
  51.3 4.5 %collective-permute-start.15 = (bf16[272,512]{1,0:T(8,128)(2,1)}, bf16[272,512]{1,0:T(8,128)(2,1)}, u32[]{:S(2)}, u32[]{:S(2)}) collective-permute-start(bf16[272,512]{1,0:T(8,128)(2,1)} %collective-permute-done.8.refs_12_.refs_27_), channel_id=1, source_target_pairs={{0,2},{2,0},{4,6},{6,4},{8,10},{10,8},{12,14},{14,12},{16,18},{18,... | collective-permute-start | bytes 835592 | tf_op jit(solution)/shard_map/ppermute | solution.py:99
  51.8 3.9 %collective-permute-start.16 = (bf16[272,512]{1,0:T(8,128)(2,1)}, bf16[272,512]{1,0:T(8,128)(2,1)}, u32[]{:S(2)}, u32[]{:S(2)}) collective-permute-start(bf16[272,512]{1,0:T(8,128)(2,1)} %collective-permute-done.9.refs_13_.refs_28_), channel_id=1, source_target_pairs={{0,2},{2,0},{4,6},{6,4},{8,10},{10,8},{12,14},{14,12},{16,18},{18,... | collective-permute-start | bytes 835592 | tf_op jit(solution)/shard_map/ppermute | solution.py:99
  52.5 10.0 %collective-permute-start.18 = (bf16[272,512]{1,0:T(8,128)(2,1)}, bf16[272,512]{1,0:T(8,128)(2,1)}, u32[]{:S(2)}, u32[]{:S(2)}) collective-permute-start(bf16[272,512]{1,0:T(8,128)(2,1)} %collective-permute-done.17.refs_8_.refs_29_), channel_id=1, source_target_pairs={{0,2},{2,0},{4,6},{6,4},{8,10},{10,8},{12,14},{14,12},{16,18},{18,... | collective-permute-start | bytes 835592 | tf_op jit(solution)/shard_map/ppermute | solution.py:99
  65.2 5.1 %collective-permute-start.19 = (bf16[8,32,256]{2,1,0:T(8,128)(2,1)S(1)}, bf16[8,32,256]{2,1,0:T(8,128)(2,1)S(1)}, u32[]{:S(2)}, u32[]{:S(2)}) collective-permute-start(bf16[8,32,256]{2,1,0:T(8,128)(2,1)S(1)} %get-tuple-element.13), channel_id=1, source_target_pairs={{0,1},{1,0},{2,3},{3,2},{4,5},{5,4},{6,7},{7,6},{8,9},{9,8},{10,11... | collective-permute-start | bytes 393224 | tf_op jit(solution)/shard_map/ppermute | solution.py:103
  70.4 7.1 %collective-permute-start.20 = (bf16[2,8,32,256]{3,2,1,0:T(8,128)(2,1)S(1)}, bf16[2,8,32,256]{3,2,1,0:T(8,128)(2,1)S(1)}, u32[]{:S(2)}, u32[]{:S(2)}) collective-permute-start(bf16[2,8,32,256]{3,2,1,0:T(8,128)(2,1)S(1)} %pad_maximum_fusion.refs_6_), channel_id=1, source_target_pairs={{0,8},{2,10},{4,0},{6,2},{8,16},{10,18},{12,4},{14,6},{16,24},{18,... | collective-permute-start | bytes 786440 | tf_op jit(solution)/shard_map/ppermute | solution.py:113
  71.9 7.0 %collective-permute-start.21 = (bf16[2,8,32,256]{3,2,1,0:T(8,128)(2,1)S(1)}, bf16[2,8,32,256]{3,2,1,0:T(8,128)(2,1)S(1)}, u32[]{:S(2)}, u32[]{:S(2)}) collective-permute-start(bf16[2,8,32,256]{3,2,1,0:T(8,128)(2,1)S(1)} %pad_maximum_fusion.refs_6_), channel_id=1, source_target_pairs={{0,4},{2,6},{4,12},{6,14},{8,0},{10,2},{12,20},{14,22},{16,8},{18,... | collective-permute-start | bytes 786440 | tf_op jit(solution)/shard_map/ppermute | solution.py:113
  77.4 6.1 %collective-permute-start.22 = (bf16[2,8,32,256]{3,2,1,0:T(8,128)(2,1)S(1)}, bf16[2,8,32,256]{3,2,1,0:T(8,128)(2,1)S(1)}, u32[]{:S(2)}, u32[]{:S(2)}) collective-permute-start(bf16[2,8,32,256]{3,2,1,0:T(8,128)(2,1)S(1)} %collective-permute-done.20.refs_7_), channel_id=1, source_target_pairs={{0,8},{2,10},{4,0},{6,2},{8,16},{10,18},{12,4},{14,6},{16,24},{18,... | collective-permute-start | bytes 786440 | tf_op jit(solution)/shard_map/ppermute | solution.py:113
  78.9 9.5 %collective-permute-start.23 = (bf16[2,8,32,256]{3,2,1,0:T(8,128)(2,1)S(1)}, bf16[2,8,32,256]{3,2,1,0:T(8,128)(2,1)S(1)}, u32[]{:S(2)}, u32[]{:S(2)}) collective-permute-start(bf16[2,8,32,256]{3,2,1,0:T(8,128)(2,1)S(1)} %collective-permute-done.21.refs_8_), channel_id=1, source_target_pairs={{0,4},{2,6},{4,12},{6,14},{8,0},{10,2},{12,20},{14,22},{16,8},{18,... | collective-permute-start | bytes 786440 | tf_op jit(solution)/shard_map/ppermute | solution.py:113
  83.6 5.2 %collective-permute-start.24 = (bf16[2,8,32,256]{3,2,1,0:T(8,128)(2,1)S(1)}, bf16[2,8,32,256]{3,2,1,0:T(8,128)(2,1)S(1)}, u32[]{:S(2)}, u32[]{:S(2)}) collective-permute-start(bf16[2,8,32,256]{3,2,1,0:T(8,128)(2,1)S(1)} %collective-permute-done.22.refs_9_), channel_id=1, source_target_pairs={{0,8},{2,10},{4,0},{6,2},{8,16},{10,18},{12,4},{14,6},{16,24},{18,... | collective-permute-start | bytes 786440 | tf_op jit(solution)/shard_map/ppermute | solution.py:113
  85.0 5.2 %collective-permute-start.27 = (bf16[2,8,32,256]{3,2,1,0:T(8,128)(2,1)S(1)}, bf16[2,8,32,256]{3,2,1,0:T(8,128)(2,1)S(1)}, u32[]{:S(2)}, u32[]{:S(2)}) collective-permute-start(bf16[2,8,32,256]{3,2,1,0:T(8,128)(2,1)S(1)} %pad_maximum_fusion.refs_6_), channel_id=1, source_target_pairs={{0,2},{2,0},{4,6},{6,4},{8,10},{10,8},{12,14},{14,12},{16,18},{18,... | collective-permute-start | bytes 786440 | tf_op jit(solution)/shard_map/ppermute | solution.py:99
  87.9 7.0 %collective-permute-start.28 = (bf16[2,8,32,256]{3,2,1,0:T(8,128)(2,1)S(1)}, bf16[2,8,32,256]{3,2,1,0:T(8,128)(2,1)S(1)}, u32[]{:S(2)}, u32[]{:S(2)}) collective-permute-start(bf16[2,8,32,256]{3,2,1,0:T(8,128)(2,1)S(1)} %collective-permute-done.20.refs_7_), channel_id=1, source_target_pairs={{0,2},{2,0},{4,6},{6,4},{8,10},{10,8},{12,14},{14,12},{16,18},{18,... | collective-permute-start | bytes 786440 | tf_op jit(solution)/shard_map/ppermute | solution.py:99
  87.9 7.1 %collective-permute-start.29 = (bf16[2,8,32,256]{3,2,1,0:T(8,128)(2,1)S(1)}, bf16[2,8,32,256]{3,2,1,0:T(8,128)(2,1)S(1)}, u32[]{:S(2)}, u32[]{:S(2)}) collective-permute-start(bf16[2,8,32,256]{3,2,1,0:T(8,128)(2,1)S(1)} %collective-permute-done.21.refs_8_), channel_id=1, source_target_pairs={{0,2},{2,0},{4,6},{6,4},{8,10},{10,8},{12,14},{14,12},{16,18},{18,... | collective-permute-start | bytes 786440 | tf_op jit(solution)/shard_map/ppermute | solution.py:99
  88.4 7.9 %collective-permute-start.25 = (bf16[2,8,32,256]{3,2,1,0:T(8,128)(2,1)S(1)}, bf16[2,8,32,256]{3,2,1,0:T(8,128)(2,1)S(1)}, u32[]{:S(2)}, u32[]{:S(2)}) collective-permute-start(bf16[2,8,32,256]{3,2,1,0:T(8,128)(2,1)S(1)} %collective-permute-done.23.refs_10_), channel_id=1, source_target_pairs={{0,4},{2,6},{4,12},{6,14},{8,0},{10,2},{12,20},{14,22},{16,8},{18,... | collective-permute-start | bytes 786440 | tf_op jit(solution)/shard_map/ppermute | solution.py:113
  88.8 8.3 %collective-permute-start.26 = (bf16[2,8,32,256]{3,2,1,0:T(8,128)(2,1)S(1)}, bf16[2,8,32,256]{3,2,1,0:T(8,128)(2,1)S(1)}, u32[]{:S(2)}, u32[]{:S(2)}) collective-permute-start(bf16[2,8,32,256]{3,2,1,0:T(8,128)(2,1)S(1)} %collective-permute-done.24.refs_11_), channel_id=1, source_target_pairs={{0,8},{2,10},{4,0},{6,2},{8,16},{10,18},{12,4},{14,6},{16,24},{18,... | collective-permute-start | bytes 786440 | tf_op jit(solution)/shard_map/ppermute | solution.py:113
  90.3 9.2 %collective-permute-start.30 = (bf16[2,8,32,256]{3,2,1,0:T(8,128)(2,1)S(1)}, bf16[2,8,32,256]{3,2,1,0:T(8,128)(2,1)S(1)}, u32[]{:S(2)}, u32[]{:S(2)}) collective-permute-start(bf16[2,8,32,256]{3,2,1,0:T(8,128)(2,1)S(1)} %collective-permute-done.22.refs_9_), channel_id=1, source_target_pairs={{0,2},{2,0},{4,6},{6,4},{8,10},{10,8},{12,14},{14,12},{16,18},{18,... | collective-permute-start | bytes 786440 | tf_op jit(solution)/shard_map/ppermute | solution.py:99
  94.9 4.6 %collective-permute-start.31 = (bf16[2,8,32,256]{3,2,1,0:T(8,128)(2,1)S(1)}, bf16[2,8,32,256]{3,2,1,0:T(8,128)(2,1)S(1)}, u32[]{:S(2)}, u32[]{:S(2)}) collective-permute-start(bf16[2,8,32,256]{3,2,1,0:T(8,128)(2,1)S(1)} %collective-permute-done.23.refs_10_), channel_id=1, source_target_pairs={{0,2},{2,0},{4,6},{6,4},{8,10},{10,8},{12,14},{14,12},{16,18},{18,... | collective-permute-start | bytes 786440 | tf_op jit(solution)/shard_map/ppermute | solution.py:99
  95.0 4.6 %collective-permute-start.32 = (bf16[2,8,32,256]{3,2,1,0:T(8,128)(2,1)S(1)}, bf16[2,8,32,256]{3,2,1,0:T(8,128)(2,1)S(1)}, u32[]{:S(2)}, u32[]{:S(2)}) collective-permute-start(bf16[2,8,32,256]{3,2,1,0:T(8,128)(2,1)S(1)} %collective-permute-done.24.refs_11_), channel_id=1, source_target_pairs={{0,2},{2,0},{4,6},{6,4},{8,10},{10,8},{12,14},{14,12},{16,18},{18,... | collective-permute-start | bytes 786440 | tf_op jit(solution)/shard_map/ppermute | solution.py:99
  107.9 3.9 %collective-permute-start.35 = (bf16[176,256]{1,0:T(8,128)(2,1)S(1)}, bf16[176,256]{1,0:T(8,128)(2,1)S(1)}, u32[]{:S(2)}, u32[]{:S(2)}) collective-permute-start(bf16[176,256]{1,0:T(8,128)(2,1)S(1)} %get-tuple-element.15), channel_id=1, source_target_pairs={{0,1},{1,0},{2,3},{3,2},{4,5},{5,4},{6,7},{7,6},{8,9},{9,8},{10,11... | collective-permute-start | bytes 270344 | tf_op jit(solution)/shard_map/ppermute | solution.py:103
  111.8 8.2 %collective-permute-start.36 = (bf16[2,176,256]{2,1,0:T(8,128)(2,1)S(1)}, bf16[2,176,256]{2,1,0:T(8,128)(2,1)S(1)}, u32[]{:S(2)}, u32[]{:S(2)}) collective-permute-start(bf16[2,176,256]{2,1,0:T(8,128)(2,1)S(1)} %pad_maximum_fusion.1.refs_3_), channel_id=1, source_target_pairs={{0,8},{2,10},{4,0},{6,2},{8,16},{10,18},{12,4},{14,6},{16,24},{18,... | collective-permute-start | bytes 540680 | tf_op jit(solution)/shard_map/ppermute | solution.py:113
  113.3 20.8 %collective-permute-start = (bf16[512,512]{1,0:T(8,128)(2,1)S(1)}, bf16[512,512]{1,0:T(8,128)(2,1)S(1)}, u32[]{:S(2)}, u32[]{:S(2)}) collective-permute-start(bf16[512,512]{1,0:T(8,128)(2,1)S(1)} %bitcast.26), channel_id=1, source_target_pairs={{0,2},{2,4},{4,6},{6,8},{8,10},{10,12},{12,14},{14,16},{16,18},{18... | collective-permute-start | bytes 1572872 | tf_op jit(solution)/shard_map/ppermute | solution.py:433
  116.7 18.0 %collective-permute-start.1 = (bf16[512,512]{1,0:T(8,128)(2,1)S(1)}, bf16[512,512]{1,0:T(8,128)(2,1)S(1)}, u32[]{:S(2)}, u32[]{:S(2)}) collective-permute-start(bf16[512,512]{1,0:T(8,128)(2,1)S(1)} %bitcast.27), channel_id=1, source_target_pairs={{2,0},{4,2},{6,4},{8,6},{10,8},{12,10},{14,12},{16,14},{18,16},{20... | collective-permute-start | bytes 1572872 | tf_op jit(solution)/shard_map/ppermute | solution.py:434
  118.6 13.7 %collective-permute-start.37 = (bf16[2,176,256]{2,1,0:T(8,128)(2,1)S(1)}, bf16[2,176,256]{2,1,0:T(8,128)(2,1)S(1)}, u32[]{:S(2)}, u32[]{:S(2)}) collective-permute-start(bf16[2,176,256]{2,1,0:T(8,128)(2,1)S(1)} %pad_maximum_fusion.1.refs_3_), channel_id=1, source_target_pairs={{0,4},{2,6},{4,12},{6,14},{8,0},{10,2},{12,20},{14,22},{16,8},{18,... | collective-permute-start | bytes 540680 | tf_op jit(solution)/shard_map/ppermute | solution.py:113
  120.1 14.1 %collective-permute-start.38 = (bf16[2,176,256]{2,1,0:T(8,128)(2,1)S(1)}, bf16[2,176,256]{2,1,0:T(8,128)(2,1)S(1)}, u32[]{:S(2)}, u32[]{:S(2)}) collective-permute-start(bf16[2,176,256]{2,1,0:T(8,128)(2,1)S(1)} %collective-permute-done.36.refs_4_), channel_id=1, source_target_pairs={{0,8},{2,10},{4,0},{6,2},{8,16},{10,18},{12,4},{14,6},{16,24},{18,... | collective-permute-start | bytes 540680 | tf_op jit(solution)/shard_map/ppermute | solution.py:113
  132.2 6.5 %collective-permute-start.39 = (bf16[2,176,256]{2,1,0:T(8,128)(2,1)S(1)}, bf16[2,176,256]{2,1,0:T(8,128)(2,1)S(1)}, u32[]{:S(2)}, u32[]{:S(2)}) collective-permute-start(bf16[2,176,256]{2,1,0:T(8,128)(2,1)S(1)} %collective-permute-done.37.refs_5_), channel_id=1, source_target_pairs={{0,4},{2,6},{4,12},{6,14},{8,0},{10,2},{12,20},{14,22},{16,8},{18,... | collective-permute-start | bytes 540680 | tf_op jit(solution)/shard_map/ppermute | solution.py:113
  134.1 6.5 %collective-permute-start.40 = (bf16[2,176,256]{2,1,0:T(8,128)(2,1)S(1)}, bf16[2,176,256]{2,1,0:T(8,128)(2,1)S(1)}, u32[]{:S(2)}, u32[]{:S(2)}) collective-permute-start(bf16[2,176,256]{2,1,0:T(8,128)(2,1)S(1)} %collective-permute-done.38.refs_6_), channel_id=1, source_target_pairs={{0,8},{2,10},{4,0},{6,2},{8,16},{10,18},{12,4},{14,6},{16,24},{18,... | collective-permute-start | bytes 540680 | tf_op jit(solution)/shard_map/ppermute | solution.py:113
  134.1 7.1 %collective-permute-start.43 = (bf16[2,176,256]{2,1,0:T(8,128)(2,1)S(1)}, bf16[2,176,256]{2,1,0:T(8,128)(2,1)S(1)}, u32[]{:S(2)}, u32[]{:S(2)}) collective-permute-start(bf16[2,176,256]{2,1,0:T(8,128)(2,1)S(1)} %pad_maximum_fusion.1.refs_3_), channel_id=1, source_target_pairs={{0,2},{2,0},{4,6},{6,4},{8,10},{10,8},{12,14},{14,12},{16,18},{18,... | collective-permute-start | bytes 540680 | tf_op jit(solution)/shard_map/ppermute | solution.py:99
  134.2 7.7 %collective-permute-start.44 = (bf16[2,176,256]{2,1,0:T(8,128)(2,1)S(1)}, bf16[2,176,256]{2,1,0:T(8,128)(2,1)S(1)}, u32[]{:S(2)}, u32[]{:S(2)}) collective-permute-start(bf16[2,176,256]{2,1,0:T(8,128)(2,1)S(1)} %collective-permute-done.36.refs_4_), channel_id=1, source_target_pairs={{0,2},{2,0},{4,6},{6,4},{8,10},{10,8},{12,14},{14,12},{16,18},{18,... | collective-permute-start | bytes 540680 | tf_op jit(solution)/shard_map/ppermute | solution.py:99
  134.7 7.3 %collective-permute-start.45 = (bf16[2,176,256]{2,1,0:T(8,128)(2,1)S(1)}, bf16[2,176,256]{2,1,0:T(8,128)(2,1)S(1)}, u32[]{:S(2)}, u32[]{:S(2)}) collective-permute-start(bf16[2,176,256]{2,1,0:T(8,128)(2,1)S(1)} %collective-permute-done.37.refs_5_), channel_id=1, source_target_pairs={{0,2},{2,0},{4,6},{6,4},{8,10},{10,8},{12,14},{14,12},{16,18},{18,... | collective-permute-start | bytes 540680 | tf_op jit(solution)/shard_map/ppermute | solution.py:99
  138.8 5.7 %collective-permute-start.41 = (bf16[2,176,256]{2,1,0:T(8,128)(2,1)S(1)}, bf16[2,176,256]{2,1,0:T(8,128)(2,1)S(1)}, u32[]{:S(2)}, u32[]{:S(2)}) collective-permute-start(bf16[2,176,256]{2,1,0:T(8,128)(2,1)S(1)} %collective-permute-done.39.refs_7_), channel_id=1, source_target_pairs={{0,4},{2,6},{4,12},{6,14},{8,0},{10,2},{12,20},{14,22},{16,8},{18,... | collective-permute-start | bytes 540680 | tf_op jit(solution)/shard_map/ppermute | solution.py:113
  140.6 5.6 %collective-permute-start.42 = (bf16[2,176,256]{2,1,0:T(8,128)(2,1)S(1)}, bf16[2,176,256]{2,1,0:T(8,128)(2,1)S(1)}, u32[]{:S(2)}, u32[]{:S(2)}) collective-permute-start(bf16[2,176,256]{2,1,0:T(8,128)(2,1)S(1)} %collective-permute-done.40.refs_8_), channel_id=1, source_target_pairs={{0,8},{2,10},{4,0},{6,2},{8,16},{10,18},{12,4},{14,6},{16,24},{18,... | collective-permute-start | bytes 540680 | tf_op jit(solution)/shard_map/ppermute | solution.py:113
  141.3 8.6 %collective-permute-start.46 = (bf16[2,176,256]{2,1,0:T(8,128)(2,1)S(1)}, bf16[2,176,256]{2,1,0:T(8,128)(2,1)S(1)}, u32[]{:S(2)}, u32[]{:S(2)}) collective-permute-start(bf16[2,176,256]{2,1,0:T(8,128)(2,1)S(1)} %collective-permute-done.38.refs_6_), channel_id=1, source_target_pairs={{0,2},{2,0},{4,6},{6,4},{8,10},{10,8},{12,14},{14,12},{16,18},{18,... | collective-permute-start | bytes 540680 | tf_op jit(solution)/shard_map/ppermute | solution.py:99
  141.9 8.0 %collective-permute-start.47 = (bf16[2,176,256]{2,1,0:T(8,128)(2,1)S(1)}, bf16[2,176,256]{2,1,0:T(8,128)(2,1)S(1)}, u32[]{:S(2)}, u32[]{:S(2)}) collective-permute-start(bf16[2,176,256]{2,1,0:T(8,128)(2,1)S(1)} %collective-permute-done.39.refs_7_), channel_id=1, source_target_pairs={{0,2},{2,0},{4,6},{6,4},{8,10},{10,8},{12,14},{14,12},{16,18},{18,... | collective-permute-start | bytes 540680 | tf_op jit(solution)/shard_map/ppermute | solution.py:99
  142.0 7.9 %collective-permute-start.48 = (bf16[2,176,256]{2,1,0:T(8,128)(2,1)S(1)}, bf16[2,176,256]{2,1,0:T(8,128)(2,1)S(1)}, u32[]{:S(2)}, u32[]{:S(2)}) collective-permute-start(bf16[2,176,256]{2,1,0:T(8,128)(2,1)S(1)} %collective-permute-done.40.refs_8_), channel_id=1, source_target_pairs={{0,2},{2,0},{4,6},{6,4},{8,10},{10,8},{12,14},{14,12},{16,18},{18,... | collective-permute-start | bytes 540680 | tf_op jit(solution)/shard_map/ppermute | solution.py:99
  144.4 5.4 %collective-permute-start.49 = (bf16[2,176,256]{2,1,0:T(8,128)(2,1)S(1)}, bf16[2,176,256]{2,1,0:T(8,128)(2,1)S(1)}, u32[]{:S(2)}, u32[]{:S(2)}) collective-permute-start(bf16[2,176,256]{2,1,0:T(8,128)(2,1)S(1)} %collective-permute-done.41.refs_9_), channel_id=1, source_target_pairs={{0,2},{2,0},{4,6},{6,4},{8,10},{10,8},{12,14},{14,12},{16,18},{18,... | collective-permute-start | bytes 540680 | tf_op jit(solution)/shard_map/ppermute | solution.py:99
  (14 other events, 226.1 us)

commit v3 on v2

--- a/solution.py
+++ b/solution.py
@@ -269,21 +269,24 @@
     return parts
 
 
-def iter2_kernel(slots, *refs):
-    n_slots = len(slots)
+def iter2_kernel(n_slots, early, late, *refs):
     scal_ref, table_ref, sizes_ref, factor_ref, left_ref, prev_ref = refs[:6]
-    psi_pieces = refs[6 : 6 + n_slots]
-    right_pieces = refs[6 + n_slots : 6 + 2 * n_slots]
-    keep_ref, send_ref, psi, inner, right, low, psems, rsems = refs[6 + 2 * n_slots :]
+    psi_pieces = refs[6 : 6 + 2 * n_slots]
+    right_pieces = refs[6 + 2 * n_slots : 9 + 2 * n_slots]
+    keep_ref, send_ref, psi, inner, right, low, psems, rsems = refs[9 + 2 * n_slots :]
     sec = scal_ref[2]
     sectors, rows, cols = prev_ref.shape
     local = sectors // 2
     pairs = []
     for i, piece in enumerate(psi_pieces):
-        at = pl.ds(table_ref[i] * rows, rows)
-        pairs += [(piece.at[h], psi.at[sec if h == 0 else 1 - sec, :, at]) for h in range(2)]
+        at = pl.ds(table_ref[i % n_slots] * rows, rows)
+        pairs.append((piece, psi.at[sec if i < n_slots else 1 - sec, :, at]))
     psi_copies = copy_in(pairs, psems)
-    right_copies = copy_in([(piece, right.at[i]) for i, piece in enumerate(right_pieces)], rsems)
+    right_copies = copy_in(
+        [(right_pieces[0], right.at[pl.ds(0, len(early))])]
+        + [(right_pieces[1 + c], right.at[len(early) + c]) for c in range(2)],
+        rsems,
+    )
     wait_all(psi_copies)
 
     @pl.loop(0, sectors, unroll=2)
@@ -292,7 +295,7 @@
             inner[:, s, :, h * cols : (h + 1) * cols] = first_stage(left_ref, psi[h, s], inner.shape)
 
     wait_all(right_copies)
-    acc = second_stage([inner.at[table_ref[i]] for i in range(n_slots)], right, cols)
+    acc = second_stage([inner.at[table_ref[i]] for i in early + late], right, cols)
     before = jnp.zeros((rows, cols), jnp.float32)
     after = jnp.zeros((rows, cols), jnp.float32)
     for s in range(sectors):
@@ -319,25 +322,25 @@
 
 def final_kernel(slots, values, *refs):
     n_slots = len(slots)
-    scal_ref, table_ref, mixer_ref = refs[:3]
-    pieces = refs[3 : 3 + n_slots]
-    wave_ref, mixed_ref, basis = refs[3 + n_slots :]
-    sec = scal_ref[2]
+    scal_ref, table_ref, weights_ref = refs[:3]
+    left_refs = refs[3:6]
+    pieces = refs[6 : 6 + 2 * n_slots]
+    wave_ref, mixed_ref, basis, lefts, sems = refs[6 + 2 * n_slots :]
+    copies = copy_in([(ref, lefts.at[d]) for d, ref in enumerate(left_refs)], sems)
+    core, sec = scal_ref[1], scal_ref[2]
     local, width, _ = wave_ref.shape
     cols = width // 2
     rows = width // n_slots
-    tail = pieces[0].shape[1] - (local + 1) * rows
+    tail = pieces[0].shape[0] - (local + 1) * rows
     stats = jnp.zeros((tail, cols), jnp.float32)
     views = []
     for i, piece in enumerate(pieces):
-        at = pl.ds(pl.multiple_of(table_ref[i] * rows, rows), rows)
-        for h in range(2):
-            side = sec if h == 0 else 1 - sec
-            across = pl.ds(pl.multiple_of(side * cols, cols), cols)
-            view = piece.at[h]
-            views.append((view, at, across))
-            stats += view[(local + 1) * rows :].astype(jnp.float32)
-            basis[at, across] = view[local * rows : (local + 1) * rows]
+        at = pl.ds(pl.multiple_of(table_ref[i % n_slots] * rows, rows), rows)
+        side = sec if i < n_slots else 1 - sec
+        across = pl.ds(pl.multiple_of(side * cols, cols), cols)
+        views.append((piece, at, across))
+        stats += piece[(local + 1) * rows :].astype(jnp.float32)
+        basis[at, across] = piece[local * rows : (local + 1) * rows]
     line = lax.broadcasted_iota(jnp.int32, (tail, cols), 0)
     first = jnp.sum(jnp.where(line < 3, stats, 0.0), axis=0, keepdims=True)[:, :1]
     second = jnp.sum(jnp.where((line >= 3) & (line < 6), stats, 0.0), axis=0, keepdims=True)[:, :1]
@@ -348,7 +351,15 @@
         for view, at, across in views:
             wave_ref[s, at, across] = view[s * rows : (s + 1) * rows].astype(jnp.float32) * scale
     across = pl.ds(pl.multiple_of(sec * cols, cols), cols)
-    right = jnp.dot(mixer_ref[...], basis[:, across], preferred_element_type=jnp.float32)
+    swapped = core != 0
+    weights = (
+        weights_ref[1],
+        jnp.where(swapped, weights_ref[2], weights_ref[0]),
+        jnp.where(swapped, weights_ref[0], weights_ref[2]),
+    )
+    wait_all(copies)
+    mixer = sum(weights[d] * lefts[d].astype(jnp.float32) for d in range(3))
+    right = jnp.dot(mixer.astype(jnp.bfloat16), basis[:, across], preferred_element_type=jnp.float32)
     rotated = lax.dot_general(
         basis[...], right.astype(jnp.bfloat16), (((0,), (0,)), ((), ())), preferred_element_type=jnp.float32
     )
@@ -407,12 +418,15 @@
         [pltpu.VMEM((local, width, width), bf16), dma((local,))],
         10, sectors * width**3, psi_bytes,
     )(scal, sector_sizes, left_rows, wavefunction)
-    acc, rest = kernel_call(
+    acc, rest, right_early = kernel_call(
         functools.partial(early_kernel, early, late),
-        (shape((sectors * rows, cols), f32), shape((2, sectors, rows, width), bf16)),
+        (
+            shape((sectors * rows, cols), f32),
+            shape((2, sectors, rows, width), bf16),
+            shape((len(early), tall, width), bf16),
+        ),
         "sssvaaa" + "a" * len(early),
         [
-            pltpu.VMEM((len(early), tall, width), bf16),
             pltpu.VMEM((n, sectors, rows, width), bf16),
             pltpu.VMEM((local, width, width), bf16),
             dma((local,)),
@@ -430,38 +444,34 @@
     )(scal, sector_sizes, factors[:1], acc, rest, wavefunction, near, far, *[right_pieces[i] for i in late])
 
     low_2 = swap_sec(low_1)
-    below = lax.ppermute(left_ops[0], "ops", [(i, i + 1) for i in range(n - 1)])
-    above = lax.ppermute(left_ops[0], "ops", [(i + 1, i) for i in range(n - 1)])
-    psi_pieces = ring_gather(jnp.stack([low_1, low_2]), n)
-    mixer = (
-        integrals[0, 0] * below.astype(f32)
-        + integrals[0, 1] * left_ops[0].astype(f32)
-        + integrals[0, 2] * above.astype(f32)
-    ).astype(bf16)
-
+    pairs = [(k, k + 1) for k in range(1, n - 1, 2)]
+    left_cross = lax.ppermute(left_ops[0], "ops", pairs + [(b, a) for a, b in pairs])
+    left_local = swap_core(left_ops[0], n)
+    psi_pieces = ring_gather(low_1, n) + ring_gather(low_2, n)
     message = (local + 1) * rows + 16
     keep, send = kernel_call(
-        functools.partial(iter2_kernel, slots), (shape((message, cols), bf16),) * 2,
-        "ssssvv" + "a" * (2 * n_slots),
+        functools.partial(iter2_kernel, n_slots, early, late), (shape((message, cols), bf16),) * 2,
+        "ssssvv" + "a" * (2 * n_slots + 3),
         [
             pltpu.VMEM((2, sectors, width, cols), bf16),
             pltpu.VMEM((n, sectors, rows, width), bf16),
             pltpu.VMEM((n, tall, width), bf16),
             pltpu.VMEM((sectors, rows, cols), bf16),
             dma((2 * n_slots,)),
-            dma((n_slots,)),
+            dma((3,)),
         ],
         18, 3 * sectors * width**3, 2 * psi_bytes,
-    )(scal, table, sector_sizes, factors[1:2], left_rows, psi_1, *psi_pieces, *right_pieces)
+    )(scal, table, sector_sizes, factors[1:2], left_rows, psi_1, *psi_pieces, right_early, *[right_pieces[i] for i in late])
 
     recv = swap_sec(send)
-    last_pieces = ring_gather(jnp.stack([keep, recv]), n)
+    last_pieces = ring_gather(keep, n) + ring_gather(recv, n)
     wave, mixed = kernel_call(
         functools.partial(final_kernel, slots, float(sectors * width * width)),
         (shape((local, width, width), f32), shape((width, cols), bf16)),
-        "ssv" + "v" * n_slots, [pltpu.VMEM((width, width), bf16)],
+        "sssaaa" + "v" * (2 * n_slots),
+        [pltpu.VMEM((width, width), bf16), pltpu.VMEM((3, width, width), bf16), dma((3,))],
         16, 2 * width**3, 6 * local * width**2,
-    )(scal, table, mixer, *last_pieces)
+    )(scal, table, integrals[0], left_ops[0], left_cross, left_local, *last_pieces)
     return (wave, mixed[None])
 
 

time: 154 us -> 146 us (0.948)
  waiting for transfers between devices: 65.4 us -> 32.9 us
  starting transfers between devices: 55.4 us -> 83 us
  other arithmetic: 2.39 us -> 0.08 us
    ppermute x21 -> x35, waiting for transfers between devices: 48.3 us -> 20.1 us  [along_ring(): return lax.ppermute(x, 'ops', perm)]
    ppermute x25 -> x42, starting transfers between devices: 21 us -> 41.9 us  [swap_core(): return lax.ppermute(x, 'ops', [(o, o ^ 1) for o in range(n)])]
    ppermute x21 -> x35, starting transfers between devices: 19.6 us -> 29.1 us  [along_ring(): return lax.ppermute(x, 'ops', perm)]
    ppermute x3, waiting for transfers between devices: 15.2 us -> 10.1 us  [swap_sec(): return lax.ppermute(x, 'sec', [(0, 1), (1, 0)])]
    ppermute x2 -> x1, starting transfers between devices: 5.22 us -> 2.35 us  [gather_form(): lax.ppermute(left_ops[0], 'ops', pairs + [(b, a) for a, b in pairs])]
    convert_element_type x1 -> x0, other arithmetic: 2.27 us -> none  [gather_form(): mixer = (integrals[0, 0] * below.astype(f32) + integrals[0, 1] * left_ops...]
  transfers between devices with their start and end apart: 52 -> 82, of which waited for: 17 -> 12; matrix products, arithmetic and copies ran while one was open for 3% -> 1% of each run, Pallas kernels for 6% -> 12%
where the time goes in v3:
time: 146 us
  starting transfers between devices  83 us (57%)
  waiting for transfers between devices  32.9 us (23%)
  Pallas kernels  22.8 us (16%)
  local copies, waits for them, and re-layouts  5.27 us (4%)
  between operations  1.77 us (1%)
    ppermute x42, starting transfers between devices, swap_core(): return lax.ppermute(x, 'ops', [(o, o ^ 1) for o in range(n)])  41.9 us
    ppermute x35, starting transfers between devices, along_ring(): return lax.ppermute(x, 'ops', perm)  29.1 us
    ppermute x35, waiting for transfers between devices, along_ring(): return lax.ppermute(x, 'ops', perm)  20.1 us
    ppermute x3, waiting for transfers between devices, swap_sec(): return lax.ppermute(x, 'sec', [(0, 1), (1, 0)])  10.1 us
    pallas_call x1, Pallas kernels, gather_form(): kernel_call(functools.partial(iter2_kernel, n_slots, early, late), (shape...  7.53 us
    all_to_all x1, starting transfers between devices, gather_form(): left_rows = lax.all_to_all(left_ops[0], 'ops', 0, 0, tiled=True)  6.89 us
    pallas_call x1, Pallas kernels, gather_form(): kernel_call(functools.partial(early_kernel, early, late), (shape((sectors...  6.74 us
    pallas_call x1, Pallas kernels, gather_form(): kernel_call(functools.partial(final_kernel, slots, float(sectors * width...  3.24 us
  transfers between devices with their start and end apart: 82, of which 12 were waited for; matrix products, arithmetic and copies ran while one was open for 1% of the time, Pallas kernels for 12%

profile of v3, /device:TPU:1, one launch (start us, length us, event | category | flops | bytes accessed | tf_op | source)
XLA Modules:
  0.0 145.8 jit_solution(13009146326043041183)
XLA Ops:
  0.7 2.4 %constant_dynamic-slice_fusion = bf16[2,512,512]{2,1,0:T(8,128)(2,1)} fusion(bf16[4,512,512]{2,1,0:T(8,128)(2,1)} %refs_5_.1, s32[]{:T(128)S(6)} %select_n.10), kind=kLoop, calls=%fused_computation.1 | loop fusion | bytes 2097156 | tf_op jit(solution)/shard_map/dynamic_slice | solution.py:412
  3.1 2.1 %collective-permute-start.2 = (bf16[2,512,512]{2,1,0:T(8,128)(2,1)}, bf16[2,512,512]{2,1,0:T(8,128)(2,1)}, u32[]{:S(2)}, u32[]{:S(2)}) collective-permute-start(bf16[2,512,512]{2,1,0:T(8,128)(2,1)} %constant_dynamic-slice_fusion), channel_id=1, source_target_pairs={{0,1},{1,0},{2,3},{3,2},{4,5},{5,4},{6,7},{7,6},{8,9},{9,8},{10,11... | collective-permute-start | bytes 3145736 | tf_op jit(solution)/shard_map/ppermute | solution.py:103
  5.9 1.3 collective-permute-start.4
  7.4 5.9 %collective-permute-done.4.refs_8_ = bf16[272,512]{1,0:T(8,128)(2,1)} collective-permute-done((bf16[272,512]{1,0:T(8,128)(2,1)S(1)}, bf16[272,512]{1,0:T(8,128)(2,1)}, u32[]{:S(2)}, u32[]{:S(2)}) %collective-permute-start.4) | collective-permute-done | bytes 278560 | tf_op jit(solution)/shard_map/ppermute | solution.py:113
  13.3 1.3 collective-permute-start.6
  14.6 6.9 %all-to-all-start = ((bf16[16,32,512]{2,1,0:T(8,128)(2,1)}), bf16[16,32,512]{2,1,0:T(8,128)(2,1)S(1)}, u32[]{:S(2)}, u32[]{:S(2)}) async-start(bf16[16,32,512]{2,1,0:T(8,128)(2,1)} %bitcast.16), calls=%async_computation | async-start | bytes 1048576 | tf_op jit(solution)/shard_map/all_to_all | solution.py:411
  21.5 6.8 %collective-permute-done.2.refs_5_.refs_6_ = bf16[2,512,512]{2,1,0:T(8,128)(2,1)} collective-permute-done((bf16[2,512,512]{2,1,0:T(8,128)(2,1)}, bf16[2,512,512]{2,1,0:T(8,128)(2,1)}, u32[]{:S(2)}, u32[]{:S(2)}) %collective-permute-start.2) | collective-permute-done | bytes 1048608 | tf_op jit(solution)/shard_map/ppermute | solution.py:103
  28.3 1.3 collective-permute-start.3
  29.6 1.4 collective-permute-start.7
  33.6 5.7 %collective-permute-done.7.refs_11_ = bf16[272,512]{1,0:T(8,128)(2,1)} collective-permute-done((bf16[272,512]{1,0:T(8,128)(2,1)}, bf16[272,512]{1,0:T(8,128)(2,1)}, u32[]{:S(2)}, u32[]{:S(2)}) %collective-permute-start.7) | collective-permute-done | bytes 278560 | tf_op jit(solution)/shard_map/ppermute | solution.py:113
  39.3 1.1 collective-permute-start.13
  41.9 2.1 %collective-permute-start.17 = (bf16[272,512]{1,0:T(8,128)(2,1)}, bf16[272,512]{1,0:T(8,128)(2,1)}, u32[]{:S(2)}, u32[]{:S(2)}) collective-permute-start(bf16[272,512]{1,0:T(8,128)(2,1)} %collective-permute-done.8.refs_12_), channel_id=1, source_target_pairs={{0,8},{2,10},{4,0},{6,2},{8,16},{10,18},{12,4},{14,6},{16,24},{18,... | collective-permute-start | bytes 835592 | tf_op jit(solution)/shard_map/ppermute | solution.py:113
  44.9 6.4 %collective-permute-done.9.refs_13_ = bf16[272,512]{1,0:T(8,128)(2,1)} collective-permute-done((bf16[272,512]{1,0:T(8,128)(2,1)}, bf16[272,512]{1,0:T(8,128)(2,1)}, u32[]{:S(2)}, u32[]{:S(2)}) %collective-permute-start.9) | collective-permute-done | bytes 278560 | tf_op jit(solution)/shard_map/ppermute | solution.py:113
  53.2 2.6 %shard_map.95.refs_4_ = bf16[16,4,32,512]{3,2,1,0:T(8,128)(2,1)S(1)} custom-call(s32[3]{0:T(128)S(1)} %pad_add_fusion.scal_ref.refs_0_, s32[8]{0:T(128)S(1)} %copy-done.7, bf16[512,512]{1,0:T(8,128)(2,1)S(1)} %bitcast.13, bf16[4,512,512]{2,1,0:T(8,128)(2,1)S(1)} %copy-done.1), custom_call_target="tpu_custom_call" | custom-call | flops 1073741824 | bytes 4194304 | tf_op jit(solution)/shard_map/pallas_call | solution.py:416
  55.8 6.7 %shard_map.96 = (f32[256,256]{1,0:T(8,128)S(1)}, bf16[2,8,32,512]{3,2,1,0:T(8,128)(2,1)S(1)}, bf16[14,272,512]{2,1,0:T(8,128)(2,1)S(1)}) custom-call(s32[3]{0:T(128)S(1)} %pad_add_fusion.scal_ref.refs_0_, s32[16]{0:T(128)S(1)} %fusion.refs_1_, s32[8]{0:T(128)S(1)} %copy-done.7, bf16[512,512]{1,0:T(8,128)(2,1)S(1)} %bitcast.14, ...), custom_call_target="tpu_custom_call" | custom-call | flops 1073741824 | bytes 8388608 | tf_op jit(solution)/shard_map/pallas_call | solution.py:421
  62.6 2.7 %shard_map.97 = (f32[8,32,256]{2,1,0:T(8,128)S(1)}, bf16[8,32,256]{2,1,0:T(8,128)(2,1)S(1)}) custom-call(s32[3]{0:T(128)S(1)} %pad_add_fusion.scal_ref.refs_0_, s32[8]{0:T(128)S(1)} %copy-done.7, f32[1]{0:T(128)} %get-tuple-element.20.refs_2_, f32[256,256]{1,0:T(8,128)S(1)} %get-tuple-element.11.refs_3_, ...), custom_call_target="tpu_custom_call" | custom-call | flops 268435456 | bytes 1048576 | tf_op jit(solution)/shard_map/pallas_call | solution.py:438
  65.6 1.5 %collective-permute-start.19 = (bf16[8,32,256]{2,1,0:T(8,128)(2,1)S(1)}, bf16[8,32,256]{2,1,0:T(8,128)(2,1)S(1)}, u32[]{:S(2)}, u32[]{:S(2)}) collective-permute-start(bf16[8,32,256]{2,1,0:T(8,128)(2,1)S(1)} %get-tuple-element.14.refs_6_), channel_id=1, source_target_pairs={{0,8},{2,10},{4,0},{6,2},{8,16},{10,18},{12,4},{14,6},{16,24},{18,... | collective-permute-start | bytes 393224 | tf_op jit(solution)/shard_map/ppermute | solution.py:113
  67.9 2.5 %collective-permute-done.34.refs_22_ = bf16[8,32,256]{2,1,0:T(8,128)(2,1)S(1)} collective-permute-done((bf16[8,32,256]{2,1,0:T(8,128)(2,1)S(1)}, bf16[8,32,256]{2,1,0:T(8,128)(2,1)S(1)}, u32[]{:S(2)}, u32[]{:S(2)}) %collective-permute-start.34) | collective-permute-done | bytes 131104 | tf_op jit(solution)/shard_map/ppermute | solution.py:103
  70.4 1.5 collective-permute-start.35
  72.1 1.2 collective-permute-start.36
  73.4 2.0 %collective-permute-start.27 = (bf16[8,32,256]{2,1,0:T(8,128)(2,1)S(1)}, bf16[8,32,256]{2,1,0:T(8,128)(2,1)S(1)}, u32[]{:S(2)}, u32[]{:S(2)}) collective-permute-start(bf16[8,32,256]{2,1,0:T(8,128)(2,1)S(1)} %collective-permute-done.19.refs_7_), channel_id=1, source_target_pairs={{0,2},{2,0},{4,6},{6,4},{8,10},{10,8},{12,14},{14,12},{16,18},{18,... | collective-permute-start | bytes 393224 | tf_op jit(solution)/shard_map/ppermute | solution.py:99
  75.3 2.3 %collective-permute-start.28 = (bf16[8,32,256]{2,1,0:T(8,128)(2,1)S(1)}, bf16[8,32,256]{2,1,0:T(8,128)(2,1)S(1)}, u32[]{:S(2)}, u32[]{:S(2)}) collective-permute-start(bf16[8,32,256]{2,1,0:T(8,128)(2,1)S(1)} %collective-permute-done.20.refs_8_), channel_id=1, source_target_pairs={{0,2},{2,0},{4,6},{6,4},{8,10},{10,8},{12,14},{14,12},{16,18},{18,... | collective-permute-start | bytes 393224 | tf_op jit(solution)/shard_map/ppermute | solution.py:99
  77.6 1.5 %collective-permute-start.42 = (bf16[8,32,256]{2,1,0:T(8,128)(2,1)S(1)}, bf16[8,32,256]{2,1,0:T(8,128)(2,1)S(1)}, u32[]{:S(2)}, u32[]{:S(2)}) collective-permute-start(bf16[8,32,256]{2,1,0:T(8,128)(2,1)S(1)} %collective-permute-done.34.refs_22_), channel_id=1, source_target_pairs={{0,2},{2,0},{4,6},{6,4},{8,10},{10,8},{12,14},{14,12},{16,18},{18,... | collective-permute-start | bytes 393224 | tf_op jit(solution)/shard_map/ppermute | solution.py:99
  79.1 1.5 %collective-permute-start.37 = (bf16[8,32,256]{2,1,0:T(8,128)(2,1)S(1)}, bf16[8,32,256]{2,1,0:T(8,128)(2,1)S(1)}, u32[]{:S(2)}, u32[]{:S(2)}) collective-permute-start(bf16[8,32,256]{2,1,0:T(8,128)(2,1)S(1)} %collective-permute-done.35.refs_23_), channel_id=1, source_target_pairs={{0,8},{2,10},{4,0},{6,2},{8,16},{10,18},{12,4},{14,6},{16,24},{18,... | collective-permute-start | bytes 393224 | tf_op jit(solution)/shard_map/ppermute | solution.py:113
  80.9 1.2 collective-permute-start.38
  82.1 2.2 %collective-permute-start.29 = (bf16[8,32,256]{2,1,0:T(8,128)(2,1)S(1)}, bf16[8,32,256]{2,1,0:T(8,128)(2,1)S(1)}, u32[]{:S(2)}, u32[]{:S(2)}) collective-permute-start(bf16[8,32,256]{2,1,0:T(8,128)(2,1)S(1)} %collective-permute-done.21.refs_9_), channel_id=1, source_target_pairs={{0,2},{2,0},{4,6},{6,4},{8,10},{10,8},{12,14},{14,12},{16,18},{18,... | collective-permute-start | bytes 393224 | tf_op jit(solution)/shard_map/ppermute | solution.py:99
  84.4 1.5 collective-permute-start.30
  86.7 1.2 collective-permute-start.43
  88.1 1.3 collective-permute-start.39
  90.9 1.3 collective-permute-start.31
  92.3 3.1 %collective-permute-start.45 = (bf16[8,32,256]{2,1,0:T(8,128)(2,1)S(1)}, bf16[8,32,256]{2,1,0:T(8,128)(2,1)S(1)}, u32[]{:S(2)}, u32[]{:S(2)}) collective-permute-start(bf16[8,32,256]{2,1,0:T(8,128)(2,1)S(1)} %collective-permute-done.37.refs_25_), channel_id=1, source_target_pairs={{0,2},{2,0},{4,6},{6,4},{8,10},{10,8},{12,14},{14,12},{16,18},{18,... | collective-permute-start | bytes 393224 | tf_op jit(solution)/shard_map/ppermute | solution.py:99
  95.4 1.4 collective-permute-start.46
  96.8 1.3 collective-permute-start.41
  98.4 2.3 %collective-permute-start = (bf16[512,512]{1,0:T(8,128)(2,1)S(1)}, bf16[512,512]{1,0:T(8,128)(2,1)S(1)}, u32[]{:S(2)}, u32[]{:S(2)}) collective-permute-start(bf16[512,512]{1,0:T(8,128)(2,1)S(1)} %bitcast.17), channel_id=1, source_target_pairs={{2,4},{6,8},{10,12},{14,16},{18,20},{22,24},{26,28},{4,2},{8,6},{1... | collective-permute-start | bytes 1572872 | tf_op jit(solution)/shard_map/ppermute | solution.py:448
  103.7 7.5 %shard_map.98 = (bf16[176,256]{1,0:T(8,128)(2,1)S(1)}, bf16[176,256]{1,0:T(8,128)(2,1)S(1)}) custom-call(s32[3]{0:T(128)S(1)} %pad_add_fusion.scal_ref.refs_0_, s32[16]{0:T(128)S(1)} %fusion.refs_1_, s32[8]{0:T(128)S(1)} %copy-done.7, f32[1]{0:T(128)} %get-tuple-element.21.refs_3_, bf16[512,512]{1,0:T(8,128)(2,1)S(1)} %bitcast.15, ...), custom_call_target="tpu_custom_call" | custom-call | flops 3221225472 | bytes 8388608 | tf_op jit(solution)/shard_map/pallas_call | solution.py:452
  111.6 1.2 collective-permute-start.50
  113.1 1.2 collective-permute-start.57
  115.1 1.3 collective-permute-start.66
  116.9 1.0 collective-permute-start.67
  118.1 2.3 %collective-permute-start.58 = (bf16[176,256]{1,0:T(8,128)(2,1)S(1)}, bf16[176,256]{1,0:T(8,128)(2,1)S(1)}, u32[]{:S(2)}, u32[]{:S(2)}) collective-permute-start(bf16[176,256]{1,0:T(8,128)(2,1)S(1)} %collective-permute-done.50.refs_7_), channel_id=1, source_target_pairs={{0,2},{2,0},{4,6},{6,4},{8,10},{10,8},{12,14},{14,12},{16,18},{18,... | collective-permute-start | bytes 270344 | tf_op jit(solution)/shard_map/ppermute | solution.py:99
  120.4 1.1 collective-permute-start.59
  121.5 1.0 collective-permute-start.73
  125.4 2.1 %collective-permute-start.60 = (bf16[176,256]{1,0:T(8,128)(2,1)S(1)}, bf16[176,256]{1,0:T(8,128)(2,1)S(1)}, u32[]{:S(2)}, u32[]{:S(2)}) collective-permute-start(bf16[176,256]{1,0:T(8,128)(2,1)S(1)} %collective-permute-done.52.refs_9_), channel_id=1, source_target_pairs={{0,2},{2,0},{4,6},{6,4},{8,10},{10,8},{12,14},{14,12},{16,18},{18,... | collective-permute-start | bytes 270344 | tf_op jit(solution)/shard_map/ppermute | solution.py:99
  132.3 1.8 %collective-permute-start.62 = (bf16[176,256]{1,0:T(8,128)(2,1)S(1)}, bf16[176,256]{1,0:T(8,128)(2,1)S(1)}, u32[]{:S(2)}, u32[]{:S(2)}) collective-permute-start(bf16[176,256]{1,0:T(8,128)(2,1)S(1)} %collective-permute-done.54.refs_11_), channel_id=1, source_target_pairs={{0,2},{2,0},{4,6},{6,4},{8,10},{10,8},{12,14},{14,12},{16,18},{18,... | collective-permute-start | bytes 270344 | tf_op jit(solution)/shard_map/ppermute | solution.py:99
  134.2 1.8 %collective-permute-start.76 = (bf16[176,256]{1,0:T(8,128)(2,1)S(1)}, bf16[176,256]{1,0:T(8,128)(2,1)S(1)}, u32[]{:S(2)}, u32[]{:S(2)}) collective-permute-start(bf16[176,256]{1,0:T(8,128)(2,1)S(1)} %collective-permute-done.68.refs_25_), channel_id=1, source_target_pairs={{0,2},{2,0},{4,6},{6,4},{8,10},{10,8},{12,14},{14,12},{16,18},{18,... | collective-permute-start | bytes 270344 | tf_op jit(solution)/shard_map/ppermute | solution.py:99
  136.9 1.2 collective-permute-start.77
  139.4 2.1 %collective-permute-start.80 = (bf16[176,256]{1,0:T(8,128)(2,1)S(1)}, bf16[176,256]{1,0:T(8,128)(2,1)S(1)}, u32[]{:S(2)}, u32[]{:S(2)}) collective-permute-start(bf16[176,256]{1,0:T(8,128)(2,1)S(1)} %collective-permute-done.72.refs_29_), channel_id=1, source_target_pairs={{0,2},{2,0},{4,6},{6,4},{8,10},{10,8},{12,14},{14,12},{16,18},{18,... | collective-permute-start | bytes 270344 | tf_op jit(solution)/shard_map/ppermute | solution.py:99
  142.4 3.2 %shard_map.99 = (f32[4,512,512]{2,1,0:T(8,128)}, bf16[512,256]{1,0:T(8,128)(2,1)}) custom-call(s32[3]{0:T(128)S(1)} %pad_add_fusion.scal_ref.refs_0_, s32[16]{0:T(128)S(1)} %fusion.refs_1_, f32[3]{0:T(128)S(1)} %bitcast.20, bf16[512,512]{1,0:T(8,128)(2,1)S(1)} %bitcast.19, bf16[512,512]{1,0:T(8,128)(2,1)S(1)} %collective-permute-done.refs_4_, ...), custom_call_target="tpu_custom_call" | custom-call | flops 268435456 | bytes 6291456 | tf_op jit(solution)/shard_map/pallas_call | solution.py:468
  (148 shorter events, 27.7 us)
Async XLA Ops:
  3.1 25.2 %collective-permute-start.2 = (bf16[2,512,512]{2,1,0:T(8,128)(2,1)}, bf16[2,512,512]{2,1,0:T(8,128)(2,1)}, u32[]{:S(2)}, u32[]{:S(2)}) collective-permute-start(bf16[2,512,512]{2,1,0:T(8,128)(2,1)} %constant_dynamic-slice_fusion), channel_id=1, source_target_pairs={{0,1},{1,0},{2,3},{3,2},{4,5},{5,4},{6,7},{7,6},{8,9},{9,8},{10,11... | collective-permute-start | bytes 3145736 | tf_op jit(solution)/shard_map/ppermute | solution.py:103
  5.9 7.4 %collective-permute-start.4 = (bf16[272,512]{1,0:T(8,128)(2,1)S(1)}, bf16[272,512]{1,0:T(8,128)(2,1)}, u32[]{:S(2)}, u32[]{:S(2)}) collective-permute-start(bf16[272,512]{1,0:T(8,128)(2,1)S(1)} %concatenate.3.refs_7_), channel_id=1, source_target_pairs={{0,8},{2,10},{4,0},{6,2},{8,16},{10,18},{12,4},{14,6},{16,24},{18,... | collective-permute-start | bytes 835592 | tf_op jit(solution)/shard_map/ppermute | solution.py:113
  7.2 22.4 %collective-permute-start.5 = (bf16[272,512]{1,0:T(8,128)(2,1)S(1)}, bf16[272,512]{1,0:T(8,128)(2,1)}, u32[]{:S(2)}, u32[]{:S(2)}) collective-permute-start(bf16[272,512]{1,0:T(8,128)(2,1)S(1)} %concatenate.3.refs_7_), channel_id=1, source_target_pairs={{0,4},{2,6},{4,12},{6,14},{8,0},{10,2},{12,20},{14,22},{16,8},{18,... | collective-permute-start | bytes 835592 | tf_op jit(solution)/shard_map/ppermute | solution.py:113
  13.3 18.5 %collective-permute-start.6 = (bf16[272,512]{1,0:T(8,128)(2,1)}, bf16[272,512]{1,0:T(8,128)(2,1)}, u32[]{:S(2)}, u32[]{:S(2)}) collective-permute-start(bf16[272,512]{1,0:T(8,128)(2,1)} %collective-permute-done.4.refs_8_), channel_id=1, source_target_pairs={{0,8},{2,10},{4,0},{6,2},{8,16},{10,18},{12,4},{14,6},{16,24},{18,... | collective-permute-start | bytes 835592 | tf_op jit(solution)/shard_map/ppermute | solution.py:113
  14.6 38.5 %all-to-all-start = ((bf16[16,32,512]{2,1,0:T(8,128)(2,1)}), bf16[16,32,512]{2,1,0:T(8,128)(2,1)S(1)}, u32[]{:S(2)}, u32[]{:S(2)}) async-start(bf16[16,32,512]{2,1,0:T(8,128)(2,1)} %bitcast.16), calls=%async_computation | async-start | bytes 1048576 | tf_op jit(solution)/shard_map/all_to_all | solution.py:411
  28.3 27.4 %collective-permute-start.3 = (bf16[2,512,512]{2,1,0:T(8,128)(2,1)}, bf16[2,512,512]{2,1,0:T(8,128)(2,1)}, u32[]{:S(2)}, u32[]{:S(2)}) collective-permute-start(bf16[2,512,512]{2,1,0:T(8,128)(2,1)} %collective-permute-done.2.refs_5_.refs_6_), channel_id=1, source_target_pairs={{0,2},{2,0},{4,6},{6,4},{8,10},{10,8},{12,14},{14,12},{16,18},{18,... | collective-permute-start | bytes 3145736 | tf_op jit(solution)/shard_map/ppermute | solution.py:99
  29.6 9.7 %collective-permute-start.7 = (bf16[272,512]{1,0:T(8,128)(2,1)}, bf16[272,512]{1,0:T(8,128)(2,1)}, u32[]{:S(2)}, u32[]{:S(2)}) collective-permute-start(bf16[272,512]{1,0:T(8,128)(2,1)} %collective-permute-done.5.refs_9_), channel_id=1, source_target_pairs={{0,4},{2,6},{4,12},{6,14},{8,0},{10,2},{12,20},{14,22},{16,8},{18,... | collective-permute-start | bytes 835592 | tf_op jit(solution)/shard_map/ppermute | solution.py:113
  31.0 9.4 %collective-permute-start.11 = (bf16[272,512]{1,0:T(8,128)(2,1)}, bf16[272,512]{1,0:T(8,128)(2,1)S(1)}, u32[]{:S(2)}, u32[]{:S(2)}) collective-permute-start(bf16[272,512]{1,0:T(8,128)(2,1)} %collective-permute-done.4.refs_8_), channel_id=1, source_target_pairs={{0,2},{2,0},{4,6},{6,4},{8,10},{10,8},{12,14},{14,12},{16,18},{18,... | collective-permute-start | bytes 835592 | tf_op jit(solution)/shard_map/ppermute | solution.py:99
  31.8 10.0 %collective-permute-start.8 = (bf16[272,512]{1,0:T(8,128)(2,1)}, bf16[272,512]{1,0:T(8,128)(2,1)}, u32[]{:S(2)}, u32[]{:S(2)}) collective-permute-start(bf16[272,512]{1,0:T(8,128)(2,1)} %collective-permute-done.6.refs_10_), channel_id=1, source_target_pairs={{0,8},{2,10},{4,0},{6,2},{8,16},{10,18},{12,4},{14,6},{16,24},{18,... | collective-permute-start | bytes 835592 | tf_op jit(solution)/shard_map/ppermute | solution.py:113
  33.2 11.4 %collective-permute-start.12 = (bf16[272,512]{1,0:T(8,128)(2,1)}, bf16[272,512]{1,0:T(8,128)(2,1)}, u32[]{:S(2)}, u32[]{:S(2)}) collective-permute-start(bf16[272,512]{1,0:T(8,128)(2,1)} %collective-permute-done.5.refs_9_), channel_id=1, source_target_pairs={{0,2},{2,0},{4,6},{6,4},{8,10},{10,8},{12,14},{14,12},{16,18},{18,... | collective-permute-start | bytes 835592 | tf_op jit(solution)/shard_map/ppermute | solution.py:99
  39.3 12.5 %collective-permute-start.13 = (bf16[272,512]{1,0:T(8,128)(2,1)}, bf16[272,512]{1,0:T(8,128)(2,1)}, u32[]{:S(2)}, u32[]{:S(2)}) collective-permute-start(bf16[272,512]{1,0:T(8,128)(2,1)} %collective-permute-done.6.refs_10_), channel_id=1, source_target_pairs={{0,2},{2,0},{4,6},{6,4},{8,10},{10,8},{12,14},{14,12},{16,18},{18,... | collective-permute-start | bytes 835592 | tf_op jit(solution)/shard_map/ppermute | solution.py:99
  41.1 10.1 %collective-permute-start.9 = (bf16[272,512]{1,0:T(8,128)(2,1)}, bf16[272,512]{1,0:T(8,128)(2,1)}, u32[]{:S(2)}, u32[]{:S(2)}) collective-permute-start(bf16[272,512]{1,0:T(8,128)(2,1)} %collective-permute-done.7.refs_11_), channel_id=1, source_target_pairs={{0,4},{2,6},{4,12},{6,14},{8,0},{10,2},{12,20},{14,22},{16,8},{18,... | collective-permute-start | bytes 835592 | tf_op jit(solution)/shard_map/ppermute | solution.py:113
  41.9 10.7 %collective-permute-start.17 = (bf16[272,512]{1,0:T(8,128)(2,1)}, bf16[272,512]{1,0:T(8,128)(2,1)}, u32[]{:S(2)}, u32[]{:S(2)}) collective-permute-start(bf16[272,512]{1,0:T(8,128)(2,1)} %collective-permute-done.8.refs_12_), channel_id=1, source_target_pairs={{0,8},{2,10},{4,0},{6,2},{8,16},{10,18},{12,4},{14,6},{16,24},{18,... | collective-permute-start | bytes 835592 | tf_op jit(solution)/shard_map/ppermute | solution.py:113
  44.6 11.2 %collective-permute-start.14 = (bf16[272,512]{1,0:T(8,128)(2,1)}, bf16[272,512]{1,0:T(8,128)(2,1)}, u32[]{:S(2)}, u32[]{:S(2)}) collective-permute-start(bf16[272,512]{1,0:T(8,128)(2,1)} %collective-permute-done.7.refs_11_), channel_id=1, source_target_pairs={{0,2},{2,0},{4,6},{6,4},{8,10},{10,8},{12,14},{14,12},{16,18},{18,... | collective-permute-start | bytes 835592 | tf_op jit(solution)/shard_map/ppermute | solution.py:99
  52.5 10.0 %collective-permute-start.18 = (bf16[272,512]{1,0:T(8,128)(2,1)}, bf16[272,512]{1,0:T(8,128)(2,1)}, u32[]{:S(2)}, u32[]{:S(2)}) collective-permute-start(bf16[272,512]{1,0:T(8,128)(2,1)} %collective-permute-done.17.refs_8_.refs_39_), channel_id=1, source_target_pairs={{0,2},{2,0},{4,6},{6,4},{8,10},{10,8},{12,14},{14,12},{16,18},{18,... | collective-permute-start | bytes 835592 | tf_op jit(solution)/shard_map/ppermute | solution.py:99
  65.3 5.1 %collective-permute-start.34 = (bf16[8,32,256]{2,1,0:T(8,128)(2,1)S(1)}, bf16[8,32,256]{2,1,0:T(8,128)(2,1)S(1)}, u32[]{:S(2)}, u32[]{:S(2)}) collective-permute-start(bf16[8,32,256]{2,1,0:T(8,128)(2,1)S(1)} %get-tuple-element.14.refs_6_), channel_id=1, source_target_pairs={{0,1},{1,0},{2,3},{3,2},{4,5},{5,4},{6,7},{7,6},{8,9},{9,8},{10,11... | collective-permute-start | bytes 393224 | tf_op jit(solution)/shard_map/ppermute | solution.py:103
  65.6 6.3 %collective-permute-start.19 = (bf16[8,32,256]{2,1,0:T(8,128)(2,1)S(1)}, bf16[8,32,256]{2,1,0:T(8,128)(2,1)S(1)}, u32[]{:S(2)}, u32[]{:S(2)}) collective-permute-start(bf16[8,32,256]{2,1,0:T(8,128)(2,1)S(1)} %get-tuple-element.14.refs_6_), channel_id=1, source_target_pairs={{0,8},{2,10},{4,0},{6,2},{8,16},{10,18},{12,4},{14,6},{16,24},{18,... | collective-permute-start | bytes 393224 | tf_op jit(solution)/shard_map/ppermute | solution.py:113
  67.0 6.3 %collective-permute-start.20 = (bf16[8,32,256]{2,1,0:T(8,128)(2,1)S(1)}, bf16[8,32,256]{2,1,0:T(8,128)(2,1)S(1)}, u32[]{:S(2)}, u32[]{:S(2)}) collective-permute-start(bf16[8,32,256]{2,1,0:T(8,128)(2,1)S(1)} %get-tuple-element.14.refs_6_), channel_id=1, source_target_pairs={{0,4},{2,6},{4,12},{6,14},{8,0},{10,2},{12,20},{14,22},{16,8},{18,... | collective-permute-start | bytes 393224 | tf_op jit(solution)/shard_map/ppermute | solution.py:113
  67.1 6.3 %collective-permute-start.26 = (bf16[8,32,256]{2,1,0:T(8,128)(2,1)S(1)}, bf16[8,32,256]{2,1,0:T(8,128)(2,1)S(1)}, u32[]{:S(2)}, u32[]{:S(2)}) collective-permute-start(bf16[8,32,256]{2,1,0:T(8,128)(2,1)S(1)} %get-tuple-element.14.refs_6_), channel_id=1, source_target_pairs={{0,2},{2,0},{4,6},{6,4},{8,10},{10,8},{12,14},{14,12},{16,18},{18,... | collective-permute-start | bytes 393224 | tf_op jit(solution)/shard_map/ppermute | solution.py:99
  71.9 5.8 %collective-permute-start.21 = (bf16[8,32,256]{2,1,0:T(8,128)(2,1)S(1)}, bf16[8,32,256]{2,1,0:T(8,128)(2,1)S(1)}, u32[]{:S(2)}, u32[]{:S(2)}) collective-permute-start(bf16[8,32,256]{2,1,0:T(8,128)(2,1)S(1)} %collective-permute-done.19.refs_7_), channel_id=1, source_target_pairs={{0,8},{2,10},{4,0},{6,2},{8,16},{10,18},{12,4},{14,6},{16,24},{18,... | collective-permute-start | bytes 393224 | tf_op jit(solution)/shard_map/ppermute | solution.py:113
  72.1 7.0 %collective-permute-start.36 = (bf16[8,32,256]{2,1,0:T(8,128)(2,1)S(1)}, bf16[8,32,256]{2,1,0:T(8,128)(2,1)S(1)}, u32[]{:S(2)}, u32[]{:S(2)}) collective-permute-start(bf16[8,32,256]{2,1,0:T(8,128)(2,1)S(1)} %collective-permute-done.34.refs_22_), channel_id=1, source_target_pairs={{0,4},{2,6},{4,12},{6,14},{8,0},{10,2},{12,20},{14,22},{16,8},{18,... | collective-permute-start | bytes 393224 | tf_op jit(solution)/shard_map/ppermute | solution.py:113
  73.3 7.3 %collective-permute-start.22 = (bf16[8,32,256]{2,1,0:T(8,128)(2,1)S(1)}, bf16[8,32,256]{2,1,0:T(8,128)(2,1)S(1)}, u32[]{:S(2)}, u32[]{:S(2)}) collective-permute-start(bf16[8,32,256]{2,1,0:T(8,128)(2,1)S(1)} %collective-permute-done.20.refs_8_), channel_id=1, source_target_pairs={{0,4},{2,6},{4,12},{6,14},{8,0},{10,2},{12,20},{14,22},{16,8},{18,... | collective-permute-start | bytes 393224 | tf_op jit(solution)/shard_map/ppermute | solution.py:113
  73.4 7.5 %collective-permute-start.27 = (bf16[8,32,256]{2,1,0:T(8,128)(2,1)S(1)}, bf16[8,32,256]{2,1,0:T(8,128)(2,1)S(1)}, u32[]{:S(2)}, u32[]{:S(2)}) collective-permute-start(bf16[8,32,256]{2,1,0:T(8,128)(2,1)S(1)} %collective-permute-done.19.refs_7_), channel_id=1, source_target_pairs={{0,2},{2,0},{4,6},{6,4},{8,10},{10,8},{12,14},{14,12},{16,18},{18,... | collective-permute-start | bytes 393224 | tf_op jit(solution)/shard_map/ppermute | solution.py:99
  75.3 6.7 %collective-permute-start.28 = (bf16[8,32,256]{2,1,0:T(8,128)(2,1)S(1)}, bf16[8,32,256]{2,1,0:T(8,128)(2,1)S(1)}, u32[]{:S(2)}, u32[]{:S(2)}) collective-permute-start(bf16[8,32,256]{2,1,0:T(8,128)(2,1)S(1)} %collective-permute-done.20.refs_8_), channel_id=1, source_target_pairs={{0,2},{2,0},{4,6},{6,4},{8,10},{10,8},{12,14},{14,12},{16,18},{18,... | collective-permute-start | bytes 393224 | tf_op jit(solution)/shard_map/ppermute | solution.py:99
  79.1 5.2 %collective-permute-start.37 = (bf16[8,32,256]{2,1,0:T(8,128)(2,1)S(1)}, bf16[8,32,256]{2,1,0:T(8,128)(2,1)S(1)}, u32[]{:S(2)}, u32[]{:S(2)}) collective-permute-start(bf16[8,32,256]{2,1,0:T(8,128)(2,1)S(1)} %collective-permute-done.35.refs_23_), channel_id=1, source_target_pairs={{0,8},{2,10},{4,0},{6,2},{8,16},{10,18},{12,4},{14,6},{16,24},{18,... | collective-permute-start | bytes 393224 | tf_op jit(solution)/shard_map/ppermute | solution.py:113
  80.6 6.1 %collective-permute-start.23 = (bf16[8,32,256]{2,1,0:T(8,128)(2,1)S(1)}, bf16[8,32,256]{2,1,0:T(8,128)(2,1)S(1)}, u32[]{:S(2)}, u32[]{:S(2)}) collective-permute-start(bf16[8,32,256]{2,1,0:T(8,128)(2,1)S(1)} %collective-permute-done.21.refs_9_), channel_id=1, source_target_pairs={{0,8},{2,10},{4,0},{6,2},{8,16},{10,18},{12,4},{14,6},{16,24},{18,... | collective-permute-start | bytes 393224 | tf_op jit(solution)/shard_map/ppermute | solution.py:113
  80.9 7.0 %collective-permute-start.38 = (bf16[8,32,256]{2,1,0:T(8,128)(2,1)S(1)}, bf16[8,32,256]{2,1,0:T(8,128)(2,1)S(1)}, u32[]{:S(2)}, u32[]{:S(2)}) collective-permute-start(bf16[8,32,256]{2,1,0:T(8,128)(2,1)S(1)} %collective-permute-done.36.refs_24_), channel_id=1, source_target_pairs={{0,4},{2,6},{4,12},{6,14},{8,0},{10,2},{12,20},{14,22},{16,8},{18,... | collective-permute-start | bytes 393224 | tf_op jit(solution)/shard_map/ppermute | solution.py:113
  82.1 6.0 %collective-permute-start.24 = (bf16[8,32,256]{2,1,0:T(8,128)(2,1)S(1)}, bf16[8,32,256]{2,1,0:T(8,128)(2,1)S(1)}, u32[]{:S(2)}, u32[]{:S(2)}) collective-permute-start(bf16[8,32,256]{2,1,0:T(8,128)(2,1)S(1)} %collective-permute-done.22.refs_10_), channel_id=1, source_target_pairs={{0,4},{2,6},{4,12},{6,14},{8,0},{10,2},{12,20},{14,22},{16,8},{18,... | collective-permute-start | bytes 393224 | tf_op jit(solution)/shard_map/ppermute | solution.py:113
  82.1 7.3 %collective-permute-start.29 = (bf16[8,32,256]{2,1,0:T(8,128)(2,1)S(1)}, bf16[8,32,256]{2,1,0:T(8,128)(2,1)S(1)}, u32[]{:S(2)}, u32[]{:S(2)}) collective-permute-start(bf16[8,32,256]{2,1,0:T(8,128)(2,1)S(1)} %collective-permute-done.21.refs_9_), channel_id=1, source_target_pairs={{0,2},{2,0},{4,6},{6,4},{8,10},{10,8},{12,14},{14,12},{16,18},{18,... | collective-permute-start | bytes 393224 | tf_op jit(solution)/shard_map/ppermute | solution.py:99
  84.4 5.5 %collective-permute-start.30 = (bf16[8,32,256]{2,1,0:T(8,128)(2,1)S(1)}, bf16[8,32,256]{2,1,0:T(8,128)(2,1)S(1)}, u32[]{:S(2)}, u32[]{:S(2)}) collective-permute-start(bf16[8,32,256]{2,1,0:T(8,128)(2,1)S(1)} %collective-permute-done.22.refs_10_), channel_id=1, source_target_pairs={{0,2},{2,0},{4,6},{6,4},{8,10},{10,8},{12,14},{14,12},{16,18},{18,... | collective-permute-start | bytes 393224 | tf_op jit(solution)/shard_map/ppermute | solution.py:99
  89.4 6.0 %collective-permute-start.25 = (bf16[8,32,256]{2,1,0:T(8,128)(2,1)S(1)}, bf16[8,32,256]{2,1,0:T(8,128)(2,1)S(1)}, u32[]{:S(2)}, u32[]{:S(2)}) collective-permute-start(bf16[8,32,256]{2,1,0:T(8,128)(2,1)S(1)} %collective-permute-done.23.refs_11_), channel_id=1, source_target_pairs={{0,8},{2,10},{4,0},{6,2},{8,16},{10,18},{12,4},{14,6},{16,24},{18,... | collective-permute-start | bytes 393224 | tf_op jit(solution)/shard_map/ppermute | solution.py:113
  89.9 6.9 %collective-permute-start.40 = (bf16[8,32,256]{2,1,0:T(8,128)(2,1)S(1)}, bf16[8,32,256]{2,1,0:T(8,128)(2,1)S(1)}, u32[]{:S(2)}, u32[]{:S(2)}) collective-permute-start(bf16[8,32,256]{2,1,0:T(8,128)(2,1)S(1)} %collective-permute-done.38.refs_26_), channel_id=1, source_target_pairs={{0,4},{2,6},{4,12},{6,14},{8,0},{10,2},{12,20},{14,22},{16,8},{18,... | collective-permute-start | bytes 393224 | tf_op jit(solution)/shard_map/ppermute | solution.py:113
  90.9 7.3 %collective-permute-start.31 = (bf16[8,32,256]{2,1,0:T(8,128)(2,1)S(1)}, bf16[8,32,256]{2,1,0:T(8,128)(2,1)S(1)}, u32[]{:S(2)}, u32[]{:S(2)}) collective-permute-start(bf16[8,32,256]{2,1,0:T(8,128)(2,1)S(1)} %collective-permute-done.23.refs_11_), channel_id=1, source_target_pairs={{0,2},{2,0},{4,6},{6,4},{8,10},{10,8},{12,14},{14,12},{16,18},{18,... | collective-permute-start | bytes 393224 | tf_op jit(solution)/shard_map/ppermute | solution.py:99
  92.2 6.2 %collective-permute-start.32 = (bf16[8,32,256]{2,1,0:T(8,128)(2,1)S(1)}, bf16[8,32,256]{2,1,0:T(8,128)(2,1)S(1)}, u32[]{:S(2)}, u32[]{:S(2)}) collective-permute-start(bf16[8,32,256]{2,1,0:T(8,128)(2,1)S(1)} %collective-permute-done.24.refs_12_), channel_id=1, source_target_pairs={{0,2},{2,0},{4,6},{6,4},{8,10},{10,8},{12,14},{14,12},{16,18},{18,... | collective-permute-start | bytes 393224 | tf_op jit(solution)/shard_map/ppermute | solution.py:99
  92.3 8.5 %collective-permute-start.45 = (bf16[8,32,256]{2,1,0:T(8,128)(2,1)S(1)}, bf16[8,32,256]{2,1,0:T(8,128)(2,1)S(1)}, u32[]{:S(2)}, u32[]{:S(2)}) collective-permute-start(bf16[8,32,256]{2,1,0:T(8,128)(2,1)S(1)} %collective-permute-done.37.refs_25_), channel_id=1, source_target_pairs={{0,2},{2,0},{4,6},{6,4},{8,10},{10,8},{12,14},{14,12},{16,18},{18,... | collective-permute-start | bytes 393224 | tf_op jit(solution)/shard_map/ppermute | solution.py:99
  95.4 5.5 %collective-permute-start.46 = (bf16[8,32,256]{2,1,0:T(8,128)(2,1)S(1)}, bf16[8,32,256]{2,1,0:T(8,128)(2,1)S(1)}, u32[]{:S(2)}, u32[]{:S(2)}) collective-permute-start(bf16[8,32,256]{2,1,0:T(8,128)(2,1)S(1)} %collective-permute-done.38.refs_26_), channel_id=1, source_target_pairs={{0,2},{2,0},{4,6},{6,4},{8,10},{10,8},{12,14},{14,12},{16,18},{18,... | collective-permute-start | bytes 393224 | tf_op jit(solution)/shard_map/ppermute | solution.py:99
  98.4 14.7 %collective-permute-start = (bf16[512,512]{1,0:T(8,128)(2,1)S(1)}, bf16[512,512]{1,0:T(8,128)(2,1)S(1)}, u32[]{:S(2)}, u32[]{:S(2)}) collective-permute-start(bf16[512,512]{1,0:T(8,128)(2,1)S(1)} %bitcast.17), channel_id=1, source_target_pairs={{2,4},{6,8},{10,12},{14,16},{18,20},{22,24},{26,28},{4,2},{8,6},{1... | collective-permute-start | bytes 1572872 | tf_op jit(solution)/shard_map/ppermute | solution.py:448
  102.7 14.2 %collective-permute-start.1 = (bf16[512,512]{1,0:T(8,128)(2,1)S(1)}, bf16[512,512]{1,0:T(8,128)(2,1)S(1)}, u32[]{:S(2)}, u32[]{:S(2)}) collective-permute-start(bf16[512,512]{1,0:T(8,128)(2,1)S(1)} %bitcast.18), channel_id=1, source_target_pairs={{0,2},{2,0},{4,6},{6,4},{8,10},{10,8},{12,14},{14,12},{16,18},{18,... | collective-permute-start | bytes 1572872 | tf_op jit(solution)/shard_map/ppermute | solution.py:99
  115.1 5.3 %collective-permute-start.66 = (bf16[176,256]{1,0:T(8,128)(2,1)S(1)}, bf16[176,256]{1,0:T(8,128)(2,1)S(1)}, u32[]{:S(2)}, u32[]{:S(2)}) collective-permute-start(bf16[176,256]{1,0:T(8,128)(2,1)S(1)} %collective-permute-done.65.refs_22_), channel_id=1, source_target_pairs={{0,8},{2,10},{4,0},{6,2},{8,16},{10,18},{12,4},{14,6},{16,24},{18,... | collective-permute-start | bytes 270344 | tf_op jit(solution)/shard_map/ppermute | solution.py:113
  116.9 5.5 %collective-permute-start.67 = (bf16[176,256]{1,0:T(8,128)(2,1)S(1)}, bf16[176,256]{1,0:T(8,128)(2,1)S(1)}, u32[]{:S(2)}, u32[]{:S(2)}) collective-permute-start(bf16[176,256]{1,0:T(8,128)(2,1)S(1)} %collective-permute-done.65.refs_22_), channel_id=1, source_target_pairs={{0,4},{2,6},{4,12},{6,14},{8,0},{10,2},{12,20},{14,22},{16,8},{18,... | collective-permute-start | bytes 270344 | tf_op jit(solution)/shard_map/ppermute | solution.py:113
  117.9 5.5 %collective-permute-start.53 = (bf16[176,256]{1,0:T(8,128)(2,1)S(1)}, bf16[176,256]{1,0:T(8,128)(2,1)S(1)}, u32[]{:S(2)}, u32[]{:S(2)}) collective-permute-start(bf16[176,256]{1,0:T(8,128)(2,1)S(1)} %collective-permute-done.51.refs_8_), channel_id=1, source_target_pairs={{0,4},{2,6},{4,12},{6,14},{8,0},{10,2},{12,20},{14,22},{16,8},{18,... | collective-permute-start | bytes 270344 | tf_op jit(solution)/shard_map/ppermute | solution.py:113
  118.1 5.9 %collective-permute-start.58 = (bf16[176,256]{1,0:T(8,128)(2,1)S(1)}, bf16[176,256]{1,0:T(8,128)(2,1)S(1)}, u32[]{:S(2)}, u32[]{:S(2)}) collective-permute-start(bf16[176,256]{1,0:T(8,128)(2,1)S(1)} %collective-permute-done.50.refs_7_), channel_id=1, source_target_pairs={{0,2},{2,0},{4,6},{6,4},{8,10},{10,8},{12,14},{14,12},{16,18},{18,... | collective-permute-start | bytes 270344 | tf_op jit(solution)/shard_map/ppermute | solution.py:99
  123.9 5.5 %collective-permute-start.69 = (bf16[176,256]{1,0:T(8,128)(2,1)S(1)}, bf16[176,256]{1,0:T(8,128)(2,1)S(1)}, u32[]{:S(2)}, u32[]{:S(2)}) collective-permute-start(bf16[176,256]{1,0:T(8,128)(2,1)S(1)} %collective-permute-done.67.refs_24_), channel_id=1, source_target_pairs={{0,4},{2,6},{4,12},{6,14},{8,0},{10,2},{12,20},{14,22},{16,8},{18,... | collective-permute-start | bytes 270344 | tf_op jit(solution)/shard_map/ppermute | solution.py:113
  124.9 5.1 %collective-permute-start.55 = (bf16[176,256]{1,0:T(8,128)(2,1)S(1)}, bf16[176,256]{1,0:T(8,128)(2,1)S(1)}, u32[]{:S(2)}, u32[]{:S(2)}) collective-permute-start(bf16[176,256]{1,0:T(8,128)(2,1)S(1)} %collective-permute-done.53.refs_10_), channel_id=1, source_target_pairs={{0,4},{2,6},{4,12},{6,14},{8,0},{10,2},{12,20},{14,22},{16,8},{18,... | collective-permute-start | bytes 270344 | tf_op jit(solution)/shard_map/ppermute | solution.py:113
  125.4 5.5 %collective-permute-start.60 = (bf16[176,256]{1,0:T(8,128)(2,1)S(1)}, bf16[176,256]{1,0:T(8,128)(2,1)S(1)}, u32[]{:S(2)}, u32[]{:S(2)}) collective-permute-start(bf16[176,256]{1,0:T(8,128)(2,1)S(1)} %collective-permute-done.52.refs_9_), channel_id=1, source_target_pairs={{0,2},{2,0},{4,6},{6,4},{8,10},{10,8},{12,14},{14,12},{16,18},{18,... | collective-permute-start | bytes 270344 | tf_op jit(solution)/shard_map/ppermute | solution.py:99
  130.9 5.1 %collective-permute-start.56 = (bf16[176,256]{1,0:T(8,128)(2,1)S(1)}, bf16[176,256]{1,0:T(8,128)(2,1)S(1)}, u32[]{:S(2)}, u32[]{:S(2)}) collective-permute-start(bf16[176,256]{1,0:T(8,128)(2,1)S(1)} %collective-permute-done.54.refs_11_), channel_id=1, source_target_pairs={{0,8},{2,10},{4,0},{6,2},{8,16},{10,18},{12,4},{14,6},{16,24},{18,... | collective-permute-start | bytes 270344 | tf_op jit(solution)/shard_map/ppermute | solution.py:113
  131.5 5.4 %collective-permute-start.71 = (bf16[176,256]{1,0:T(8,128)(2,1)S(1)}, bf16[176,256]{1,0:T(8,128)(2,1)S(1)}, u32[]{:S(2)}, u32[]{:S(2)}) collective-permute-start(bf16[176,256]{1,0:T(8,128)(2,1)S(1)} %collective-permute-done.69.refs_26_), channel_id=1, source_target_pairs={{0,4},{2,6},{4,12},{6,14},{8,0},{10,2},{12,20},{14,22},{16,8},{18,... | collective-permute-start | bytes 270344 | tf_op jit(solution)/shard_map/ppermute | solution.py:113
  132.3 5.8 %collective-permute-start.62 = (bf16[176,256]{1,0:T(8,128)(2,1)S(1)}, bf16[176,256]{1,0:T(8,128)(2,1)S(1)}, u32[]{:S(2)}, u32[]{:S(2)}) collective-permute-start(bf16[176,256]{1,0:T(8,128)(2,1)S(1)} %collective-permute-done.54.refs_11_), channel_id=1, source_target_pairs={{0,2},{2,0},{4,6},{6,4},{8,10},{10,8},{12,14},{14,12},{16,18},{18,... | collective-permute-start | bytes 270344 | tf_op jit(solution)/shard_map/ppermute | solution.py:99
  (44 other events, 371.5 us)

commit v4 on v3

--- a/solution.py
+++ b/solution.py
@@ -174,9 +174,12 @@
     return product.reshape(inner_shape[0], inner_shape[2], psi.shape[1])
 
 
-def own_kernel(scal_ref, sizes_ref, left_ref, wave_ref, out_ref, waves, sems):
+def own_kernel(scal_ref, sizes_ref, mine_ref, other_ref, wave_ref, out_ref, left_ref, waves, sems):
     local = wave_ref.shape[0]
     copies = copy_in([(wave_ref.at[i], waves.at[i]) for i in range(local)], sems)
+    sec, cols = scal_ref[2], mine_ref.shape[1]
+    left_ref[:, pl.ds(pl.multiple_of(sec * cols, cols), cols)] = mine_ref[...]
+    left_ref[:, pl.ds(pl.multiple_of((1 - sec) * cols, cols), cols)] = other_ref[...]
     for i in range(local):
         copies[i].wait()
         psi = cut_psi(waves[i], sizes_ref[scal_ref[2] * local + i])
@@ -207,16 +210,17 @@
 
 
 def early_kernel(early, late, *refs):
-    scal_ref, table_ref, sizes_ref, left_ref, own_ref, near_ref, far_ref = refs[:7]
+    scal_ref, table_ref, sizes_ref, left_ref, own_ref = refs[:5]
+    local = own_ref.shape[1]
+    half = local // 2
+    sources = refs[5:7]
     pieces = refs[7 : 7 + len(early)]
     acc_ref, rest_ref, right, inner, waves, wsems, rsems, isem = refs[7 + len(early) :]
     core, sec = scal_ref[1], scal_ref[2]
     cols = acc_ref.shape[1]
-    local = own_ref.shape[1]
-    half = local // 2
-    sources = [(near_ref.at[i], waves.at[i]) for i in range(half)]
-    sources += [(far_ref.at[i], waves.at[half + i]) for i in range(half)]
-    wave_copies = copy_in(sources, wsems)
+    wave_copies = copy_in(
+        [(ref.at[i], waves.at[c * half + i]) for c, ref in enumerate(sources) for i in range(half)], wsems
+    )
     copies = copy_in([(own_ref, inner.at[:, pl.ds(sec * local, local)])], isem)
     copies += copy_in([(piece, right.at[i]) for i, piece in enumerate(pieces)], rsems)
     foreign = (1 - sec) * local
@@ -235,23 +239,20 @@
 
 
 def late_kernel(*refs):
-    scal_ref, sizes_ref, factor_ref, acc_ref, rest_ref, own_ref, near_ref, far_ref = refs[:8]
+    scal_ref, sizes_ref, factor_ref, acc_ref, rest_ref, own_ref = refs[:6]
+    local = own_ref.shape[0]
+    others = refs[6:8]
     pieces = refs[8:10]
     out_ref, send_ref, right, start, rsems, ssems = refs[10:]
     o, core, sec = scal_ref[0], scal_ref[1], scal_ref[2]
-    local = own_ref.shape[0]
     _, rows, cols = out_ref.shape
     here = (slice(None), pl.ds(o * rows, rows), pl.ds(sec * cols, cols))
     foreign, half = (1 - sec) * local, local // 2
     copies = copy_in([(piece, right.at[c]) for c, piece in enumerate(pieces)], rsems)
-    copies += copy_in(
-        [
-            (own_ref.at[here], start.at[pl.ds(sec * local, local)]),
-            (near_ref.at[here], start.at[pl.ds(foreign + core * half, half)]),
-            (far_ref.at[here], start.at[pl.ds(foreign + (1 - core) * half, half)]),
-        ],
-        ssems,
-    )
+    moves = [(own_ref.at[here], start.at[pl.ds(sec * local, local)])]
+    for c, ref in enumerate(others):
+        moves.append((ref.at[here], start.at[pl.ds(foreign + lax.rem((core + c) * half, local), half)]))
+    copies += copy_in(moves, ssems)
     wait_all(copies)
     acc = acc_ref[...] + second_stage([rest_ref.at[c] for c in range(2)], right, cols)
     for s in range(out_ref.shape[0]):
@@ -408,16 +409,16 @@
         ]
     )
     right_pieces = ring_gather(right_cols, n)
-    left_rows = lax.all_to_all(left_ops[0], "ops", 0, 0, tiled=True)
-    part = lax.dynamic_slice_in_dim(wavefunction, core * (local // 2), local // 2, 0)
-    near = swap_sec(part)
+    near = swap_sec(lax.dynamic_slice_in_dim(wavefunction, core * (local // 2), local // 2, 0))
     far = swap_core(near, n)
-
-    inner = kernel_call(
-        own_kernel, shape((n, local, rows, width), bf16), "ssva",
+    left_mine = lax.all_to_all(lax.dynamic_slice_in_dim(left_ops[0], sec * cols, cols, 1), "ops", 0, 0, tiled=True)
+    left_other = swap_sec(left_mine)
+
+    inner, left_rows = kernel_call(
+        own_kernel, (shape((n, local, rows, width), bf16), shape((width, width), bf16)), "ssvva",
         [pltpu.VMEM((local, width, width), bf16), dma((local,))],
         10, sectors * width**3, psi_bytes,
-    )(scal, sector_sizes, left_rows, wavefunction)
+    )(scal, sector_sizes, left_mine, left_other, wavefunction)
     acc, rest, right_early = kernel_call(
         functools.partial(early_kernel, early, late),
         (

time: 146 us -> 147 us (level)
  starting transfers between devices: 83 us -> 88.5 us
  waiting for transfers between devices: 32.9 us -> 28.2 us
    ppermute x35, waiting for transfers between devices: 20.1 us -> 13.6 us  [along_ring(): return lax.ppermute(x, 'ops', perm)]
    ppermute x42, starting transfers between devices: 41.9 us -> 47.5 us  [swap_core(): return lax.ppermute(x, 'ops', [(o, o ^ 1) for o in range(n)])]
    ppermute x3 -> x4, waiting for transfers between devices: 10.1 us -> 12.3 us  [swap_sec(): return lax.ppermute(x, 'sec', [(0, 1), (1, 0)])]
    ppermute x35, starting transfers between devices: 29.1 us -> 27.3 us  [along_ring(): return lax.ppermute(x, 'ops', perm)]
    ppermute x3 -> x4, starting transfers between devices: 2.75 us -> 3.98 us  [swap_sec(): return lax.ppermute(x, 'sec', [(0, 1), (1, 0)])]
  transfers between devices with their start and end apart: 82 -> 83, of which waited for: 12 -> 12; matrix products, arithmetic and copies ran while one was open for 1% -> 1% of each run, Pallas kernels for 12% -> 12%
where the time goes in v4:
time: 147 us; the launch traced here: 146 us
  starting transfers between devices  88.5 us (60%)
  waiting for transfers between devices  28.2 us (19%)
  Pallas kernels  23.2 us (16%)
  local copies, waits for them, and re-layouts  4.49 us (3%)
  between operations  1.73 us (1%)
    ppermute x42, starting transfers between devices, swap_core(): return lax.ppermute(x, 'ops', [(o, o ^ 1) for o in range(n)])  47.5 us
    ppermute x35, starting transfers between devices, along_ring(): return lax.ppermute(x, 'ops', perm)  27.3 us
    ppermute x35, waiting for transfers between devices, along_ring(): return lax.ppermute(x, 'ops', perm)  13.6 us
    ppermute x4, waiting for transfers between devices, swap_sec(): return lax.ppermute(x, 'sec', [(0, 1), (1, 0)])  12.3 us
    pallas_call x1, Pallas kernels, gather_form(): kernel_call(functools.partial(iter2_kernel, n_slots, early, late), (shape...  7.53 us
    all_to_all x1, starting transfers between devices, gather_form(): lax.all_to_all(lax.dynamic_slice_in_dim(left_ops[0], sec * cols, cols, 1)...  6.89 us
    pallas_call x1, Pallas kernels, gather_form(): kernel_call(functools.partial(early_kernel, early, late), (shape((sectors...  6.76 us
    ppermute x4, starting transfers between devices, swap_sec(): return lax.ppermute(x, 'sec', [(0, 1), (1, 0)])  3.98 us
  transfers between devices with their start and end apart: 83, of which 12 were waited for; matrix products, arithmetic and copies ran while one was open for 1% of the time, Pallas kernels for 12%

profile of v4, /device:TPU:1, one launch (start us, length us, event | category | flops | bytes accessed | tf_op | source)
XLA Modules:
  0.0 146.3 jit_solution(12581397441252233558)
XLA Ops:
  0.7 2.4 %constant_dynamic-slice_fusion = bf16[2,512,512]{2,1,0:T(8,128)(2,1)} fusion(bf16[4,512,512]{2,1,0:T(8,128)(2,1)} %refs_5_.1, s32[]{:T(128)S(6)} %select_n.12), kind=kLoop, calls=%fused_computation.1 | loop fusion | bytes 2097156 | tf_op jit(solution)/shard_map/dynamic_slice | solution.py:412
  3.1 2.1 %collective-permute-start.3 = (bf16[2,512,512]{2,1,0:T(8,128)(2,1)}, bf16[2,512,512]{2,1,0:T(8,128)(2,1)}, u32[]{:S(2)}, u32[]{:S(2)}) collective-permute-start(bf16[2,512,512]{2,1,0:T(8,128)(2,1)} %constant_dynamic-slice_fusion), channel_id=1, source_target_pairs={{0,1},{1,0},{2,3},{3,2},{4,5},{5,4},{6,7},{7,6},{8,9},{9,8},{10,11... | collective-permute-start | bytes 3145736 | tf_op jit(solution)/shard_map/ppermute | solution.py:103
  5.9 1.3 collective-permute-start.5
  7.4 1.5 %collective-permute-start.11 = (bf16[272,512]{1,0:T(8,128)(2,1)S(1)}, bf16[272,512]{1,0:T(8,128)(2,1)}, u32[]{:S(2)}, u32[]{:S(2)}) collective-permute-start(bf16[272,512]{1,0:T(8,128)(2,1)S(1)} %concatenate.3.refs_7_), channel_id=1, source_target_pairs={{0,2},{2,0},{4,6},{6,4},{8,10},{10,8},{12,14},{14,12},{16,18},{18,... | collective-permute-start | bytes 835592 | tf_op jit(solution)/shard_map/ppermute | solution.py:99
  8.9 4.4 %collective-permute-done.5.refs_8_ = bf16[272,512]{1,0:T(8,128)(2,1)} collective-permute-done((bf16[272,512]{1,0:T(8,128)(2,1)S(1)}, bf16[272,512]{1,0:T(8,128)(2,1)}, u32[]{:S(2)}, u32[]{:S(2)}) %collective-permute-start.5) | collective-permute-done | bytes 278560 | tf_op jit(solution)/shard_map/ppermute | solution.py:113
  13.3 1.3 collective-permute-start.7
  15.3 6.9 %all-to-all-start = ((bf16[16,32,256]{2,1,0:T(8,128)(2,1)}), bf16[16,32,256]{2,1,0:T(8,128)(2,1)}, u32[]{:S(2)}, u32[]{:S(2)}) async-start(bf16[16,32,256]{2,1,0:T(8,128)(2,1)} %bitcast.17), calls=%async_computation | async-start | bytes 524288 | tf_op jit(solution)/shard_map/all_to_all | solution.py:414
  22.2 6.1 %collective-permute-done.3.refs_5_.refs_6_ = bf16[2,512,512]{2,1,0:T(8,128)(2,1)} collective-permute-done((bf16[2,512,512]{2,1,0:T(8,128)(2,1)}, bf16[2,512,512]{2,1,0:T(8,128)(2,1)}, u32[]{:S(2)}, u32[]{:S(2)}) %collective-permute-start.3) | collective-permute-done | bytes 1048608 | tf_op jit(solution)/shard_map/ppermute | solution.py:103
  28.3 1.3 collective-permute-start.4
  29.6 1.4 collective-permute-start.8
  31.9 6.4 %collective-permute-done.8.refs_11_ = bf16[272,512]{1,0:T(8,128)(2,1)} collective-permute-done((bf16[272,512]{1,0:T(8,128)(2,1)}, bf16[272,512]{1,0:T(8,128)(2,1)}, u32[]{:S(2)}, u32[]{:S(2)}) %collective-permute-start.8) | collective-permute-done | bytes 278560 | tf_op jit(solution)/shard_map/ppermute | solution.py:113
  38.2 1.4 collective-permute-start.2
  40.7 1.2 collective-permute-start.10
  42.8 2.8 %collective-permute-done.2.other_ref = bf16[512,256]{1,0:T(8,128)(2,1)} collective-permute-done((bf16[512,256]{1,0:T(8,128)(2,1)}, bf16[512,256]{1,0:T(8,128)(2,1)}, u32[]{:S(2)}, u32[]{:S(2)}) %collective-permute-start.2) | collective-permute-done | bytes 262176 | tf_op jit(solution)/shard_map/ppermute | solution.py:103
  45.6 1.7 %collective-permute-start.15 = (bf16[272,512]{1,0:T(8,128)(2,1)}, bf16[272,512]{1,0:T(8,128)(2,1)S(1)}, u32[]{:S(2)}, u32[]{:S(2)}) collective-permute-start(bf16[272,512]{1,0:T(8,128)(2,1)} %collective-permute-done.8.refs_11_), channel_id=1, source_target_pairs={{0,2},{2,0},{4,6},{6,4},{8,10},{10,8},{12,14},{14,12},{16,18},{18,... | collective-permute-start | bytes 835592 | tf_op jit(solution)/shard_map/ppermute | solution.py:99
  47.3 1.9 %collective-permute-done.10.refs_13_ = bf16[272,512]{1,0:T(8,128)(2,1)} collective-permute-done((bf16[272,512]{1,0:T(8,128)(2,1)}, bf16[272,512]{1,0:T(8,128)(2,1)}, u32[]{:S(2)}, u32[]{:S(2)}) %collective-permute-start.10) | collective-permute-done | bytes 278560 | tf_op jit(solution)/shard_map/ppermute | solution.py:113
  51.4 3.1 %shard_map.95 = (bf16[16,4,32,512]{3,2,1,0:T(8,128)(2,1)S(1)}, bf16[512,512]{1,0:T(8,128)(2,1)S(1)}) custom-call(s32[3]{0:T(128)S(1)} %pad_add_fusion.scal_ref.refs_0_, s32[8]{0:T(128)S(1)} %copy-done.3, bf16[512,256]{1,0:T(8,128)(2,1)} %bitcast.7.mine_ref, bf16[512,256]{1,0:T(8,128)(2,1)} %collective-permute-done.2.other_ref, bf16[4,512,512]{2,1,0:T(8,128)(2,1)S(1)} %copy-done.1), custom_call_target="tpu_custom_call" | custom-call | flops 1073741824 | bytes 4194304 | tf_op jit(solution)/shard_map/pallas_call | solution.py:417
  54.6 6.8 %shard_map.96 = (f32[256,256]{1,0:T(8,128)S(1)}, bf16[2,8,32,512]{3,2,1,0:T(8,128)(2,1)S(1)}, bf16[14,272,512]{2,1,0:T(8,128)(2,1)S(1)}) custom-call(s32[3]{0:T(128)S(1)} %pad_add_fusion.scal_ref.refs_0_, s32[16]{0:T(128)S(1)} %fusion.refs_1_, s32[8]{0:T(128)S(1)} %copy-done.3, bf16[512,512]{1,0:T(8,128)(2,1)S(1)} %get-tuple-element.13.refs_3_.refs_4_, ...), custom_call_target="tpu_custom_call" | custom-call | flops 1073741824 | bytes 8388608 | tf_op jit(solution)/shard_map/pallas_call | solution.py:422
  61.4 2.6 %shard_map.97 = (f32[8,32,256]{2,1,0:T(8,128)S(1)}, bf16[8,32,256]{2,1,0:T(8,128)(2,1)S(1)}) custom-call(s32[3]{0:T(128)S(1)} %pad_add_fusion.scal_ref.refs_0_, s32[8]{0:T(128)S(1)} %copy-done.3, f32[1]{0:T(128)} %get-tuple-element.24.refs_2_, f32[256,256]{1,0:T(8,128)S(1)} %get-tuple-element.15.refs_3_, ...), custom_call_target="tpu_custom_call" | custom-call | flops 268435456 | bytes 1048576 | tf_op jit(solution)/shard_map/pallas_call | solution.py:439
  64.3 1.3 collective-permute-start.20
  66.6 2.5 %collective-permute-done.35.refs_22_ = bf16[8,32,256]{2,1,0:T(8,128)(2,1)S(1)} collective-permute-done((bf16[8,32,256]{2,1,0:T(8,128)(2,1)S(1)}, bf16[8,32,256]{2,1,0:T(8,128)(2,1)S(1)}, u32[]{:S(2)}, u32[]{:S(2)}) %collective-permute-start.35) | collective-permute-done | bytes 131104 | tf_op jit(solution)/shard_map/ppermute | solution.py:103
  69.1 1.3 collective-permute-start.36
  70.4 1.3 collective-permute-start.22
  72.0 2.0 %collective-permute-start.28 = (bf16[8,32,256]{2,1,0:T(8,128)(2,1)S(1)}, bf16[8,32,256]{2,1,0:T(8,128)(2,1)S(1)}, u32[]{:S(2)}, u32[]{:S(2)}) collective-permute-start(bf16[8,32,256]{2,1,0:T(8,128)(2,1)S(1)} %collective-permute-done.20.refs_7_), channel_id=1, source_target_pairs={{0,2},{2,0},{4,6},{6,4},{8,10},{10,8},{12,14},{14,12},{16,18},{18,... | collective-permute-start | bytes 393224 | tf_op jit(solution)/shard_map/ppermute | solution.py:99
  74.0 2.3 %collective-permute-start.29 = (bf16[8,32,256]{2,1,0:T(8,128)(2,1)S(1)}, bf16[8,32,256]{2,1,0:T(8,128)(2,1)S(1)}, u32[]{:S(2)}, u32[]{:S(2)}) collective-permute-start(bf16[8,32,256]{2,1,0:T(8,128)(2,1)S(1)} %collective-permute-done.21.refs_8_), channel_id=1, source_target_pairs={{0,2},{2,0},{4,6},{6,4},{8,10},{10,8},{12,14},{14,12},{16,18},{18,... | collective-permute-start | bytes 393224 | tf_op jit(solution)/shard_map/ppermute | solution.py:99
  76.3 1.5 %collective-permute-start.43 = (bf16[8,32,256]{2,1,0:T(8,128)(2,1)S(1)}, bf16[8,32,256]{2,1,0:T(8,128)(2,1)S(1)}, u32[]{:S(2)}, u32[]{:S(2)}) collective-permute-start(bf16[8,32,256]{2,1,0:T(8,128)(2,1)S(1)} %collective-permute-done.35.refs_22_), channel_id=1, source_target_pairs={{0,2},{2,0},{4,6},{6,4},{8,10},{10,8},{12,14},{14,12},{16,18},{18,... | collective-permute-start | bytes 393224 | tf_op jit(solution)/shard_map/ppermute | solution.py:99
  77.8 1.3 collective-permute-start.38
  79.1 1.3 collective-permute-start.24
  80.8 2.3 %collective-permute-start.30 = (bf16[8,32,256]{2,1,0:T(8,128)(2,1)S(1)}, bf16[8,32,256]{2,1,0:T(8,128)(2,1)S(1)}, u32[]{:S(2)}, u32[]{:S(2)}) collective-permute-start(bf16[8,32,256]{2,1,0:T(8,128)(2,1)S(1)} %collective-permute-done.22.refs_9_), channel_id=1, source_target_pairs={{0,2},{2,0},{4,6},{6,4},{8,10},{10,8},{12,14},{14,12},{16,18},{18,... | collective-permute-start | bytes 393224 | tf_op jit(solution)/shard_map/ppermute | solution.py:99
  83.1 2.0 %collective-permute-start.31 = (bf16[8,32,256]{2,1,0:T(8,128)(2,1)S(1)}, bf16[8,32,256]{2,1,0:T(8,128)(2,1)S(1)}, u32[]{:S(2)}, u32[]{:S(2)}) collective-permute-start(bf16[8,32,256]{2,1,0:T(8,128)(2,1)S(1)} %collective-permute-done.23.refs_10_), channel_id=1, source_target_pairs={{0,2},{2,0},{4,6},{6,4},{8,10},{10,8},{12,14},{14,12},{16,18},{18,... | collective-permute-start | bytes 393224 | tf_op jit(solution)/shard_map/ppermute | solution.py:99
  85.1 1.4 collective-permute-start.44
  86.5 1.2 collective-permute-start.45
  87.8 1.3 collective-permute-start.40
  90.5 2.2 %collective-permute-start.32 = (bf16[8,32,256]{2,1,0:T(8,128)(2,1)S(1)}, bf16[8,32,256]{2,1,0:T(8,128)(2,1)S(1)}, u32[]{:S(2)}, u32[]{:S(2)}) collective-permute-start(bf16[8,32,256]{2,1,0:T(8,128)(2,1)S(1)} %collective-permute-done.24.refs_11_), channel_id=1, source_target_pairs={{0,2},{2,0},{4,6},{6,4},{8,10},{10,8},{12,14},{14,12},{16,18},{18,... | collective-permute-start | bytes 393224 | tf_op jit(solution)/shard_map/ppermute | solution.py:99
  92.8 2.2 %collective-permute-start.46 = (bf16[8,32,256]{2,1,0:T(8,128)(2,1)S(1)}, bf16[8,32,256]{2,1,0:T(8,128)(2,1)S(1)}, u32[]{:S(2)}, u32[]{:S(2)}) collective-permute-start(bf16[8,32,256]{2,1,0:T(8,128)(2,1)S(1)} %collective-permute-done.38.refs_25_), channel_id=1, source_target_pairs={{0,2},{2,0},{4,6},{6,4},{8,10},{10,8},{12,14},{14,12},{16,18},{18,... | collective-permute-start | bytes 393224 | tf_op jit(solution)/shard_map/ppermute | solution.py:99
  95.1 1.4 collective-permute-start.47
  96.5 1.3 collective-permute-start.42
  98.0 2.9 %collective-permute-start = (bf16[512,512]{1,0:T(8,128)(2,1)S(1)}, bf16[512,512]{1,0:T(8,128)(2,1)S(1)}, u32[]{:S(2)}, u32[]{:S(2)}) collective-permute-start(bf16[512,512]{1,0:T(8,128)(2,1)S(1)} %bitcast.13), channel_id=1, source_target_pairs={{2,4},{6,8},{10,12},{14,16},{18,20},{22,24},{26,28},{4,2},{8,6},{1... | collective-permute-start | bytes 1572872 | tf_op jit(solution)/shard_map/ppermute | solution.py:449
  103.4 7.5 %shard_map.98 = (bf16[176,256]{1,0:T(8,128)(2,1)S(1)}, bf16[176,256]{1,0:T(8,128)(2,1)S(1)}) custom-call(s32[3]{0:T(128)S(1)} %pad_add_fusion.scal_ref.refs_0_, s32[16]{0:T(128)S(1)} %fusion.refs_1_, s32[8]{0:T(128)S(1)} %copy-done.3, f32[1]{0:T(128)} %get-tuple-element.25.refs_3_, bf16[512,512]{1,0:T(8,128)(2,1)S(1)} %get-tuple-element.13.refs_3_.refs_4_, ...), custom_call_target="tpu_custom_call" | custom-call | flops 3221225472 | bytes 8388608 | tf_op jit(solution)/shard_map/pallas_call | solution.py:453
  111.2 1.3 collective-permute-start.51
  114.8 1.3 collective-permute-start.67
  117.8 2.3 %collective-permute-start.59 = (bf16[176,256]{1,0:T(8,128)(2,1)S(1)}, bf16[176,256]{1,0:T(8,128)(2,1)S(1)}, u32[]{:S(2)}, u32[]{:S(2)}) collective-permute-start(bf16[176,256]{1,0:T(8,128)(2,1)S(1)} %collective-permute-done.51.refs_7_), channel_id=1, source_target_pairs={{0,2},{2,0},{4,6},{6,4},{8,10},{10,8},{12,14},{14,12},{16,18},{18,... | collective-permute-start | bytes 270344 | tf_op jit(solution)/shard_map/ppermute | solution.py:99
  125.1 2.6 %collective-permute-start.61 = (bf16[176,256]{1,0:T(8,128)(2,1)S(1)}, bf16[176,256]{1,0:T(8,128)(2,1)S(1)}, u32[]{:S(2)}, u32[]{:S(2)}) collective-permute-start(bf16[176,256]{1,0:T(8,128)(2,1)S(1)} %collective-permute-done.53.refs_9_), channel_id=1, source_target_pairs={{0,2},{2,0},{4,6},{6,4},{8,10},{10,8},{12,14},{14,12},{16,18},{18,... | collective-permute-start | bytes 270344 | tf_op jit(solution)/shard_map/ppermute | solution.py:99
  132.6 1.9 %collective-permute-start.63 = (bf16[176,256]{1,0:T(8,128)(2,1)S(1)}, bf16[176,256]{1,0:T(8,128)(2,1)S(1)}, u32[]{:S(2)}, u32[]{:S(2)}) collective-permute-start(bf16[176,256]{1,0:T(8,128)(2,1)S(1)} %collective-permute-done.55.refs_11_), channel_id=1, source_target_pairs={{0,2},{2,0},{4,6},{6,4},{8,10},{10,8},{12,14},{14,12},{16,18},{18,... | collective-permute-start | bytes 270344 | tf_op jit(solution)/shard_map/ppermute | solution.py:99
  134.6 1.9 %collective-permute-start.77 = (bf16[176,256]{1,0:T(8,128)(2,1)S(1)}, bf16[176,256]{1,0:T(8,128)(2,1)S(1)}, u32[]{:S(2)}, u32[]{:S(2)}) collective-permute-start(bf16[176,256]{1,0:T(8,128)(2,1)S(1)} %collective-permute-done.69.refs_25_), channel_id=1, source_target_pairs={{0,2},{2,0},{4,6},{6,4},{8,10},{10,8},{12,14},{14,12},{16,18},{18,... | collective-permute-start | bytes 270344 | tf_op jit(solution)/shard_map/ppermute | solution.py:99
  137.1 1.2 collective-permute-start.78
  139.8 2.1 %collective-permute-start.81 = (bf16[176,256]{1,0:T(8,128)(2,1)S(1)}, bf16[176,256]{1,0:T(8,128)(2,1)S(1)}, u32[]{:S(2)}, u32[]{:S(2)}) collective-permute-start(bf16[176,256]{1,0:T(8,128)(2,1)S(1)} %collective-permute-done.73.refs_29_), channel_id=1, source_target_pairs={{0,2},{2,0},{4,6},{6,4},{8,10},{10,8},{12,14},{14,12},{16,18},{18,... | collective-permute-start | bytes 270344 | tf_op jit(solution)/shard_map/ppermute | solution.py:99
  142.9 3.2 %shard_map.99 = (f32[4,512,512]{2,1,0:T(8,128)}, bf16[512,256]{1,0:T(8,128)(2,1)}) custom-call(s32[3]{0:T(128)S(1)} %pad_add_fusion.scal_ref.refs_0_, s32[16]{0:T(128)S(1)} %fusion.refs_1_, f32[3]{0:T(128)S(1)} %bitcast.16, bf16[512,512]{1,0:T(8,128)(2,1)S(1)} %bitcast.15, bf16[512,512]{1,0:T(8,128)(2,1)S(1)} %collective-permute-done.refs_4_, ...), custom_call_target="tpu_custom_call" | custom-call | flops 268435456 | bytes 6291456 | tf_op jit(solution)/shard_map/pallas_call | solution.py:469
  (143 shorter events, 29.5 us)
Async XLA Ops:
  3.1 25.2 %collective-permute-start.3 = (bf16[2,512,512]{2,1,0:T(8,128)(2,1)}, bf16[2,512,512]{2,1,0:T(8,128)(2,1)}, u32[]{:S(2)}, u32[]{:S(2)}) collective-permute-start(bf16[2,512,512]{2,1,0:T(8,128)(2,1)} %constant_dynamic-slice_fusion), channel_id=1, source_target_pairs={{0,1},{1,0},{2,3},{3,2},{4,5},{5,4},{6,7},{7,6},{8,9},{9,8},{10,11... | collective-permute-start | bytes 3145736 | tf_op jit(solution)/shard_map/ppermute | solution.py:103
  5.9 7.4 %collective-permute-start.5 = (bf16[272,512]{1,0:T(8,128)(2,1)S(1)}, bf16[272,512]{1,0:T(8,128)(2,1)}, u32[]{:S(2)}, u32[]{:S(2)}) collective-permute-start(bf16[272,512]{1,0:T(8,128)(2,1)S(1)} %concatenate.3.refs_7_), channel_id=1, source_target_pairs={{0,8},{2,10},{4,0},{6,2},{8,16},{10,18},{12,4},{14,6},{16,24},{18,... | collective-permute-start | bytes 835592 | tf_op jit(solution)/shard_map/ppermute | solution.py:113
  7.3 22.4 %collective-permute-start.6 = (bf16[272,512]{1,0:T(8,128)(2,1)S(1)}, bf16[272,512]{1,0:T(8,128)(2,1)}, u32[]{:S(2)}, u32[]{:S(2)}) collective-permute-start(bf16[272,512]{1,0:T(8,128)(2,1)S(1)} %concatenate.3.refs_7_), channel_id=1, source_target_pairs={{0,4},{2,6},{4,12},{6,14},{8,0},{10,2},{12,20},{14,22},{16,8},{18,... | collective-permute-start | bytes 835592 | tf_op jit(solution)/shard_map/ppermute | solution.py:113
  7.4 23.9 %collective-permute-start.11 = (bf16[272,512]{1,0:T(8,128)(2,1)S(1)}, bf16[272,512]{1,0:T(8,128)(2,1)}, u32[]{:S(2)}, u32[]{:S(2)}) collective-permute-start(bf16[272,512]{1,0:T(8,128)(2,1)S(1)} %concatenate.3.refs_7_), channel_id=1, source_target_pairs={{0,2},{2,0},{4,6},{6,4},{8,10},{10,8},{12,14},{14,12},{16,18},{18,... | collective-permute-start | bytes 835592 | tf_op jit(solution)/shard_map/ppermute | solution.py:99
  13.3 18.2 %collective-permute-start.7 = (bf16[272,512]{1,0:T(8,128)(2,1)}, bf16[272,512]{1,0:T(8,128)(2,1)}, u32[]{:S(2)}, u32[]{:S(2)}) collective-permute-start(bf16[272,512]{1,0:T(8,128)(2,1)} %collective-permute-done.5.refs_8_), channel_id=1, source_target_pairs={{0,8},{2,10},{4,0},{6,2},{8,16},{10,18},{12,4},{14,6},{16,24},{18,... | collective-permute-start | bytes 835592 | tf_op jit(solution)/shard_map/ppermute | solution.py:113
  15.3 16.5 %all-to-all-start = ((bf16[16,32,256]{2,1,0:T(8,128)(2,1)}), bf16[16,32,256]{2,1,0:T(8,128)(2,1)}, u32[]{:S(2)}, u32[]{:S(2)}) async-start(bf16[16,32,256]{2,1,0:T(8,128)(2,1)} %bitcast.17), calls=%async_computation | async-start | bytes 524288 | tf_op jit(solution)/shard_map/all_to_all | solution.py:414
  28.3 26.2 %collective-permute-start.4 = (bf16[2,512,512]{2,1,0:T(8,128)(2,1)}, bf16[2,512,512]{2,1,0:T(8,128)(2,1)}, u32[]{:S(2)}, u32[]{:S(2)}) collective-permute-start(bf16[2,512,512]{2,1,0:T(8,128)(2,1)} %collective-permute-done.3.refs_5_.refs_6_), channel_id=1, source_target_pairs={{0,2},{2,0},{4,6},{6,4},{8,10},{10,8},{12,14},{14,12},{16,18},{18,... | collective-permute-start | bytes 3145736 | tf_op jit(solution)/shard_map/ppermute | solution.py:99
  29.6 8.6 %collective-permute-start.8 = (bf16[272,512]{1,0:T(8,128)(2,1)}, bf16[272,512]{1,0:T(8,128)(2,1)}, u32[]{:S(2)}, u32[]{:S(2)}) collective-permute-start(bf16[272,512]{1,0:T(8,128)(2,1)} %collective-permute-done.6.refs_9_), channel_id=1, source_target_pairs={{0,4},{2,6},{4,12},{6,14},{8,0},{10,2},{12,20},{14,22},{16,8},{18,... | collective-permute-start | bytes 835592 | tf_op jit(solution)/shard_map/ppermute | solution.py:113
  31.0 8.6 %collective-permute-start.12 = (bf16[272,512]{1,0:T(8,128)(2,1)}, bf16[272,512]{1,0:T(8,128)(2,1)}, u32[]{:S(2)}, u32[]{:S(2)}) collective-permute-start(bf16[272,512]{1,0:T(8,128)(2,1)} %collective-permute-done.5.refs_8_), channel_id=1, source_target_pairs={{0,2},{2,0},{4,6},{6,4},{8,10},{10,8},{12,14},{14,12},{16,18},{18,... | collective-permute-start | bytes 835592 | tf_op jit(solution)/shard_map/ppermute | solution.py:99
  31.3 9.4 %collective-permute-start.13 = (bf16[272,512]{1,0:T(8,128)(2,1)}, bf16[272,512]{1,0:T(8,128)(2,1)}, u32[]{:S(2)}, u32[]{:S(2)}) collective-permute-start(bf16[272,512]{1,0:T(8,128)(2,1)} %collective-permute-done.6.refs_9_), channel_id=1, source_target_pairs={{0,2},{2,0},{4,6},{6,4},{8,10},{10,8},{12,14},{14,12},{16,18},{18,... | collective-permute-start | bytes 835592 | tf_op jit(solution)/shard_map/ppermute | solution.py:99
  31.6 10.4 %collective-permute-start.9 = (bf16[272,512]{1,0:T(8,128)(2,1)}, bf16[272,512]{1,0:T(8,128)(2,1)}, u32[]{:S(2)}, u32[]{:S(2)}) collective-permute-start(bf16[272,512]{1,0:T(8,128)(2,1)} %collective-permute-done.7.refs_10_), channel_id=1, source_target_pairs={{0,8},{2,10},{4,0},{6,2},{8,16},{10,18},{12,4},{14,6},{16,24},{18,... | collective-permute-start | bytes 835592 | tf_op jit(solution)/shard_map/ppermute | solution.py:113
  38.2 7.4 %collective-permute-start.2 = (bf16[512,256]{1,0:T(8,128)(2,1)}, bf16[512,256]{1,0:T(8,128)(2,1)}, u32[]{:S(2)}, u32[]{:S(2)}) collective-permute-start(bf16[512,256]{1,0:T(8,128)(2,1)} %bitcast.7.mine_ref), channel_id=1, source_target_pairs={{0,1},{1,0},{2,3},{3,2},{4,5},{5,4},{6,7},{7,6},{8,9},{9,8},{10,11... | collective-permute-start | bytes 786440 | tf_op jit(solution)/shard_map/ppermute | solution.py:103
  39.6 10.5 %collective-permute-start.14 = (bf16[272,512]{1,0:T(8,128)(2,1)}, bf16[272,512]{1,0:T(8,128)(2,1)}, u32[]{:S(2)}, u32[]{:S(2)}) collective-permute-start(bf16[272,512]{1,0:T(8,128)(2,1)} %collective-permute-done.7.refs_10_), channel_id=1, source_target_pairs={{0,2},{2,0},{4,6},{6,4},{8,10},{10,8},{12,14},{14,12},{16,18},{18,... | collective-permute-start | bytes 835592 | tf_op jit(solution)/shard_map/ppermute | solution.py:99
  40.7 8.5 %collective-permute-start.10 = (bf16[272,512]{1,0:T(8,128)(2,1)}, bf16[272,512]{1,0:T(8,128)(2,1)}, u32[]{:S(2)}, u32[]{:S(2)}) collective-permute-start(bf16[272,512]{1,0:T(8,128)(2,1)} %collective-permute-done.8.refs_11_), channel_id=1, source_target_pairs={{0,4},{2,6},{4,12},{6,14},{8,0},{10,2},{12,20},{14,22},{16,8},{18,... | collective-permute-start | bytes 835592 | tf_op jit(solution)/shard_map/ppermute | solution.py:113
  42.0 8.9 %collective-permute-start.18 = (bf16[272,512]{1,0:T(8,128)(2,1)}, bf16[272,512]{1,0:T(8,128)(2,1)}, u32[]{:S(2)}, u32[]{:S(2)}) collective-permute-start(bf16[272,512]{1,0:T(8,128)(2,1)} %collective-permute-done.9.refs_12_), channel_id=1, source_target_pairs={{0,8},{2,10},{4,0},{6,2},{8,16},{10,18},{12,4},{14,6},{16,24},{18,... | collective-permute-start | bytes 835592 | tf_op jit(solution)/shard_map/ppermute | solution.py:113
  45.6 8.9 %collective-permute-start.15 = (bf16[272,512]{1,0:T(8,128)(2,1)}, bf16[272,512]{1,0:T(8,128)(2,1)S(1)}, u32[]{:S(2)}, u32[]{:S(2)}) collective-permute-start(bf16[272,512]{1,0:T(8,128)(2,1)} %collective-permute-done.8.refs_11_), channel_id=1, source_target_pairs={{0,2},{2,0},{4,6},{6,4},{8,10},{10,8},{12,14},{14,12},{16,18},{18,... | collective-permute-start | bytes 835592 | tf_op jit(solution)/shard_map/ppermute | solution.py:99
  49.2 5.3 %collective-permute-start.16 = (bf16[272,512]{1,0:T(8,128)(2,1)}, bf16[272,512]{1,0:T(8,128)(2,1)S(1)}, u32[]{:S(2)}, u32[]{:S(2)}) collective-permute-start(bf16[272,512]{1,0:T(8,128)(2,1)} %collective-permute-done.9.refs_12_), channel_id=1, source_target_pairs={{0,2},{2,0},{4,6},{6,4},{8,10},{10,8},{12,14},{14,12},{16,18},{18,... | collective-permute-start | bytes 835592 | tf_op jit(solution)/shard_map/ppermute | solution.py:99
  50.8 10.5 %collective-permute-start.19 = (bf16[272,512]{1,0:T(8,128)(2,1)}, bf16[272,512]{1,0:T(8,128)(2,1)S(1)}, u32[]{:S(2)}, u32[]{:S(2)}) collective-permute-start(bf16[272,512]{1,0:T(8,128)(2,1)} %collective-permute-done.18.refs_8_.refs_39_), channel_id=1, source_target_pairs={{0,2},{2,0},{4,6},{6,4},{8,10},{10,8},{12,14},{14,12},{16,18},{18,... | collective-permute-start | bytes 835592 | tf_op jit(solution)/shard_map/ppermute | solution.py:99
  64.3 6.1 %collective-permute-start.20 = (bf16[8,32,256]{2,1,0:T(8,128)(2,1)S(1)}, bf16[8,32,256]{2,1,0:T(8,128)(2,1)S(1)}, u32[]{:S(2)}, u32[]{:S(2)}) collective-permute-start(bf16[8,32,256]{2,1,0:T(8,128)(2,1)S(1)} %get-tuple-element.18.refs_6_), channel_id=1, source_target_pairs={{0,8},{2,10},{4,0},{6,2},{8,16},{10,18},{12,4},{14,6},{16,24},{18,... | collective-permute-start | bytes 393224 | tf_op jit(solution)/shard_map/ppermute | solution.py:113
  65.6 6.3 %collective-permute-start.21 = (bf16[8,32,256]{2,1,0:T(8,128)(2,1)S(1)}, bf16[8,32,256]{2,1,0:T(8,128)(2,1)S(1)}, u32[]{:S(2)}, u32[]{:S(2)}) collective-permute-start(bf16[8,32,256]{2,1,0:T(8,128)(2,1)S(1)} %get-tuple-element.18.refs_6_), channel_id=1, source_target_pairs={{0,4},{2,6},{4,12},{6,14},{8,0},{10,2},{12,20},{14,22},{16,8},{18,... | collective-permute-start | bytes 393224 | tf_op jit(solution)/shard_map/ppermute | solution.py:113
  65.7 6.3 %collective-permute-start.27 = (bf16[8,32,256]{2,1,0:T(8,128)(2,1)S(1)}, bf16[8,32,256]{2,1,0:T(8,128)(2,1)S(1)}, u32[]{:S(2)}, u32[]{:S(2)}) collective-permute-start(bf16[8,32,256]{2,1,0:T(8,128)(2,1)S(1)} %get-tuple-element.18.refs_6_), channel_id=1, source_target_pairs={{0,2},{2,0},{4,6},{6,4},{8,10},{10,8},{12,14},{14,12},{16,18},{18,... | collective-permute-start | bytes 393224 | tf_op jit(solution)/shard_map/ppermute | solution.py:99
  70.4 5.9 %collective-permute-start.22 = (bf16[8,32,256]{2,1,0:T(8,128)(2,1)S(1)}, bf16[8,32,256]{2,1,0:T(8,128)(2,1)S(1)}, u32[]{:S(2)}, u32[]{:S(2)}) collective-permute-start(bf16[8,32,256]{2,1,0:T(8,128)(2,1)S(1)} %collective-permute-done.20.refs_7_), channel_id=1, source_target_pairs={{0,8},{2,10},{4,0},{6,2},{8,16},{10,18},{12,4},{14,6},{16,24},{18,... | collective-permute-start | bytes 393224 | tf_op jit(solution)/shard_map/ppermute | solution.py:113
  71.7 6.1 %collective-permute-start.37 = (bf16[8,32,256]{2,1,0:T(8,128)(2,1)S(1)}, bf16[8,32,256]{2,1,0:T(8,128)(2,1)S(1)}, u32[]{:S(2)}, u32[]{:S(2)}) collective-permute-start(bf16[8,32,256]{2,1,0:T(8,128)(2,1)S(1)} %collective-permute-done.35.refs_22_), channel_id=1, source_target_pairs={{0,4},{2,6},{4,12},{6,14},{8,0},{10,2},{12,20},{14,22},{16,8},{18,... | collective-permute-start | bytes 393224 | tf_op jit(solution)/shard_map/ppermute | solution.py:113
  71.9 7.3 %collective-permute-start.23 = (bf16[8,32,256]{2,1,0:T(8,128)(2,1)S(1)}, bf16[8,32,256]{2,1,0:T(8,128)(2,1)S(1)}, u32[]{:S(2)}, u32[]{:S(2)}) collective-permute-start(bf16[8,32,256]{2,1,0:T(8,128)(2,1)S(1)} %collective-permute-done.21.refs_8_), channel_id=1, source_target_pairs={{0,4},{2,6},{4,12},{6,14},{8,0},{10,2},{12,20},{14,22},{16,8},{18,... | collective-permute-start | bytes 393224 | tf_op jit(solution)/shard_map/ppermute | solution.py:113
  72.0 8.4 %collective-permute-start.28 = (bf16[8,32,256]{2,1,0:T(8,128)(2,1)S(1)}, bf16[8,32,256]{2,1,0:T(8,128)(2,1)S(1)}, u32[]{:S(2)}, u32[]{:S(2)}) collective-permute-start(bf16[8,32,256]{2,1,0:T(8,128)(2,1)S(1)} %collective-permute-done.20.refs_7_), channel_id=1, source_target_pairs={{0,2},{2,0},{4,6},{6,4},{8,10},{10,8},{12,14},{14,12},{16,18},{18,... | collective-permute-start | bytes 393224 | tf_op jit(solution)/shard_map/ppermute | solution.py:99
  74.0 6.6 %collective-permute-start.29 = (bf16[8,32,256]{2,1,0:T(8,128)(2,1)S(1)}, bf16[8,32,256]{2,1,0:T(8,128)(2,1)S(1)}, u32[]{:S(2)}, u32[]{:S(2)}) collective-permute-start(bf16[8,32,256]{2,1,0:T(8,128)(2,1)S(1)} %collective-permute-done.21.refs_8_), channel_id=1, source_target_pairs={{0,2},{2,0},{4,6},{6,4},{8,10},{10,8},{12,14},{14,12},{16,18},{18,... | collective-permute-start | bytes 393224 | tf_op jit(solution)/shard_map/ppermute | solution.py:99
  79.1 6.0 %collective-permute-start.24 = (bf16[8,32,256]{2,1,0:T(8,128)(2,1)S(1)}, bf16[8,32,256]{2,1,0:T(8,128)(2,1)S(1)}, u32[]{:S(2)}, u32[]{:S(2)}) collective-permute-start(bf16[8,32,256]{2,1,0:T(8,128)(2,1)S(1)} %collective-permute-done.22.refs_9_), channel_id=1, source_target_pairs={{0,8},{2,10},{4,0},{6,2},{8,16},{10,18},{12,4},{14,6},{16,24},{18,... | collective-permute-start | bytes 393224 | tf_op jit(solution)/shard_map/ppermute | solution.py:113
  80.4 6.1 %collective-permute-start.39 = (bf16[8,32,256]{2,1,0:T(8,128)(2,1)S(1)}, bf16[8,32,256]{2,1,0:T(8,128)(2,1)S(1)}, u32[]{:S(2)}, u32[]{:S(2)}) collective-permute-start(bf16[8,32,256]{2,1,0:T(8,128)(2,1)S(1)} %collective-permute-done.37.refs_24_), channel_id=1, source_target_pairs={{0,4},{2,6},{4,12},{6,14},{8,0},{10,2},{12,20},{14,22},{16,8},{18,... | collective-permute-start | bytes 393224 | tf_op jit(solution)/shard_map/ppermute | solution.py:113
  80.6 7.2 %collective-permute-start.25 = (bf16[8,32,256]{2,1,0:T(8,128)(2,1)S(1)}, bf16[8,32,256]{2,1,0:T(8,128)(2,1)S(1)}, u32[]{:S(2)}, u32[]{:S(2)}) collective-permute-start(bf16[8,32,256]{2,1,0:T(8,128)(2,1)S(1)} %collective-permute-done.23.refs_10_), channel_id=1, source_target_pairs={{0,4},{2,6},{4,12},{6,14},{8,0},{10,2},{12,20},{14,22},{16,8},{18,... | collective-permute-start | bytes 393224 | tf_op jit(solution)/shard_map/ppermute | solution.py:113
  80.8 8.3 %collective-permute-start.30 = (bf16[8,32,256]{2,1,0:T(8,128)(2,1)S(1)}, bf16[8,32,256]{2,1,0:T(8,128)(2,1)S(1)}, u32[]{:S(2)}, u32[]{:S(2)}) collective-permute-start(bf16[8,32,256]{2,1,0:T(8,128)(2,1)S(1)} %collective-permute-done.22.refs_9_), channel_id=1, source_target_pairs={{0,2},{2,0},{4,6},{6,4},{8,10},{10,8},{12,14},{14,12},{16,18},{18,... | collective-permute-start | bytes 393224 | tf_op jit(solution)/shard_map/ppermute | solution.py:99
  83.1 7.1 %collective-permute-start.31 = (bf16[8,32,256]{2,1,0:T(8,128)(2,1)S(1)}, bf16[8,32,256]{2,1,0:T(8,128)(2,1)S(1)}, u32[]{:S(2)}, u32[]{:S(2)}) collective-permute-start(bf16[8,32,256]{2,1,0:T(8,128)(2,1)S(1)} %collective-permute-done.23.refs_10_), channel_id=1, source_target_pairs={{0,2},{2,0},{4,6},{6,4},{8,10},{10,8},{12,14},{14,12},{16,18},{18,... | collective-permute-start | bytes 393224 | tf_op jit(solution)/shard_map/ppermute | solution.py:99
  85.1 5.4 %collective-permute-start.44 = (bf16[8,32,256]{2,1,0:T(8,128)(2,1)S(1)}, bf16[8,32,256]{2,1,0:T(8,128)(2,1)S(1)}, u32[]{:S(2)}, u32[]{:S(2)}) collective-permute-start(bf16[8,32,256]{2,1,0:T(8,128)(2,1)S(1)} %collective-permute-done.36.refs_23_), channel_id=1, source_target_pairs={{0,2},{2,0},{4,6},{6,4},{8,10},{10,8},{12,14},{14,12},{16,18},{18,... | collective-permute-start | bytes 393224 | tf_op jit(solution)/shard_map/ppermute | solution.py:99
  86.5 6.2 %collective-permute-start.45 = (bf16[8,32,256]{2,1,0:T(8,128)(2,1)S(1)}, bf16[8,32,256]{2,1,0:T(8,128)(2,1)S(1)}, u32[]{:S(2)}, u32[]{:S(2)}) collective-permute-start(bf16[8,32,256]{2,1,0:T(8,128)(2,1)S(1)} %collective-permute-done.37.refs_24_), channel_id=1, source_target_pairs={{0,2},{2,0},{4,6},{6,4},{8,10},{10,8},{12,14},{14,12},{16,18},{18,... | collective-permute-start | bytes 393224 | tf_op jit(solution)/shard_map/ppermute | solution.py:99
  89.0 6.0 %collective-permute-start.26 = (bf16[8,32,256]{2,1,0:T(8,128)(2,1)S(1)}, bf16[8,32,256]{2,1,0:T(8,128)(2,1)S(1)}, u32[]{:S(2)}, u32[]{:S(2)}) collective-permute-start(bf16[8,32,256]{2,1,0:T(8,128)(2,1)S(1)} %collective-permute-done.24.refs_11_), channel_id=1, source_target_pairs={{0,8},{2,10},{4,0},{6,2},{8,16},{10,18},{12,4},{14,6},{16,24},{18,... | collective-permute-start | bytes 393224 | tf_op jit(solution)/shard_map/ppermute | solution.py:113
  90.2 6.2 %collective-permute-start.41 = (bf16[8,32,256]{2,1,0:T(8,128)(2,1)S(1)}, bf16[8,32,256]{2,1,0:T(8,128)(2,1)S(1)}, u32[]{:S(2)}, u32[]{:S(2)}) collective-permute-start(bf16[8,32,256]{2,1,0:T(8,128)(2,1)S(1)} %collective-permute-done.39.refs_26_), channel_id=1, source_target_pairs={{0,4},{2,6},{4,12},{6,14},{8,0},{10,2},{12,20},{14,22},{16,8},{18,... | collective-permute-start | bytes 393224 | tf_op jit(solution)/shard_map/ppermute | solution.py:113
  90.5 7.3 %collective-permute-start.32 = (bf16[8,32,256]{2,1,0:T(8,128)(2,1)S(1)}, bf16[8,32,256]{2,1,0:T(8,128)(2,1)S(1)}, u32[]{:S(2)}, u32[]{:S(2)}) collective-permute-start(bf16[8,32,256]{2,1,0:T(8,128)(2,1)S(1)} %collective-permute-done.24.refs_11_), channel_id=1, source_target_pairs={{0,2},{2,0},{4,6},{6,4},{8,10},{10,8},{12,14},{14,12},{16,18},{18,... | collective-permute-start | bytes 393224 | tf_op jit(solution)/shard_map/ppermute | solution.py:99
  92.8 5.3 %collective-permute-start.33 = (bf16[8,32,256]{2,1,0:T(8,128)(2,1)S(1)}, bf16[8,32,256]{2,1,0:T(8,128)(2,1)S(1)}, u32[]{:S(2)}, u32[]{:S(2)}) collective-permute-start(bf16[8,32,256]{2,1,0:T(8,128)(2,1)S(1)} %collective-permute-done.25.refs_12_), channel_id=1, source_target_pairs={{0,2},{2,0},{4,6},{6,4},{8,10},{10,8},{12,14},{14,12},{16,18},{18,... | collective-permute-start | bytes 393224 | tf_op jit(solution)/shard_map/ppermute | solution.py:99
  92.8 8.1 %collective-permute-start.46 = (bf16[8,32,256]{2,1,0:T(8,128)(2,1)S(1)}, bf16[8,32,256]{2,1,0:T(8,128)(2,1)S(1)}, u32[]{:S(2)}, u32[]{:S(2)}) collective-permute-start(bf16[8,32,256]{2,1,0:T(8,128)(2,1)S(1)} %collective-permute-done.38.refs_25_), channel_id=1, source_target_pairs={{0,2},{2,0},{4,6},{6,4},{8,10},{10,8},{12,14},{14,12},{16,18},{18,... | collective-permute-start | bytes 393224 | tf_op jit(solution)/shard_map/ppermute | solution.py:99
  95.1 5.9 %collective-permute-start.47 = (bf16[8,32,256]{2,1,0:T(8,128)(2,1)S(1)}, bf16[8,32,256]{2,1,0:T(8,128)(2,1)S(1)}, u32[]{:S(2)}, u32[]{:S(2)}) collective-permute-start(bf16[8,32,256]{2,1,0:T(8,128)(2,1)S(1)} %collective-permute-done.39.refs_26_), channel_id=1, source_target_pairs={{0,2},{2,0},{4,6},{6,4},{8,10},{10,8},{12,14},{14,12},{16,18},{18,... | collective-permute-start | bytes 393224 | tf_op jit(solution)/shard_map/ppermute | solution.py:99
  98.0 14.6 %collective-permute-start = (bf16[512,512]{1,0:T(8,128)(2,1)S(1)}, bf16[512,512]{1,0:T(8,128)(2,1)S(1)}, u32[]{:S(2)}, u32[]{:S(2)}) collective-permute-start(bf16[512,512]{1,0:T(8,128)(2,1)S(1)} %bitcast.13), channel_id=1, source_target_pairs={{2,4},{6,8},{10,12},{14,16},{18,20},{22,24},{26,28},{4,2},{8,6},{1... | collective-permute-start | bytes 1572872 | tf_op jit(solution)/shard_map/ppermute | solution.py:449
  102.4 14.9 %collective-permute-start.1 = (bf16[512,512]{1,0:T(8,128)(2,1)S(1)}, bf16[512,512]{1,0:T(8,128)(2,1)S(1)}, u32[]{:S(2)}, u32[]{:S(2)}) collective-permute-start(bf16[512,512]{1,0:T(8,128)(2,1)S(1)} %bitcast.14), channel_id=1, source_target_pairs={{0,2},{2,0},{4,6},{6,4},{8,10},{10,8},{12,14},{14,12},{16,18},{18,... | collective-permute-start | bytes 1572872 | tf_op jit(solution)/shard_map/ppermute | solution.py:99
  117.6 5.8 %collective-permute-start.54 = (bf16[176,256]{1,0:T(8,128)(2,1)S(1)}, bf16[176,256]{1,0:T(8,128)(2,1)S(1)}, u32[]{:S(2)}, u32[]{:S(2)}) collective-permute-start(bf16[176,256]{1,0:T(8,128)(2,1)S(1)} %collective-permute-done.52.refs_8_), channel_id=1, source_target_pairs={{0,4},{2,6},{4,12},{6,14},{8,0},{10,2},{12,20},{14,22},{16,8},{18,... | collective-permute-start | bytes 270344 | tf_op jit(solution)/shard_map/ppermute | solution.py:113
  117.8 6.5 %collective-permute-start.59 = (bf16[176,256]{1,0:T(8,128)(2,1)S(1)}, bf16[176,256]{1,0:T(8,128)(2,1)S(1)}, u32[]{:S(2)}, u32[]{:S(2)}) collective-permute-start(bf16[176,256]{1,0:T(8,128)(2,1)S(1)} %collective-permute-done.51.refs_7_), channel_id=1, source_target_pairs={{0,2},{2,0},{4,6},{6,4},{8,10},{10,8},{12,14},{14,12},{16,18},{18,... | collective-permute-start | bytes 270344 | tf_op jit(solution)/shard_map/ppermute | solution.py:99
  122.1 5.6 %collective-permute-start.69 = (bf16[176,256]{1,0:T(8,128)(2,1)S(1)}, bf16[176,256]{1,0:T(8,128)(2,1)S(1)}, u32[]{:S(2)}, u32[]{:S(2)}) collective-permute-start(bf16[176,256]{1,0:T(8,128)(2,1)S(1)} %collective-permute-done.67.refs_23_), channel_id=1, source_target_pairs={{0,8},{2,10},{4,0},{6,2},{8,16},{10,18},{12,4},{14,6},{16,24},{18,... | collective-permute-start | bytes 270344 | tf_op jit(solution)/shard_map/ppermute | solution.py:113
  124.8 5.6 %collective-permute-start.56 = (bf16[176,256]{1,0:T(8,128)(2,1)S(1)}, bf16[176,256]{1,0:T(8,128)(2,1)S(1)}, u32[]{:S(2)}, u32[]{:S(2)}) collective-permute-start(bf16[176,256]{1,0:T(8,128)(2,1)S(1)} %collective-permute-done.54.refs_10_), channel_id=1, source_target_pairs={{0,4},{2,6},{4,12},{6,14},{8,0},{10,2},{12,20},{14,22},{16,8},{18,... | collective-permute-start | bytes 270344 | tf_op jit(solution)/shard_map/ppermute | solution.py:113
  125.1 6.0 %collective-permute-start.61 = (bf16[176,256]{1,0:T(8,128)(2,1)S(1)}, bf16[176,256]{1,0:T(8,128)(2,1)S(1)}, u32[]{:S(2)}, u32[]{:S(2)}) collective-permute-start(bf16[176,256]{1,0:T(8,128)(2,1)S(1)} %collective-permute-done.53.refs_9_), channel_id=1, source_target_pairs={{0,2},{2,0},{4,6},{6,4},{8,10},{10,8},{12,14},{14,12},{16,18},{18,... | collective-permute-start | bytes 270344 | tf_op jit(solution)/shard_map/ppermute | solution.py:99
  131.1 5.3 %collective-permute-start.57 = (bf16[176,256]{1,0:T(8,128)(2,1)S(1)}, bf16[176,256]{1,0:T(8,128)(2,1)S(1)}, u32[]{:S(2)}, u32[]{:S(2)}) collective-permute-start(bf16[176,256]{1,0:T(8,128)(2,1)S(1)} %collective-permute-done.55.refs_11_), channel_id=1, source_target_pairs={{0,8},{2,10},{4,0},{6,2},{8,16},{10,18},{12,4},{14,6},{16,24},{18,... | collective-permute-start | bytes 270344 | tf_op jit(solution)/shard_map/ppermute | solution.py:113
  132.6 5.8 %collective-permute-start.63 = (bf16[176,256]{1,0:T(8,128)(2,1)S(1)}, bf16[176,256]{1,0:T(8,128)(2,1)S(1)}, u32[]{:S(2)}, u32[]{:S(2)}) collective-permute-start(bf16[176,256]{1,0:T(8,128)(2,1)S(1)} %collective-permute-done.55.refs_11_), channel_id=1, source_target_pairs={{0,2},{2,0},{4,6},{6,4},{8,10},{10,8},{12,14},{14,12},{16,18},{18,... | collective-permute-start | bytes 270344 | tf_op jit(solution)/shard_map/ppermute | solution.py:99
  (41 other events, 350.9 us)

commit v5 on v4

--- a/solution.py
+++ b/solution.py
@@ -190,8 +190,8 @@
     total = None
     for i, inner in enumerate(terms):
         sectors, _, _ = inner.shape
-        shift = jnp.max(right[i, cols:, :128].astype(jnp.float32)).astype(jnp.int32)
-        rhs = right[i, :cols]
+        shift = jnp.max(right[i][cols:, :128].astype(jnp.float32)).astype(jnp.int32)
+        rhs = right[i][:cols]
         lhs = jnp.concatenate([inner[lax.rem(t - shift + sectors, sectors)] for t in range(sectors)], axis=0)
         product = lax.dot_general(
             lhs, rhs, (((1,), (1,)), ((), ())), preferred_element_type=jnp.float32
@@ -233,7 +233,8 @@
         inner[:, sector] = first_stage(left_ref, psi, inner.shape)
 
     wait_all(copies)
-    acc_ref[...] = second_stage([inner.at[table_ref[i]] for i in early], right, cols)
+    places = [right.at[at] for at in range(len(early))]
+    acc_ref[...] = second_stage([inner.at[table_ref[i]] for i in early], places, cols)
     for at, i in enumerate(late):
         rest_ref[at] = inner[table_ref[i]]
 
@@ -254,7 +255,7 @@
         moves.append((ref.at[here], start.at[pl.ds(foreign + lax.rem((core + c) * half, local), half)]))
     copies += copy_in(moves, ssems)
     wait_all(copies)
-    acc = acc_ref[...] + second_stage([rest_ref.at[c] for c in range(2)], right, cols)
+    acc = acc_ref[...] + second_stage([rest_ref.at[c] for c in range(2)], [right.at[c] for c in range(2)], cols)
     for s in range(out_ref.shape[0]):
         moved = step_rows(start[s].astype(jnp.float32), acc, sizes_ref, scal_ref, factor_ref[0], s)
         out_ref[s] = moved
@@ -283,20 +284,17 @@
         at = pl.ds(table_ref[i % n_slots] * rows, rows)
         pairs.append((piece, psi.at[sec if i < n_slots else 1 - sec, :, at]))
     psi_copies = copy_in(pairs, psems)
-    right_copies = copy_in(
-        [(right_pieces[0], right.at[pl.ds(0, len(early))])]
-        + [(right_pieces[1 + c], right.at[len(early) + c]) for c in range(2)],
-        rsems,
-    )
+    right_copies = copy_in([(right_pieces[1 + c], right.at[c]) for c in range(2)], rsems)
     wait_all(psi_copies)
 
-    @pl.loop(0, sectors, unroll=2)
+    @pl.loop(0, sectors, unroll=4)
     def _(s):
         for h in range(2):
             inner[:, s, :, h * cols : (h + 1) * cols] = first_stage(left_ref, psi[h, s], inner.shape)
 
     wait_all(right_copies)
-    acc = second_stage([inner.at[table_ref[i]] for i in early + late], right, cols)
+    places = [right_pieces[0].at[at] for at in range(len(early))] + [right.at[c] for c in range(2)]
+    acc = second_stage([inner.at[table_ref[i]] for i in early + late], places, cols)
     before = jnp.zeros((rows, cols), jnp.float32)
     after = jnp.zeros((rows, cols), jnp.float32)
     for s in range(sectors):
@@ -452,14 +450,14 @@
     message = (local + 1) * rows + 16
     keep, send = kernel_call(
         functools.partial(iter2_kernel, n_slots, early, late), (shape((message, cols), bf16),) * 2,
-        "ssssvv" + "a" * (2 * n_slots + 3),
+        "ssssvv" + "a" * (2 * n_slots) + "vaa",
         [
             pltpu.VMEM((2, sectors, width, cols), bf16),
             pltpu.VMEM((n, sectors, rows, width), bf16),
-            pltpu.VMEM((n, tall, width), bf16),
+            pltpu.VMEM((2, tall, width), bf16),
             pltpu.VMEM((sectors, rows, cols), bf16),
             dma((2 * n_slots,)),
-            dma((3,)),
+            dma((2,)),
         ],
         18, 3 * sectors * width**3, 2 * psi_bytes,
     )(scal, table, sector_sizes, factors[1:2], left_rows, psi_1, *psi_pieces, right_early, *[right_pieces[i] for i in late])

time: 147 us -> 146 us (level)
  transfers between devices with their start and end apart: 83 -> 83, of which waited for: 12 -> 13; matrix products, arithmetic and copies ran while one was open for 1% -> 1% of each run, Pallas kernels for 12% -> 11%
where the time goes in v5:
time: 146 us; the launch traced here: 145 us
  starting transfers between devices  87.8 us (60%)
  waiting for transfers between devices  28.9 us (20%)
  Pallas kernels  22.3 us (15%)
  local copies, waits for them, and re-layouts  4.49 us (3%)
  between operations  1.73 us (1%)
    ppermute x42, starting transfers between devices, swap_core(): return lax.ppermute(x, 'ops', [(o, o ^ 1) for o in range(n)])  46.3 us
    ppermute x35, starting transfers between devices, along_ring(): return lax.ppermute(x, 'ops', perm)  27.7 us
    ppermute x35, waiting for transfers between devices, along_ring(): return lax.ppermute(x, 'ops', perm)  13.6 us
    ppermute x4, waiting for transfers between devices, swap_sec(): return lax.ppermute(x, 'sec', [(0, 1), (1, 0)])  12.4 us
    all_to_all x1, starting transfers between devices, gather_form(): lax.all_to_all(lax.dynamic_slice_in_dim(left_ops[0], sec * cols, cols, 1)...  6.89 us
    pallas_call x1, Pallas kernels, gather_form(): kernel_call(functools.partial(early_kernel, early, late), (shape((sectors...  6.76 us
    pallas_call x1, Pallas kernels, gather_form(): kernel_call(functools.partial(iter2_kernel, n_slots, early, late), (shape...  6.59 us
    ppermute x4, starting transfers between devices, swap_sec(): return lax.ppermute(x, 'sec', [(0, 1), (1, 0)])  3.97 us
  transfers between devices with their start and end apart: 83, of which 13 were waited for; matrix products, arithmetic and copies ran while one was open for 1% of the time, Pallas kernels for 11%

profile of v5, /device:TPU:1, one launch (start us, length us, event | category | flops | bytes accessed | tf_op | source)
XLA Modules:
  0.0 145.3 jit_solution(381442986120904864)
XLA Ops:
  0.7 2.4 %constant_dynamic-slice_fusion = bf16[2,512,512]{2,1,0:T(8,128)(2,1)} fusion(bf16[4,512,512]{2,1,0:T(8,128)(2,1)} %refs_5_.1, s32[]{:T(128)S(6)} %select_n.12), kind=kLoop, calls=%fused_computation.1 | loop fusion | bytes 2097156 | tf_op jit(solution)/shard_map/dynamic_slice | solution.py:410
  3.1 2.1 %collective-permute-start.3 = (bf16[2,512,512]{2,1,0:T(8,128)(2,1)}, bf16[2,512,512]{2,1,0:T(8,128)(2,1)}, u32[]{:S(2)}, u32[]{:S(2)}) collective-permute-start(bf16[2,512,512]{2,1,0:T(8,128)(2,1)} %constant_dynamic-slice_fusion), channel_id=1, source_target_pairs={{0,1},{1,0},{2,3},{3,2},{4,5},{5,4},{6,7},{7,6},{8,9},{9,8},{10,11... | collective-permute-start | bytes 3145736 | tf_op jit(solution)/shard_map/ppermute | solution.py:103
  5.9 1.3 collective-permute-start.5
  7.4 1.5 %collective-permute-start.11 = (bf16[272,512]{1,0:T(8,128)(2,1)S(1)}, bf16[272,512]{1,0:T(8,128)(2,1)}, u32[]{:S(2)}, u32[]{:S(2)}) collective-permute-start(bf16[272,512]{1,0:T(8,128)(2,1)S(1)} %concatenate.3.refs_7_), channel_id=1, source_target_pairs={{0,2},{2,0},{4,6},{6,4},{8,10},{10,8},{12,14},{14,12},{16,18},{18,... | collective-permute-start | bytes 835592 | tf_op jit(solution)/shard_map/ppermute | solution.py:99
  8.9 4.4 %collective-permute-done.5.refs_8_ = bf16[272,512]{1,0:T(8,128)(2,1)} collective-permute-done((bf16[272,512]{1,0:T(8,128)(2,1)S(1)}, bf16[272,512]{1,0:T(8,128)(2,1)}, u32[]{:S(2)}, u32[]{:S(2)}) %collective-permute-start.5) | collective-permute-done | bytes 278560 | tf_op jit(solution)/shard_map/ppermute | solution.py:113
  13.3 1.3 collective-permute-start.7
  15.3 6.9 %all-to-all-start = ((bf16[16,32,256]{2,1,0:T(8,128)(2,1)}), bf16[16,32,256]{2,1,0:T(8,128)(2,1)}, u32[]{:S(2)}, u32[]{:S(2)}) async-start(bf16[16,32,256]{2,1,0:T(8,128)(2,1)} %bitcast.17), calls=%async_computation | async-start | bytes 524288 | tf_op jit(solution)/shard_map/all_to_all | solution.py:412
  22.2 6.1 %collective-permute-done.3.refs_5_.refs_6_ = bf16[2,512,512]{2,1,0:T(8,128)(2,1)} collective-permute-done((bf16[2,512,512]{2,1,0:T(8,128)(2,1)}, bf16[2,512,512]{2,1,0:T(8,128)(2,1)}, u32[]{:S(2)}, u32[]{:S(2)}) %collective-permute-start.3) | collective-permute-done | bytes 1048608 | tf_op jit(solution)/shard_map/ppermute | solution.py:103
  28.3 1.3 collective-permute-start.4
  29.6 1.4 collective-permute-start.8
  31.9 6.4 %collective-permute-done.8.refs_11_ = bf16[272,512]{1,0:T(8,128)(2,1)} collective-permute-done((bf16[272,512]{1,0:T(8,128)(2,1)}, bf16[272,512]{1,0:T(8,128)(2,1)}, u32[]{:S(2)}, u32[]{:S(2)}) %collective-permute-start.8) | collective-permute-done | bytes 278560 | tf_op jit(solution)/shard_map/ppermute | solution.py:113
  38.2 1.4 collective-permute-start.2
  40.7 1.2 collective-permute-start.10
  42.8 2.8 %collective-permute-done.2.other_ref = bf16[512,256]{1,0:T(8,128)(2,1)} collective-permute-done((bf16[512,256]{1,0:T(8,128)(2,1)}, bf16[512,256]{1,0:T(8,128)(2,1)}, u32[]{:S(2)}, u32[]{:S(2)}) %collective-permute-start.2) | collective-permute-done | bytes 262176 | tf_op jit(solution)/shard_map/ppermute | solution.py:103
  45.6 1.7 %collective-permute-start.15 = (bf16[272,512]{1,0:T(8,128)(2,1)}, bf16[272,512]{1,0:T(8,128)(2,1)S(1)}, u32[]{:S(2)}, u32[]{:S(2)}) collective-permute-start(bf16[272,512]{1,0:T(8,128)(2,1)} %collective-permute-done.8.refs_11_), channel_id=1, source_target_pairs={{0,2},{2,0},{4,6},{6,4},{8,10},{10,8},{12,14},{14,12},{16,18},{18,... | collective-permute-start | bytes 835592 | tf_op jit(solution)/shard_map/ppermute | solution.py:99
  47.3 1.9 %collective-permute-done.10.refs_13_ = bf16[272,512]{1,0:T(8,128)(2,1)} collective-permute-done((bf16[272,512]{1,0:T(8,128)(2,1)}, bf16[272,512]{1,0:T(8,128)(2,1)}, u32[]{:S(2)}, u32[]{:S(2)}) %collective-permute-start.10) | collective-permute-done | bytes 278560 | tf_op jit(solution)/shard_map/ppermute | solution.py:113
  51.4 3.1 %shard_map.95 = (bf16[16,4,32,512]{3,2,1,0:T(8,128)(2,1)S(1)}, bf16[512,512]{1,0:T(8,128)(2,1)S(1)}) custom-call(s32[3]{0:T(128)S(1)} %pad_add_fusion.scal_ref.refs_0_, s32[8]{0:T(128)S(1)} %copy-done.3, bf16[512,256]{1,0:T(8,128)(2,1)} %bitcast.7.mine_ref, bf16[512,256]{1,0:T(8,128)(2,1)} %collective-permute-done.2.other_ref, bf16[4,512,512]{2,1,0:T(8,128)(2,1)S(1)} %copy-done.1), custom_call_target="tpu_custom_call" | custom-call | flops 1073741824 | bytes 4194304 | tf_op jit(solution)/shard_map/pallas_call | solution.py:415
  54.6 6.8 %shard_map.96 = (f32[256,256]{1,0:T(8,128)S(1)}, bf16[2,8,32,512]{3,2,1,0:T(8,128)(2,1)S(1)}, bf16[14,272,512]{2,1,0:T(8,128)(2,1)S(1)}) custom-call(s32[3]{0:T(128)S(1)} %pad_add_fusion.scal_ref.refs_0_, s32[16]{0:T(128)S(1)} %fusion.refs_1_, s32[8]{0:T(128)S(1)} %copy-done.3, bf16[512,512]{1,0:T(8,128)(2,1)S(1)} %get-tuple-element.13.refs_3_.refs_4_, ...), custom_call_target="tpu_custom_call" | custom-call | flops 1073741824 | bytes 8388608 | tf_op jit(solution)/shard_map/pallas_call | solution.py:420
  61.4 2.6 %shard_map.97 = (f32[8,32,256]{2,1,0:T(8,128)S(1)}, bf16[8,32,256]{2,1,0:T(8,128)(2,1)S(1)}) custom-call(s32[3]{0:T(128)S(1)} %pad_add_fusion.scal_ref.refs_0_, s32[8]{0:T(128)S(1)} %copy-done.3, f32[1]{0:T(128)} %get-tuple-element.24.refs_2_, f32[256,256]{1,0:T(8,128)S(1)} %get-tuple-element.15.refs_3_, ...), custom_call_target="tpu_custom_call" | custom-call | flops 268435456 | bytes 1048576 | tf_op jit(solution)/shard_map/pallas_call | solution.py:437
  64.3 1.3 collective-permute-start.20
  66.6 2.5 %collective-permute-done.35.refs_22_ = bf16[8,32,256]{2,1,0:T(8,128)(2,1)S(1)} collective-permute-done((bf16[8,32,256]{2,1,0:T(8,128)(2,1)S(1)}, bf16[8,32,256]{2,1,0:T(8,128)(2,1)S(1)}, u32[]{:S(2)}, u32[]{:S(2)}) %collective-permute-start.35) | collective-permute-done | bytes 131104 | tf_op jit(solution)/shard_map/ppermute | solution.py:103
  69.1 1.3 collective-permute-start.36
  70.4 1.3 collective-permute-start.22
  72.0 2.0 %collective-permute-start.28 = (bf16[8,32,256]{2,1,0:T(8,128)(2,1)S(1)}, bf16[8,32,256]{2,1,0:T(8,128)(2,1)S(1)}, u32[]{:S(2)}, u32[]{:S(2)}) collective-permute-start(bf16[8,32,256]{2,1,0:T(8,128)(2,1)S(1)} %collective-permute-done.20.refs_7_), channel_id=1, source_target_pairs={{0,2},{2,0},{4,6},{6,4},{8,10},{10,8},{12,14},{14,12},{16,18},{18,... | collective-permute-start | bytes 393224 | tf_op jit(solution)/shard_map/ppermute | solution.py:99
  74.0 2.3 %collective-permute-start.29 = (bf16[8,32,256]{2,1,0:T(8,128)(2,1)S(1)}, bf16[8,32,256]{2,1,0:T(8,128)(2,1)S(1)}, u32[]{:S(2)}, u32[]{:S(2)}) collective-permute-start(bf16[8,32,256]{2,1,0:T(8,128)(2,1)S(1)} %collective-permute-done.21.refs_8_), channel_id=1, source_target_pairs={{0,2},{2,0},{4,6},{6,4},{8,10},{10,8},{12,14},{14,12},{16,18},{18,... | collective-permute-start | bytes 393224 | tf_op jit(solution)/shard_map/ppermute | solution.py:99
  76.3 1.5 %collective-permute-start.43 = (bf16[8,32,256]{2,1,0:T(8,128)(2,1)S(1)}, bf16[8,32,256]{2,1,0:T(8,128)(2,1)S(1)}, u32[]{:S(2)}, u32[]{:S(2)}) collective-permute-start(bf16[8,32,256]{2,1,0:T(8,128)(2,1)S(1)} %collective-permute-done.35.refs_22_), channel_id=1, source_target_pairs={{0,2},{2,0},{4,6},{6,4},{8,10},{10,8},{12,14},{14,12},{16,18},{18,... | collective-permute-start | bytes 393224 | tf_op jit(solution)/shard_map/ppermute | solution.py:99
  77.8 1.3 collective-permute-start.38
  79.1 1.3 collective-permute-start.24
  80.8 2.3 %collective-permute-start.30 = (bf16[8,32,256]{2,1,0:T(8,128)(2,1)S(1)}, bf16[8,32,256]{2,1,0:T(8,128)(2,1)S(1)}, u32[]{:S(2)}, u32[]{:S(2)}) collective-permute-start(bf16[8,32,256]{2,1,0:T(8,128)(2,1)S(1)} %collective-permute-done.22.refs_9_), channel_id=1, source_target_pairs={{0,2},{2,0},{4,6},{6,4},{8,10},{10,8},{12,14},{14,12},{16,18},{18,... | collective-permute-start | bytes 393224 | tf_op jit(solution)/shard_map/ppermute | solution.py:99
  83.1 2.0 %collective-permute-start.31 = (bf16[8,32,256]{2,1,0:T(8,128)(2,1)S(1)}, bf16[8,32,256]{2,1,0:T(8,128)(2,1)S(1)}, u32[]{:S(2)}, u32[]{:S(2)}) collective-permute-start(bf16[8,32,256]{2,1,0:T(8,128)(2,1)S(1)} %collective-permute-done.23.refs_10_), channel_id=1, source_target_pairs={{0,2},{2,0},{4,6},{6,4},{8,10},{10,8},{12,14},{14,12},{16,18},{18,... | collective-permute-start | bytes 393224 | tf_op jit(solution)/shard_map/ppermute | solution.py:99
  85.1 1.4 collective-permute-start.44
  87.8 1.3 collective-permute-start.40
  90.5 2.2 %collective-permute-start.32 = (bf16[8,32,256]{2,1,0:T(8,128)(2,1)S(1)}, bf16[8,32,256]{2,1,0:T(8,128)(2,1)S(1)}, u32[]{:S(2)}, u32[]{:S(2)}) collective-permute-start(bf16[8,32,256]{2,1,0:T(8,128)(2,1)S(1)} %collective-permute-done.24.refs_11_), channel_id=1, source_target_pairs={{0,2},{2,0},{4,6},{6,4},{8,10},{10,8},{12,14},{14,12},{16,18},{18,... | collective-permute-start | bytes 393224 | tf_op jit(solution)/shard_map/ppermute | solution.py:99
  92.8 2.2 %collective-permute-start.46 = (bf16[8,32,256]{2,1,0:T(8,128)(2,1)S(1)}, bf16[8,32,256]{2,1,0:T(8,128)(2,1)S(1)}, u32[]{:S(2)}, u32[]{:S(2)}) collective-permute-start(bf16[8,32,256]{2,1,0:T(8,128)(2,1)S(1)} %collective-permute-done.38.refs_25_), channel_id=1, source_target_pairs={{0,2},{2,0},{4,6},{6,4},{8,10},{10,8},{12,14},{14,12},{16,18},{18,... | collective-permute-start | bytes 393224 | tf_op jit(solution)/shard_map/ppermute | solution.py:99
  95.1 1.4 collective-permute-start.47
  96.5 1.3 collective-permute-start.42
  98.0 2.9 %collective-permute-start = (bf16[512,512]{1,0:T(8,128)(2,1)S(1)}, bf16[512,512]{1,0:T(8,128)(2,1)S(1)}, u32[]{:S(2)}, u32[]{:S(2)}) collective-permute-start(bf16[512,512]{1,0:T(8,128)(2,1)S(1)} %bitcast.13), channel_id=1, source_target_pairs={{2,4},{6,8},{10,12},{14,16},{18,20},{22,24},{26,28},{4,2},{8,6},{1... | collective-permute-start | bytes 1572872 | tf_op jit(solution)/shard_map/ppermute | solution.py:447
  103.4 6.6 %shard_map.98 = (bf16[176,256]{1,0:T(8,128)(2,1)S(1)}, bf16[176,256]{1,0:T(8,128)(2,1)S(1)}) custom-call(s32[3]{0:T(128)S(1)} %pad_add_fusion.scal_ref.refs_0_, s32[16]{0:T(128)S(1)} %fusion.refs_1_, s32[8]{0:T(128)S(1)} %copy-done.3, f32[1]{0:T(128)} %get-tuple-element.25.refs_3_, bf16[512,512]{1,0:T(8,128)(2,1)S(1)} %get-tuple-element.13.refs_3_.refs_4_, ...), custom_call_target="tpu_custom_call" | custom-call | flops 3221225472 | bytes 8388608 | tf_op jit(solution)/shard_map/pallas_call | solution.py:451
  110.2 1.3 collective-permute-start.51
  113.9 1.8 %collective-permute-start.67 = (bf16[176,256]{1,0:T(8,128)(2,1)S(1)}, bf16[176,256]{1,0:T(8,128)(2,1)S(1)}, u32[]{:S(2)}, u32[]{:S(2)}) collective-permute-start(bf16[176,256]{1,0:T(8,128)(2,1)S(1)} %collective-permute-done.66.refs_22_), channel_id=1, source_target_pairs={{0,8},{2,10},{4,0},{6,2},{8,16},{10,18},{12,4},{14,6},{16,24},{18,... | collective-permute-start | bytes 270344 | tf_op jit(solution)/shard_map/ppermute | solution.py:113
  117.2 2.0 %collective-permute-start.59 = (bf16[176,256]{1,0:T(8,128)(2,1)S(1)}, bf16[176,256]{1,0:T(8,128)(2,1)S(1)}, u32[]{:S(2)}, u32[]{:S(2)}) collective-permute-start(bf16[176,256]{1,0:T(8,128)(2,1)S(1)} %collective-permute-done.51.refs_7_), channel_id=1, source_target_pairs={{0,2},{2,0},{4,6},{6,4},{8,10},{10,8},{12,14},{14,12},{16,18},{18,... | collective-permute-start | bytes 270344 | tf_op jit(solution)/shard_map/ppermute | solution.py:99
  119.2 1.3 collective-permute-start.60
  124.5 2.2 %collective-permute-start.61 = (bf16[176,256]{1,0:T(8,128)(2,1)S(1)}, bf16[176,256]{1,0:T(8,128)(2,1)S(1)}, u32[]{:S(2)}, u32[]{:S(2)}) collective-permute-start(bf16[176,256]{1,0:T(8,128)(2,1)S(1)} %collective-permute-done.53.refs_9_), channel_id=1, source_target_pairs={{0,2},{2,0},{4,6},{6,4},{8,10},{10,8},{12,14},{14,12},{16,18},{18,... | collective-permute-start | bytes 270344 | tf_op jit(solution)/shard_map/ppermute | solution.py:99
  131.6 1.9 %collective-permute-start.63 = (bf16[176,256]{1,0:T(8,128)(2,1)S(1)}, bf16[176,256]{1,0:T(8,128)(2,1)S(1)}, u32[]{:S(2)}, u32[]{:S(2)}) collective-permute-start(bf16[176,256]{1,0:T(8,128)(2,1)S(1)} %collective-permute-done.55.refs_11_), channel_id=1, source_target_pairs={{0,2},{2,0},{4,6},{6,4},{8,10},{10,8},{12,14},{14,12},{16,18},{18,... | collective-permute-start | bytes 270344 | tf_op jit(solution)/shard_map/ppermute | solution.py:99
  133.6 1.9 %collective-permute-start.77 = (bf16[176,256]{1,0:T(8,128)(2,1)S(1)}, bf16[176,256]{1,0:T(8,128)(2,1)S(1)}, u32[]{:S(2)}, u32[]{:S(2)}) collective-permute-start(bf16[176,256]{1,0:T(8,128)(2,1)S(1)} %collective-permute-done.69.refs_25_), channel_id=1, source_target_pairs={{0,2},{2,0},{4,6},{6,4},{8,10},{10,8},{12,14},{14,12},{16,18},{18,... | collective-permute-start | bytes 270344 | tf_op jit(solution)/shard_map/ppermute | solution.py:99
  136.2 1.2 collective-permute-start.78
  138.9 2.1 %collective-permute-start.81 = (bf16[176,256]{1,0:T(8,128)(2,1)S(1)}, bf16[176,256]{1,0:T(8,128)(2,1)S(1)}, u32[]{:S(2)}, u32[]{:S(2)}) collective-permute-start(bf16[176,256]{1,0:T(8,128)(2,1)S(1)} %collective-permute-done.73.refs_29_), channel_id=1, source_target_pairs={{0,2},{2,0},{4,6},{6,4},{8,10},{10,8},{12,14},{14,12},{16,18},{18,... | collective-permute-start | bytes 270344 | tf_op jit(solution)/shard_map/ppermute | solution.py:99
  141.9 3.2 %shard_map.99 = (f32[4,512,512]{2,1,0:T(8,128)}, bf16[512,256]{1,0:T(8,128)(2,1)}) custom-call(s32[3]{0:T(128)S(1)} %pad_add_fusion.scal_ref.refs_0_, s32[16]{0:T(128)S(1)} %fusion.refs_1_, f32[3]{0:T(128)S(1)} %bitcast.16, bf16[512,512]{1,0:T(8,128)(2,1)S(1)} %bitcast.15, bf16[512,512]{1,0:T(8,128)(2,1)S(1)} %collective-permute-done.refs_4_, ...), custom_call_target="tpu_custom_call" | custom-call | flops 268435456 | bytes 6291456 | tf_op jit(solution)/shard_map/pallas_call | solution.py:467
  (143 shorter events, 29.7 us)
Async XLA Ops:
  3.1 25.2 %collective-permute-start.3 = (bf16[2,512,512]{2,1,0:T(8,128)(2,1)}, bf16[2,512,512]{2,1,0:T(8,128)(2,1)}, u32[]{:S(2)}, u32[]{:S(2)}) collective-permute-start(bf16[2,512,512]{2,1,0:T(8,128)(2,1)} %constant_dynamic-slice_fusion), channel_id=1, source_target_pairs={{0,1},{1,0},{2,3},{3,2},{4,5},{5,4},{6,7},{7,6},{8,9},{9,8},{10,11... | collective-permute-start | bytes 3145736 | tf_op jit(solution)/shard_map/ppermute | solution.py:103
  5.9 7.4 %collective-permute-start.5 = (bf16[272,512]{1,0:T(8,128)(2,1)S(1)}, bf16[272,512]{1,0:T(8,128)(2,1)}, u32[]{:S(2)}, u32[]{:S(2)}) collective-permute-start(bf16[272,512]{1,0:T(8,128)(2,1)S(1)} %concatenate.3.refs_7_), channel_id=1, source_target_pairs={{0,8},{2,10},{4,0},{6,2},{8,16},{10,18},{12,4},{14,6},{16,24},{18,... | collective-permute-start | bytes 835592 | tf_op jit(solution)/shard_map/ppermute | solution.py:113
  7.3 22.4 %collective-permute-start.6 = (bf16[272,512]{1,0:T(8,128)(2,1)S(1)}, bf16[272,512]{1,0:T(8,128)(2,1)}, u32[]{:S(2)}, u32[]{:S(2)}) collective-permute-start(bf16[272,512]{1,0:T(8,128)(2,1)S(1)} %concatenate.3.refs_7_), channel_id=1, source_target_pairs={{0,4},{2,6},{4,12},{6,14},{8,0},{10,2},{12,20},{14,22},{16,8},{18,... | collective-permute-start | bytes 835592 | tf_op jit(solution)/shard_map/ppermute | solution.py:113
  7.4 23.9 %collective-permute-start.11 = (bf16[272,512]{1,0:T(8,128)(2,1)S(1)}, bf16[272,512]{1,0:T(8,128)(2,1)}, u32[]{:S(2)}, u32[]{:S(2)}) collective-permute-start(bf16[272,512]{1,0:T(8,128)(2,1)S(1)} %concatenate.3.refs_7_), channel_id=1, source_target_pairs={{0,2},{2,0},{4,6},{6,4},{8,10},{10,8},{12,14},{14,12},{16,18},{18,... | collective-permute-start | bytes 835592 | tf_op jit(solution)/shard_map/ppermute | solution.py:99
  13.3 18.2 %collective-permute-start.7 = (bf16[272,512]{1,0:T(8,128)(2,1)}, bf16[272,512]{1,0:T(8,128)(2,1)}, u32[]{:S(2)}, u32[]{:S(2)}) collective-permute-start(bf16[272,512]{1,0:T(8,128)(2,1)} %collective-permute-done.5.refs_8_), channel_id=1, source_target_pairs={{0,8},{2,10},{4,0},{6,2},{8,16},{10,18},{12,4},{14,6},{16,24},{18,... | collective-permute-start | bytes 835592 | tf_op jit(solution)/shard_map/ppermute | solution.py:113
  15.3 16.5 %all-to-all-start = ((bf16[16,32,256]{2,1,0:T(8,128)(2,1)}), bf16[16,32,256]{2,1,0:T(8,128)(2,1)}, u32[]{:S(2)}, u32[]{:S(2)}) async-start(bf16[16,32,256]{2,1,0:T(8,128)(2,1)} %bitcast.17), calls=%async_computation | async-start | bytes 524288 | tf_op jit(solution)/shard_map/all_to_all | solution.py:412
  28.3 26.2 %collective-permute-start.4 = (bf16[2,512,512]{2,1,0:T(8,128)(2,1)}, bf16[2,512,512]{2,1,0:T(8,128)(2,1)}, u32[]{:S(2)}, u32[]{:S(2)}) collective-permute-start(bf16[2,512,512]{2,1,0:T(8,128)(2,1)} %collective-permute-done.3.refs_5_.refs_6_), channel_id=1, source_target_pairs={{0,2},{2,0},{4,6},{6,4},{8,10},{10,8},{12,14},{14,12},{16,18},{18,... | collective-permute-start | bytes 3145736 | tf_op jit(solution)/shard_map/ppermute | solution.py:99
  29.6 8.6 %collective-permute-start.8 = (bf16[272,512]{1,0:T(8,128)(2,1)}, bf16[272,512]{1,0:T(8,128)(2,1)}, u32[]{:S(2)}, u32[]{:S(2)}) collective-permute-start(bf16[272,512]{1,0:T(8,128)(2,1)} %collective-permute-done.6.refs_9_), channel_id=1, source_target_pairs={{0,4},{2,6},{4,12},{6,14},{8,0},{10,2},{12,20},{14,22},{16,8},{18,... | collective-permute-start | bytes 835592 | tf_op jit(solution)/shard_map/ppermute | solution.py:113
  31.0 8.6 %collective-permute-start.12 = (bf16[272,512]{1,0:T(8,128)(2,1)}, bf16[272,512]{1,0:T(8,128)(2,1)}, u32[]{:S(2)}, u32[]{:S(2)}) collective-permute-start(bf16[272,512]{1,0:T(8,128)(2,1)} %collective-permute-done.5.refs_8_), channel_id=1, source_target_pairs={{0,2},{2,0},{4,6},{6,4},{8,10},{10,8},{12,14},{14,12},{16,18},{18,... | collective-permute-start | bytes 835592 | tf_op jit(solution)/shard_map/ppermute | solution.py:99
  31.3 9.4 %collective-permute-start.13 = (bf16[272,512]{1,0:T(8,128)(2,1)}, bf16[272,512]{1,0:T(8,128)(2,1)}, u32[]{:S(2)}, u32[]{:S(2)}) collective-permute-start(bf16[272,512]{1,0:T(8,128)(2,1)} %collective-permute-done.6.refs_9_), channel_id=1, source_target_pairs={{0,2},{2,0},{4,6},{6,4},{8,10},{10,8},{12,14},{14,12},{16,18},{18,... | collective-permute-start | bytes 835592 | tf_op jit(solution)/shard_map/ppermute | solution.py:99
  31.6 10.4 %collective-permute-start.9 = (bf16[272,512]{1,0:T(8,128)(2,1)}, bf16[272,512]{1,0:T(8,128)(2,1)}, u32[]{:S(2)}, u32[]{:S(2)}) collective-permute-start(bf16[272,512]{1,0:T(8,128)(2,1)} %collective-permute-done.7.refs_10_), channel_id=1, source_target_pairs={{0,8},{2,10},{4,0},{6,2},{8,16},{10,18},{12,4},{14,6},{16,24},{18,... | collective-permute-start | bytes 835592 | tf_op jit(solution)/shard_map/ppermute | solution.py:113
  38.2 7.4 %collective-permute-start.2 = (bf16[512,256]{1,0:T(8,128)(2,1)}, bf16[512,256]{1,0:T(8,128)(2,1)}, u32[]{:S(2)}, u32[]{:S(2)}) collective-permute-start(bf16[512,256]{1,0:T(8,128)(2,1)} %bitcast.7.mine_ref), channel_id=1, source_target_pairs={{0,1},{1,0},{2,3},{3,2},{4,5},{5,4},{6,7},{7,6},{8,9},{9,8},{10,11... | collective-permute-start | bytes 786440 | tf_op jit(solution)/shard_map/ppermute | solution.py:103
  39.6 10.5 %collective-permute-start.14 = (bf16[272,512]{1,0:T(8,128)(2,1)}, bf16[272,512]{1,0:T(8,128)(2,1)}, u32[]{:S(2)}, u32[]{:S(2)}) collective-permute-start(bf16[272,512]{1,0:T(8,128)(2,1)} %collective-permute-done.7.refs_10_), channel_id=1, source_target_pairs={{0,2},{2,0},{4,6},{6,4},{8,10},{10,8},{12,14},{14,12},{16,18},{18,... | collective-permute-start | bytes 835592 | tf_op jit(solution)/shard_map/ppermute | solution.py:99
  40.7 8.5 %collective-permute-start.10 = (bf16[272,512]{1,0:T(8,128)(2,1)}, bf16[272,512]{1,0:T(8,128)(2,1)}, u32[]{:S(2)}, u32[]{:S(2)}) collective-permute-start(bf16[272,512]{1,0:T(8,128)(2,1)} %collective-permute-done.8.refs_11_), channel_id=1, source_target_pairs={{0,4},{2,6},{4,12},{6,14},{8,0},{10,2},{12,20},{14,22},{16,8},{18,... | collective-permute-start | bytes 835592 | tf_op jit(solution)/shard_map/ppermute | solution.py:113
  42.0 8.9 %collective-permute-start.18 = (bf16[272,512]{1,0:T(8,128)(2,1)}, bf16[272,512]{1,0:T(8,128)(2,1)}, u32[]{:S(2)}, u32[]{:S(2)}) collective-permute-start(bf16[272,512]{1,0:T(8,128)(2,1)} %collective-permute-done.9.refs_12_), channel_id=1, source_target_pairs={{0,8},{2,10},{4,0},{6,2},{8,16},{10,18},{12,4},{14,6},{16,24},{18,... | collective-permute-start | bytes 835592 | tf_op jit(solution)/shard_map/ppermute | solution.py:113
  45.6 8.9 %collective-permute-start.15 = (bf16[272,512]{1,0:T(8,128)(2,1)}, bf16[272,512]{1,0:T(8,128)(2,1)S(1)}, u32[]{:S(2)}, u32[]{:S(2)}) collective-permute-start(bf16[272,512]{1,0:T(8,128)(2,1)} %collective-permute-done.8.refs_11_), channel_id=1, source_target_pairs={{0,2},{2,0},{4,6},{6,4},{8,10},{10,8},{12,14},{14,12},{16,18},{18,... | collective-permute-start | bytes 835592 | tf_op jit(solution)/shard_map/ppermute | solution.py:99
  49.2 5.3 %collective-permute-start.16 = (bf16[272,512]{1,0:T(8,128)(2,1)}, bf16[272,512]{1,0:T(8,128)(2,1)S(1)}, u32[]{:S(2)}, u32[]{:S(2)}) collective-permute-start(bf16[272,512]{1,0:T(8,128)(2,1)} %collective-permute-done.9.refs_12_), channel_id=1, source_target_pairs={{0,2},{2,0},{4,6},{6,4},{8,10},{10,8},{12,14},{14,12},{16,18},{18,... | collective-permute-start | bytes 835592 | tf_op jit(solution)/shard_map/ppermute | solution.py:99
  50.8 10.5 %collective-permute-start.19 = (bf16[272,512]{1,0:T(8,128)(2,1)}, bf16[272,512]{1,0:T(8,128)(2,1)S(1)}, u32[]{:S(2)}, u32[]{:S(2)}) collective-permute-start(bf16[272,512]{1,0:T(8,128)(2,1)} %collective-permute-done.18.refs_8_.refs_39_), channel_id=1, source_target_pairs={{0,2},{2,0},{4,6},{6,4},{8,10},{10,8},{12,14},{14,12},{16,18},{18,... | collective-permute-start | bytes 835592 | tf_op jit(solution)/shard_map/ppermute | solution.py:99
  64.3 6.1 %collective-permute-start.20 = (bf16[8,32,256]{2,1,0:T(8,128)(2,1)S(1)}, bf16[8,32,256]{2,1,0:T(8,128)(2,1)S(1)}, u32[]{:S(2)}, u32[]{:S(2)}) collective-permute-start(bf16[8,32,256]{2,1,0:T(8,128)(2,1)S(1)} %get-tuple-element.18.refs_6_), channel_id=1, source_target_pairs={{0,8},{2,10},{4,0},{6,2},{8,16},{10,18},{12,4},{14,6},{16,24},{18,... | collective-permute-start | bytes 393224 | tf_op jit(solution)/shard_map/ppermute | solution.py:113
  65.6 6.3 %collective-permute-start.21 = (bf16[8,32,256]{2,1,0:T(8,128)(2,1)S(1)}, bf16[8,32,256]{2,1,0:T(8,128)(2,1)S(1)}, u32[]{:S(2)}, u32[]{:S(2)}) collective-permute-start(bf16[8,32,256]{2,1,0:T(8,128)(2,1)S(1)} %get-tuple-element.18.refs_6_), channel_id=1, source_target_pairs={{0,4},{2,6},{4,12},{6,14},{8,0},{10,2},{12,20},{14,22},{16,8},{18,... | collective-permute-start | bytes 393224 | tf_op jit(solution)/shard_map/ppermute | solution.py:113
  65.7 6.3 %collective-permute-start.27 = (bf16[8,32,256]{2,1,0:T(8,128)(2,1)S(1)}, bf16[8,32,256]{2,1,0:T(8,128)(2,1)S(1)}, u32[]{:S(2)}, u32[]{:S(2)}) collective-permute-start(bf16[8,32,256]{2,1,0:T(8,128)(2,1)S(1)} %get-tuple-element.18.refs_6_), channel_id=1, source_target_pairs={{0,2},{2,0},{4,6},{6,4},{8,10},{10,8},{12,14},{14,12},{16,18},{18,... | collective-permute-start | bytes 393224 | tf_op jit(solution)/shard_map/ppermute | solution.py:99
  70.4 5.9 %collective-permute-start.22 = (bf16[8,32,256]{2,1,0:T(8,128)(2,1)S(1)}, bf16[8,32,256]{2,1,0:T(8,128)(2,1)S(1)}, u32[]{:S(2)}, u32[]{:S(2)}) collective-permute-start(bf16[8,32,256]{2,1,0:T(8,128)(2,1)S(1)} %collective-permute-done.20.refs_7_), channel_id=1, source_target_pairs={{0,8},{2,10},{4,0},{6,2},{8,16},{10,18},{12,4},{14,6},{16,24},{18,... | collective-permute-start | bytes 393224 | tf_op jit(solution)/shard_map/ppermute | solution.py:113
  71.7 6.1 %collective-permute-start.37 = (bf16[8,32,256]{2,1,0:T(8,128)(2,1)S(1)}, bf16[8,32,256]{2,1,0:T(8,128)(2,1)S(1)}, u32[]{:S(2)}, u32[]{:S(2)}) collective-permute-start(bf16[8,32,256]{2,1,0:T(8,128)(2,1)S(1)} %collective-permute-done.35.refs_22_), channel_id=1, source_target_pairs={{0,4},{2,6},{4,12},{6,14},{8,0},{10,2},{12,20},{14,22},{16,8},{18,... | collective-permute-start | bytes 393224 | tf_op jit(solution)/shard_map/ppermute | solution.py:113
  71.9 7.3 %collective-permute-start.23 = (bf16[8,32,256]{2,1,0:T(8,128)(2,1)S(1)}, bf16[8,32,256]{2,1,0:T(8,128)(2,1)S(1)}, u32[]{:S(2)}, u32[]{:S(2)}) collective-permute-start(bf16[8,32,256]{2,1,0:T(8,128)(2,1)S(1)} %collective-permute-done.21.refs_8_), channel_id=1, source_target_pairs={{0,4},{2,6},{4,12},{6,14},{8,0},{10,2},{12,20},{14,22},{16,8},{18,... | collective-permute-start | bytes 393224 | tf_op jit(solution)/shard_map/ppermute | solution.py:113
  72.0 8.4 %collective-permute-start.28 = (bf16[8,32,256]{2,1,0:T(8,128)(2,1)S(1)}, bf16[8,32,256]{2,1,0:T(8,128)(2,1)S(1)}, u32[]{:S(2)}, u32[]{:S(2)}) collective-permute-start(bf16[8,32,256]{2,1,0:T(8,128)(2,1)S(1)} %collective-permute-done.20.refs_7_), channel_id=1, source_target_pairs={{0,2},{2,0},{4,6},{6,4},{8,10},{10,8},{12,14},{14,12},{16,18},{18,... | collective-permute-start | bytes 393224 | tf_op jit(solution)/shard_map/ppermute | solution.py:99
  74.0 6.6 %collective-permute-start.29 = (bf16[8,32,256]{2,1,0:T(8,128)(2,1)S(1)}, bf16[8,32,256]{2,1,0:T(8,128)(2,1)S(1)}, u32[]{:S(2)}, u32[]{:S(2)}) collective-permute-start(bf16[8,32,256]{2,1,0:T(8,128)(2,1)S(1)} %collective-permute-done.21.refs_8_), channel_id=1, source_target_pairs={{0,2},{2,0},{4,6},{6,4},{8,10},{10,8},{12,14},{14,12},{16,18},{18,... | collective-permute-start | bytes 393224 | tf_op jit(solution)/shard_map/ppermute | solution.py:99
  79.1 6.0 %collective-permute-start.24 = (bf16[8,32,256]{2,1,0:T(8,128)(2,1)S(1)}, bf16[8,32,256]{2,1,0:T(8,128)(2,1)S(1)}, u32[]{:S(2)}, u32[]{:S(2)}) collective-permute-start(bf16[8,32,256]{2,1,0:T(8,128)(2,1)S(1)} %collective-permute-done.22.refs_9_), channel_id=1, source_target_pairs={{0,8},{2,10},{4,0},{6,2},{8,16},{10,18},{12,4},{14,6},{16,24},{18,... | collective-permute-start | bytes 393224 | tf_op jit(solution)/shard_map/ppermute | solution.py:113
  80.4 6.1 %collective-permute-start.39 = (bf16[8,32,256]{2,1,0:T(8,128)(2,1)S(1)}, bf16[8,32,256]{2,1,0:T(8,128)(2,1)S(1)}, u32[]{:S(2)}, u32[]{:S(2)}) collective-permute-start(bf16[8,32,256]{2,1,0:T(8,128)(2,1)S(1)} %collective-permute-done.37.refs_24_), channel_id=1, source_target_pairs={{0,4},{2,6},{4,12},{6,14},{8,0},{10,2},{12,20},{14,22},{16,8},{18,... | collective-permute-start | bytes 393224 | tf_op jit(solution)/shard_map/ppermute | solution.py:113
  80.6 7.2 %collective-permute-start.25 = (bf16[8,32,256]{2,1,0:T(8,128)(2,1)S(1)}, bf16[8,32,256]{2,1,0:T(8,128)(2,1)S(1)}, u32[]{:S(2)}, u32[]{:S(2)}) collective-permute-start(bf16[8,32,256]{2,1,0:T(8,128)(2,1)S(1)} %collective-permute-done.23.refs_10_), channel_id=1, source_target_pairs={{0,4},{2,6},{4,12},{6,14},{8,0},{10,2},{12,20},{14,22},{16,8},{18,... | collective-permute-start | bytes 393224 | tf_op jit(solution)/shard_map/ppermute | solution.py:113
  80.8 8.3 %collective-permute-start.30 = (bf16[8,32,256]{2,1,0:T(8,128)(2,1)S(1)}, bf16[8,32,256]{2,1,0:T(8,128)(2,1)S(1)}, u32[]{:S(2)}, u32[]{:S(2)}) collective-permute-start(bf16[8,32,256]{2,1,0:T(8,128)(2,1)S(1)} %collective-permute-done.22.refs_9_), channel_id=1, source_target_pairs={{0,2},{2,0},{4,6},{6,4},{8,10},{10,8},{12,14},{14,12},{16,18},{18,... | collective-permute-start | bytes 393224 | tf_op jit(solution)/shard_map/ppermute | solution.py:99
  83.1 7.1 %collective-permute-start.31 = (bf16[8,32,256]{2,1,0:T(8,128)(2,1)S(1)}, bf16[8,32,256]{2,1,0:T(8,128)(2,1)S(1)}, u32[]{:S(2)}, u32[]{:S(2)}) collective-permute-start(bf16[8,32,256]{2,1,0:T(8,128)(2,1)S(1)} %collective-permute-done.23.refs_10_), channel_id=1, source_target_pairs={{0,2},{2,0},{4,6},{6,4},{8,10},{10,8},{12,14},{14,12},{16,18},{18,... | collective-permute-start | bytes 393224 | tf_op jit(solution)/shard_map/ppermute | solution.py:99
  85.1 5.4 %collective-permute-start.44 = (bf16[8,32,256]{2,1,0:T(8,128)(2,1)S(1)}, bf16[8,32,256]{2,1,0:T(8,128)(2,1)S(1)}, u32[]{:S(2)}, u32[]{:S(2)}) collective-permute-start(bf16[8,32,256]{2,1,0:T(8,128)(2,1)S(1)} %collective-permute-done.36.refs_23_), channel_id=1, source_target_pairs={{0,2},{2,0},{4,6},{6,4},{8,10},{10,8},{12,14},{14,12},{16,18},{18,... | collective-permute-start | bytes 393224 | tf_op jit(solution)/shard_map/ppermute | solution.py:99
  86.5 6.2 %collective-permute-start.45 = (bf16[8,32,256]{2,1,0:T(8,128)(2,1)S(1)}, bf16[8,32,256]{2,1,0:T(8,128)(2,1)S(1)}, u32[]{:S(2)}, u32[]{:S(2)}) collective-permute-start(bf16[8,32,256]{2,1,0:T(8,128)(2,1)S(1)} %collective-permute-done.37.refs_24_), channel_id=1, source_target_pairs={{0,2},{2,0},{4,6},{6,4},{8,10},{10,8},{12,14},{14,12},{16,18},{18,... | collective-permute-start | bytes 393224 | tf_op jit(solution)/shard_map/ppermute | solution.py:99
  89.0 6.0 %collective-permute-start.26 = (bf16[8,32,256]{2,1,0:T(8,128)(2,1)S(1)}, bf16[8,32,256]{2,1,0:T(8,128)(2,1)S(1)}, u32[]{:S(2)}, u32[]{:S(2)}) collective-permute-start(bf16[8,32,256]{2,1,0:T(8,128)(2,1)S(1)} %collective-permute-done.24.refs_11_), channel_id=1, source_target_pairs={{0,8},{2,10},{4,0},{6,2},{8,16},{10,18},{12,4},{14,6},{16,24},{18,... | collective-permute-start | bytes 393224 | tf_op jit(solution)/shard_map/ppermute | solution.py:113
  90.2 6.2 %collective-permute-start.41 = (bf16[8,32,256]{2,1,0:T(8,128)(2,1)S(1)}, bf16[8,32,256]{2,1,0:T(8,128)(2,1)S(1)}, u32[]{:S(2)}, u32[]{:S(2)}) collective-permute-start(bf16[8,32,256]{2,1,0:T(8,128)(2,1)S(1)} %collective-permute-done.39.refs_26_), channel_id=1, source_target_pairs={{0,4},{2,6},{4,12},{6,14},{8,0},{10,2},{12,20},{14,22},{16,8},{18,... | collective-permute-start | bytes 393224 | tf_op jit(solution)/shard_map/ppermute | solution.py:113
  90.5 7.3 %collective-permute-start.32 = (bf16[8,32,256]{2,1,0:T(8,128)(2,1)S(1)}, bf16[8,32,256]{2,1,0:T(8,128)(2,1)S(1)}, u32[]{:S(2)}, u32[]{:S(2)}) collective-permute-start(bf16[8,32,256]{2,1,0:T(8,128)(2,1)S(1)} %collective-permute-done.24.refs_11_), channel_id=1, source_target_pairs={{0,2},{2,0},{4,6},{6,4},{8,10},{10,8},{12,14},{14,12},{16,18},{18,... | collective-permute-start | bytes 393224 | tf_op jit(solution)/shard_map/ppermute | solution.py:99
  92.8 8.1 %collective-permute-start.46 = (bf16[8,32,256]{2,1,0:T(8,128)(2,1)S(1)}, bf16[8,32,256]{2,1,0:T(8,128)(2,1)S(1)}, u32[]{:S(2)}, u32[]{:S(2)}) collective-permute-start(bf16[8,32,256]{2,1,0:T(8,128)(2,1)S(1)} %collective-permute-done.38.refs_25_), channel_id=1, source_target_pairs={{0,2},{2,0},{4,6},{6,4},{8,10},{10,8},{12,14},{14,12},{16,18},{18,... | collective-permute-start | bytes 393224 | tf_op jit(solution)/shard_map/ppermute | solution.py:99
  95.1 5.9 %collective-permute-start.47 = (bf16[8,32,256]{2,1,0:T(8,128)(2,1)S(1)}, bf16[8,32,256]{2,1,0:T(8,128)(2,1)S(1)}, u32[]{:S(2)}, u32[]{:S(2)}) collective-permute-start(bf16[8,32,256]{2,1,0:T(8,128)(2,1)S(1)} %collective-permute-done.39.refs_26_), channel_id=1, source_target_pairs={{0,2},{2,0},{4,6},{6,4},{8,10},{10,8},{12,14},{14,12},{16,18},{18,... | collective-permute-start | bytes 393224 | tf_op jit(solution)/shard_map/ppermute | solution.py:99
  98.0 14.4 %collective-permute-start = (bf16[512,512]{1,0:T(8,128)(2,1)S(1)}, bf16[512,512]{1,0:T(8,128)(2,1)S(1)}, u32[]{:S(2)}, u32[]{:S(2)}) collective-permute-start(bf16[512,512]{1,0:T(8,128)(2,1)S(1)} %bitcast.13), channel_id=1, source_target_pairs={{2,4},{6,8},{10,12},{14,16},{18,20},{22,24},{26,28},{4,2},{8,6},{1... | collective-permute-start | bytes 1572872 | tf_op jit(solution)/shard_map/ppermute | solution.py:447
  102.4 13.9 %collective-permute-start.1 = (bf16[512,512]{1,0:T(8,128)(2,1)S(1)}, bf16[512,512]{1,0:T(8,128)(2,1)S(1)}, u32[]{:S(2)}, u32[]{:S(2)}) collective-permute-start(bf16[512,512]{1,0:T(8,128)(2,1)S(1)} %bitcast.14), channel_id=1, source_target_pairs={{0,2},{2,0},{4,6},{6,4},{8,10},{10,8},{12,14},{14,12},{16,18},{18,... | collective-permute-start | bytes 1572872 | tf_op jit(solution)/shard_map/ppermute | solution.py:99
  110.2 5.4 %collective-permute-start.51 = (bf16[176,256]{1,0:T(8,128)(2,1)S(1)}, bf16[176,256]{1,0:T(8,128)(2,1)S(1)}, u32[]{:S(2)}, u32[]{:S(2)}) collective-permute-start(bf16[176,256]{1,0:T(8,128)(2,1)S(1)} %get-tuple-element.20.refs_6_), channel_id=1, source_target_pairs={{0,8},{2,10},{4,0},{6,2},{8,16},{10,18},{12,4},{14,6},{16,24},{18,... | collective-permute-start | bytes 270344 | tf_op jit(solution)/shard_map/ppermute | solution.py:113
  111.5 5.6 %collective-permute-start.52 = (bf16[176,256]{1,0:T(8,128)(2,1)S(1)}, bf16[176,256]{1,0:T(8,128)(2,1)S(1)}, u32[]{:S(2)}, u32[]{:S(2)}) collective-permute-start(bf16[176,256]{1,0:T(8,128)(2,1)S(1)} %get-tuple-element.20.refs_6_), channel_id=1, source_target_pairs={{0,4},{2,6},{4,12},{6,14},{8,0},{10,2},{12,20},{14,22},{16,8},{18,... | collective-permute-start | bytes 270344 | tf_op jit(solution)/shard_map/ppermute | solution.py:113
  117.1 5.5 %collective-permute-start.54 = (bf16[176,256]{1,0:T(8,128)(2,1)S(1)}, bf16[176,256]{1,0:T(8,128)(2,1)S(1)}, u32[]{:S(2)}, u32[]{:S(2)}) collective-permute-start(bf16[176,256]{1,0:T(8,128)(2,1)S(1)} %collective-permute-done.52.refs_8_), channel_id=1, source_target_pairs={{0,4},{2,6},{4,12},{6,14},{8,0},{10,2},{12,20},{14,22},{16,8},{18,... | collective-permute-start | bytes 270344 | tf_op jit(solution)/shard_map/ppermute | solution.py:113
  117.2 6.1 %collective-permute-start.59 = (bf16[176,256]{1,0:T(8,128)(2,1)S(1)}, bf16[176,256]{1,0:T(8,128)(2,1)S(1)}, u32[]{:S(2)}, u32[]{:S(2)}) collective-permute-start(bf16[176,256]{1,0:T(8,128)(2,1)S(1)} %collective-permute-done.51.refs_7_), channel_id=1, source_target_pairs={{0,2},{2,0},{4,6},{6,4},{8,10},{10,8},{12,14},{14,12},{16,18},{18,... | collective-permute-start | bytes 270344 | tf_op jit(solution)/shard_map/ppermute | solution.py:99
  123.3 5.3 %collective-permute-start.70 = (bf16[176,256]{1,0:T(8,128)(2,1)S(1)}, bf16[176,256]{1,0:T(8,128)(2,1)S(1)}, u32[]{:S(2)}, u32[]{:S(2)}) collective-permute-start(bf16[176,256]{1,0:T(8,128)(2,1)S(1)} %collective-permute-done.68.refs_24_), channel_id=1, source_target_pairs={{0,4},{2,6},{4,12},{6,14},{8,0},{10,2},{12,20},{14,22},{16,8},{18,... | collective-permute-start | bytes 270344 | tf_op jit(solution)/shard_map/ppermute | solution.py:113
  124.1 5.4 %collective-permute-start.56 = (bf16[176,256]{1,0:T(8,128)(2,1)S(1)}, bf16[176,256]{1,0:T(8,128)(2,1)S(1)}, u32[]{:S(2)}, u32[]{:S(2)}) collective-permute-start(bf16[176,256]{1,0:T(8,128)(2,1)S(1)} %collective-permute-done.54.refs_10_), channel_id=1, source_target_pairs={{0,4},{2,6},{4,12},{6,14},{8,0},{10,2},{12,20},{14,22},{16,8},{18,... | collective-permute-start | bytes 270344 | tf_op jit(solution)/shard_map/ppermute | solution.py:113
  124.5 5.7 %collective-permute-start.61 = (bf16[176,256]{1,0:T(8,128)(2,1)S(1)}, bf16[176,256]{1,0:T(8,128)(2,1)S(1)}, u32[]{:S(2)}, u32[]{:S(2)}) collective-permute-start(bf16[176,256]{1,0:T(8,128)(2,1)S(1)} %collective-permute-done.53.refs_9_), channel_id=1, source_target_pairs={{0,2},{2,0},{4,6},{6,4},{8,10},{10,8},{12,14},{14,12},{16,18},{18,... | collective-permute-start | bytes 270344 | tf_op jit(solution)/shard_map/ppermute | solution.py:99
  131.6 5.8 %collective-permute-start.63 = (bf16[176,256]{1,0:T(8,128)(2,1)S(1)}, bf16[176,256]{1,0:T(8,128)(2,1)S(1)}, u32[]{:S(2)}, u32[]{:S(2)}) collective-permute-start(bf16[176,256]{1,0:T(8,128)(2,1)S(1)} %collective-permute-done.55.refs_11_), channel_id=1, source_target_pairs={{0,2},{2,0},{4,6},{6,4},{8,10},{10,8},{12,14},{14,12},{16,18},{18,... | collective-permute-start | bytes 270344 | tf_op jit(solution)/shard_map/ppermute | solution.py:99
  (41 other events, 350.3 us)
